TPU v7x, 128 devices: a whole 4x4x4 slice. The times are simulated.
128 devices in a mesh: inp: 4 (over z), chan: 32 (over y, x, core).
Axes of the slice: x: 4, y: 4, z: 4, core: 2. Of those that a mesh axis runs over, the one named last changes fastest.
Arguments:
- samples: bfloat16 [1024, 512, 512], P('inp', 'chan'), may hold values from -16 to 16
- gram_owner: int32 [128], replicated, may hold values from 0 to 127, as said below
- beam_owner: int32 [256], replicated, may hold values from 0 to 31, as said below
- delays: float32 [256, 1024], replicated, may hold values from -64 to 64
- sections: int32 [256], replicated, may hold values from 0 to 255, each once
Outputs:
- visibilities: float32 [256, 2, 1024, 1024], P(('inp', 'chan'))
- beam_voltages: float32 [512, 4, 512, 128], P('chan', 'inp')
Inputs may be any that keep to these rules, and one draw needn't show every extreme that they name: `gram_owner`: no device owns more than 2 of the correlated channels, and some device owns exactly 2. `beam_owner`: no index of chan owns more than 16 channels, and some owns exactly 16. `sections`: each value once.
All inputs are finite; a program needn't handle non-finite values.
Results may differ from a plain program's by a relative error of at most 0.0048.
Values may be sent and summed in bfloat16 or wider, within the bound.
No kernel may reach another device: no remote copies, remote signals or barrier semaphores. Data moves between devices by JAX's collectives and lax.ppermute only.
A program may use at most 256 MiB of HBM per device.

v0:
```python
import math

import jax
import jax.numpy as jnp
from jax import lax
from jax.sharding import PartitionSpec as P


def fourier_table(length_total):
    half_count = length_total // 2
    rows = jnp.arange(half_count, dtype=jnp.int32)
    cols = jnp.arange(length_total, dtype=jnp.int32)
    turns = (rows[:, None] * cols[None, :] % length_total).astype(jnp.float32) * (
        2.0 * math.pi / length_total
    )
    factor = 1.0 / math.sqrt(length_total)
    return jnp.stack([jnp.cos(turns) * factor, -jnp.sin(turns) * factor]).astype(jnp.bfloat16)


def slot_table(owner_list, owner_count, slot_count):
    count = owner_list.shape[0]
    places = jnp.arange(count, dtype=jnp.int32)
    before = (owner_list[None, :] == owner_list[:, None]) & (places[None, :] < places[:, None])
    slot_of = jnp.sum(before.astype(jnp.int32), axis=1)
    keys = owner_list * slot_count + slot_of
    targets = jnp.arange(owner_count * slot_count, dtype=jnp.int32)
    match = keys[None, :] == targets[:, None]
    channel_of = jnp.sum(jnp.where(match, places[None, :], 0), axis=1)
    live_slot = jnp.any(match, axis=1)
    return (keys, channel_of, live_slot)


def apply_weights(channel_data, frequencies, delay_block, length_total, inverse):
    angle = frequencies[:, None, None] * delay_block.T[None] * (2.0 * math.pi / length_total)
    real_weight = (jnp.cos(angle) * inverse).astype(jnp.bfloat16)
    imag_weight = (-jnp.sin(angle) * inverse).astype(jnp.bfloat16)
    upper = jnp.concatenate([real_weight, imag_weight], axis=-1)
    lower = jnp.concatenate([-imag_weight, real_weight], axis=-1)
    matrix = jnp.stack([upper, lower], axis=1)
    return jnp.einsum("spfm,spmc->sfc", channel_data, matrix, preferred_element_type=jnp.float32)


def shards(samples, gram_owner, beam_owner, delays, sections):
    input_count, frame_count, length_total = samples.shape
    half_count = length_total // 2
    inp_count = lax.axis_size("inp")
    chan_count = lax.axis_size("chan")
    inp_here = lax.axis_index("inp")
    chan_here = lax.axis_index("chan")
    all_inputs = input_count * inp_count
    all_frames = frame_count * chan_count
    owner_count = inp_count * chan_count
    gram_slots = 2 * gram_owner.shape[0] // owner_count
    beam_slots = 2 * half_count // chan_count
    beam_total = delays.shape[0]
    section_width = beam_total // inp_count
    table = fourier_table(length_total)
    spectra = jnp.einsum(
        "pkw,ifw->kpfi", table, samples, preferred_element_type=jnp.float32
    ).astype(jnp.bfloat16)
    _, gram_channel, gram_live = slot_table(gram_owner, owner_count, gram_slots)
    outgoing = jnp.where(
        gram_live[:, None, None, None],
        jnp.take(spectra, gram_channel, axis=0),
        jnp.zeros((), jnp.bfloat16),
    )
    outgoing = outgoing.reshape(owner_count, gram_slots, 2, frame_count, input_count)
    arrived = lax.all_to_all(outgoing, ("inp", "chan"), split_axis=0, concat_axis=0, tiled=True)
    arrived = arrived.reshape(inp_count, chan_count, gram_slots, 2, frame_count, input_count)

    def correlate(slot_index, grams):
        block = lax.dynamic_index_in_dim(arrived, slot_index, 2, keepdims=False)
        products = jnp.einsum(
            "icpfa,jcqfb->pqiajb", block, block, preferred_element_type=jnp.float32
        )
        products = products.reshape(2, 2, all_inputs, all_inputs)
        real_part = products[0, 0] + products[1, 1]
        imag_part = products[1, 0] - products[0, 1]
        result = jnp.stack([real_part, imag_part]) / all_frames
        return lax.dynamic_update_index_in_dim(grams, result, slot_index, 0)

    empty_grams = jnp.zeros((gram_slots, 2, all_inputs, all_inputs), jnp.float32)
    visibilities = lax.fori_loop(0, gram_slots, correlate, empty_grams)
    _, beam_channel, beam_live = slot_table(beam_owner, chan_count, beam_slots)
    inverse = 1.0 / math.sqrt(all_inputs)
    delay_cols = lax.dynamic_slice_in_dim(delays, inp_here * input_count, input_count, 1)
    ordered = jnp.take(delay_cols, sections, axis=0)
    leaving = jnp.where(
        beam_live[:, None, None, None],
        jnp.take(spectra, beam_channel, axis=0),
        jnp.zeros((), jnp.bfloat16),
    )
    leaving = leaving.reshape(chan_count, beam_slots, 2, frame_count, input_count)
    beam_data = lax.all_to_all(leaving, "chan", split_axis=0, concat_axis=3, tiled=True).reshape(
        beam_slots, 2, all_frames, input_count
    )
    frequencies = lax.dynamic_slice_in_dim(beam_channel, chan_here * beam_slots, beam_slots).astype(
        jnp.float32
    )
    partial_beams = apply_weights(beam_data, frequencies, ordered, length_total, inverse)
    partial_beams = partial_beams.reshape(beam_slots, all_frames, 2, beam_total)
    formed = lax.psum_scatter(partial_beams, "inp", scatter_dimension=3, tiled=True)
    formed = formed.reshape(beam_slots, all_frames, 2 * section_width)
    return (visibilities, formed.reshape(beam_slots, 1, all_frames, 2 * section_width))


def solution(mesh):
    return jax.shard_map(
        shards,
        mesh=mesh,
        in_specs=(P("inp", "chan", None), P(), P(), P(), P()),
        out_specs=(P(("inp", "chan"), None, None, None), P("chan", "inp", None, None)),
        check_vma=False,
    )
```

profile of v0, /device:TPU:1, one launch (start us, length us, event | category | flops | bytes accessed | tf_op | source)
XLA Modules:
  0.0 408.4 jit_solution(11483879909976582024)
XLA Ops:
  7.2 0.0 copy-start
  7.2 2.2 multiply_convert_fusion.2
  9.4 0.9 convert_reduce_fusion
  10.3 0.7 multiply_add_fusion
  11.0 0.1 select_reduce_fusion
  11.2 0.2 fusion.18
  11.3 5.5 %convert_bitcast_fusion = bf16[256,2,16,256]{3,0,2,1:T(8,128)(2,1)S(1)} fusion(bf16[256,16,512]{2,1,0:T(8,128)(2,1)} %param.7, bf16[1,256,512]{2,1,0:T(8,128)(2,1)S(1)} %get-tuple-element.94, bf16[1,256,512]{2,1,0:T(8,128)(2,1)S(1)} %get-tuple-element.95), kind=kOutput, calls=%fused_computation.26 | convolution fusion | flops 2150629376 | bytes 8912896 | tf_op jit(solution)/shard_map/pkw,ifw->kpfi/dot_general | solution.py:58
  16.8 4.4 %copy.31 = bf16[256,2,16,256]{3,2,1,0:T(8,128)(2,1)} copy(bf16[256,2,16,256]{3,0,2,1:T(8,128)(2,1)S(1)} %convert_bitcast_fusion) | data formatting | bytes 8388608 | tf_op jit(solution)/shard_map/convert_element_type | solution.py:60
  21.2 0.1 reduce_sum.50
  21.4 0.1 broadcast_in_dim.119
  21.4 21.9 %gather_fusion.1 = bf16[512,2,16,256]{3,2,1,0:T(8,128)(2,1)} fusion(bf16[256,2,16,256]{3,2,1,0:T(8,128)(2,1)} %copy.31, s32[1024]{0:T(1024)S(1)} %pad_clamp_fusion.1), kind=kCustom, calls=%fused_computation.1 | custom fusion | bytes 16779264 | tf_op jit(solution)/shard_map/jit(_take)/gather | solution.py:90
  43.4 7.5 %select_select_fusion = bf16[32,16,2,16,256]{4,3,2,1,0:T(8,128)(2,1)} fusion(bf16[32,16,2,16,256]{4,3,2,1,0:T(8,128)(2,1)} %bitcast.59, pred[32,16]{1,0:T(8,128)(4,1)S(1)} %compare_and_fusion.1, pred[32,16]{1,0:T(8,128)(4,1)S(1)} %broadcast_in_dim.119), kind=kLoop, calls=%fused_computation.16 | loop fusion | flops 8388608 | bytes 16778240 | tf_op jit(solution)/shard_map/jit(_where)/select_n | solution.py:88
  50.9 8.8 %all-to-all-start.1 = ((bf16[32,16,2,16,256]{4,3,2,1,0:T(8,128)(2,1)}), bf16[32,16,2,16,256]{4,3,2,1,0:T(8,128)(2,1)}, u32[]{:S(2)}, u32[]{:S(2)}) async-start(bf16[32,16,2,16,256]{4,3,2,1,0:T(8,128)(2,1)} %select_select_fusion), calls=%async_computation.1 | async-start | bytes 16777216 | tf_op jit(solution)/shard_map/all_to_all | solution.py:94
  59.7 0.0 reduce-scatter.2.cloned.1.call-start
  59.8 1.0 gather_fusion.2
  60.8 0.1 dynamic-slice_convert_fusion
  60.9 0.1 select_bitcast_fusion
  61.0 15.1 %fusion.23 = bf16[16,256,256]{1,2,0:T(8,128)(2,1)S(1)} fusion(f32[256,256]{0,1:T(8,128)S(1)} %select_bitcast_fusion, f32[16]{0:T(128)S(1)} %dynamic-slice_convert_fusion), kind=kLoop, calls=%fused_computation.49 | loop fusion | flops 8388608 | bytes 2359360 | tf_op jit(solution)/shard_map/neg | solution.py:38
  76.1 16.2 %multiply_convert_fusion = (bf16[16,256,256]{1,2,0:T(8,128)(2,1)S(1)}, bf16[16,256,256]{1,2,0:T(8,128)(2,1)S(1)}) fusion(f32[256,256]{0,1:T(8,128)S(1)} %select_bitcast_fusion, f32[16]{0:T(128)S(1)} %dynamic-slice_convert_fusion), kind=kLoop, calls=%fused_computation.22 | loop fusion | flops 7340032 | bytes 4456512 | tf_op jit(solution)/shard_map/convert_element_type | solution.py:36
  92.3 3.5 maximum_bitcast_fusion
  95.8 63.6 %all-to-all-done.1 = bf16[32,16,2,16,256]{4,3,2,1,0:T(8,128)(2,1)} async-done(((bf16[32,16,2,16,256]{4,3,2,1,0:T(8,128)(2,1)}), bf16[32,16,2,16,256]{4,3,2,1,0:T(8,128)(2,1)}, u32[]{:S(2)}, u32[]{:S(2)}) %all-to-all-start.1) | async-done | bytes 8388640 | tf_op jit(solution)/shard_map/all_to_all | solution.py:94
  159.4 8.0 %copy.34 = bf16[1,16,2,32,16,256]{5,4,3,2,1,0:T(8,128)(2,1)} copy(bf16[1,16,2,32,16,256]{5,4,2,1,3,0:T(8,128)(2,1)} %bitcast.20) | data formatting | bytes 16777216 | tf_op jit(solution)/shard_map/all_to_all | solution.py:94
  167.5 11.0 %fusion.4 = f32[16,512,512,1]{1,2,3,0:T(8,128)} fusion(bf16[16,2,512,256]{3,2,1,0:T(8,128)(2,1)} %bitcast.62, bf16[16,1,256,512]{2,3,1,0:T(8,128)(2,1)} %get-tuple-element.91, bf16[16,1,256,512]{2,3,1,0:T(8,128)(2,1)S(1)} %copy-done.2), kind=kOutput, calls=%fused_computation.12 | convolution fusion | flops 4299161600 | bytes 33554432 | tf_op jit(solution)/shard_map/spfm,spmc->sfc/dot_general | solution.py:40
  178.4 0.0 reduce-scatter.2.cloned.1.call-update
  178.5 0.6 copy-done.4
  179.1 0.2 convert_reduce_fusion.1
  179.3 0.1 select_reduce_fusion.1
  179.4 0.1 reduce_sum.46
  179.6 5.0 %gather_fusion = bf16[256,2,16,256]{3,2,1,0:T(8,128)(2,1)} fusion(bf16[256,2,16,256]{3,2,1,0:T(8,128)(2,1)} %copy.31, s32[1024]{0:T(1024)S(1)} %pad_clamp_fusion.2), kind=kCustom, calls=%fused_computation | custom fusion | bytes 8389632 | tf_op jit(solution)/shard_map/jit(_take)/gather | solution.py:64
  184.6 0.1 fusion.24
  184.7 0.2 broadcast_in_dim.112
  184.9 4.0 select_select_fusion.1
  188.9 12.9 %all-to-all-start = ((bf16[128,2,2,16,256]{4,3,2,1,0:T(8,128)(2,1)}), bf16[128,2,2,16,256]{4,3,2,1,0:T(8,128)(2,1)}, u32[]{:S(2)}, u32[]{:S(2)}) async-start(bf16[128,2,2,16,256]{4,3,2,1,0:T(8,128)(2,1)} %select_select_fusion.1), calls=%async_computation | async-start | bytes 8388608 | tf_op jit(solution)/shard_map/all_to_all | solution.py:68
  201.8 52.6 %all-to-all-done = bf16[128,2,2,16,256]{4,3,2,1,0:T(8,128)(2,1)} async-done(((bf16[128,2,2,16,256]{4,3,2,1,0:T(8,128)(2,1)}), bf16[128,2,2,16,256]{4,3,2,1,0:T(8,128)(2,1)}, u32[]{:S(2)}, u32[]{:S(2)}) %all-to-all-start) | async-done | bytes 4194336 | tf_op jit(solution)/shard_map/all_to_all | solution.py:68
  254.4 141.7 %while.13 = (s32[]{:T(128)}, f32[2,2,1024,1024]{3,2,1,0:T(8,128)}, bf16[4,32,2,2,16,256]{5,4,3,2,1,0:T(8,128)(2,1)}, s32[]{:T(128)}) while((s32[]{:T(128)}, f32[2,2,1024,1024]{3,2,1,0:T(8,128)}, bf16[4,32,2,2,16,256]{5,4,3,2,1,0:T(8,128)(2,1)}, s32[]{:T(128)}) %tuple.44), condition=%wide.region_4.5_spmd, body=%wide.region_3.4_spmd.sunk | while | flops 4301258752 | bytes 132121144 | solution.py:83
  254.4 1.8 constant_dynamic-slice_fusion.3
  256.2 11.2 %convolution_bitcast_fusion.2 = f32[2,2,4,256,4,256]{3,5,0,2,1,4:T(8,128)} fusion(bf16[4,32,1,2,16,256]{5,4,3,2,1,0:T(8,128)(2,1)S(1)} %constant_dynamic-slice_fusion.3), kind=kOutput, calls=%fused_computation.3.clone.1 | convolution fusion | flops 4294967296 | bytes 18874368 | tf_op jit(solution)/shard_map/while/body/eval_jaxpr/icpfa,jcqfb->pqiajb/dot_general | solution.py:73
  267.5 19.4 %copy.60 = f32[2,2,4,256,4,256]{5,4,3,2,1,0:T(4,128)} copy(f32[2,2,4,256,4,256]{3,5,0,2,1,4:T(8,128)} %convolution_bitcast_fusion.2) | data formatting | bytes 33554432 | tf_op jit(solution)/shard_map/while/body/eval_jaxpr/icpfa,jcqfb->pqiajb/transpose | solution.py:73
  286.9 21.0 %reshape.244 = f32[2,2,1024,1024]{3,2,1,0:T(8,128)} reshape(f32[2,2,4,256,4,256]{5,4,3,2,1,0:T(4,128)} %copy.60) | data formatting | bytes 33554432 | tf_op jit(solution)/shard_map/while/body/eval_jaxpr/reshape | solution.py:76
  307.9 10.5 %slice_add_fusion.2 = (f32[1,1,1024,1024]{3,2,1,0:T(8,128)S(1)}, f32[1,1,1024,1024]{3,2,1,0:T(8,128)}) fusion(f32[2,2,1024,1024]{3,2,1,0:T(8,128)} %reshape.244), kind=kLoop, calls=%fused_computation.7.clone.1 | loop fusion | flops 2097152 | bytes 25165824 | tf_op jit(solution)/shard_map/while/body/eval_jaxpr/add | solution.py:77
  318.4 7.1 %fusion.34 = f32[2,2,1024,1024]{3,2,1,0:T(8,128)} fusion(f32[2,2,1024,1024]{3,2,1,0:T(8,128)} %get-tuple-element.124, s32[]{:T(128)} %get-tuple-element.123, f32[1,1,1024,1024]{3,2,1,0:T(8,128)} %get-tuple-element.117, f32[1,1,1024,1024]{3,2,1,0:T(8,128)S(1)} %get-tuple-element.118), kind=kLoop, calls=%fused_computation.5.clone.1 | loop fusion | flops 4194304 | bytes 16777728 | tf_op jit(solution)/shard_map/while/body/eval_jaxpr/jit(dynamic_update_index_in_dim)/dynamic_update_slice | solution.py:80
  325.5 1.8 constant_dynamic-slice_fusion.3
  327.3 11.2 %convolution_bitcast_fusion.2 = f32[2,2,4,256,4,256]{3,5,0,2,1,4:T(8,128)} fusion(bf16[4,32,1,2,16,256]{5,4,3,2,1,0:T(8,128)(2,1)S(1)} %constant_dynamic-slice_fusion.3), kind=kOutput, calls=%fused_computation.3.clone.1 | convolution fusion | flops 4294967296 | bytes 18874368 | tf_op jit(solution)/shard_map/while/body/eval_jaxpr/icpfa,jcqfb->pqiajb/dot_general | solution.py:73
  338.5 19.5 %copy.60 = f32[2,2,4,256,4,256]{5,4,3,2,1,0:T(4,128)} copy(f32[2,2,4,256,4,256]{3,5,0,2,1,4:T(8,128)} %convolution_bitcast_fusion.2) | data formatting | bytes 33554432 | tf_op jit(solution)/shard_map/while/body/eval_jaxpr/icpfa,jcqfb->pqiajb/transpose | solution.py:73
  358.0 20.7 %reshape.244 = f32[2,2,1024,1024]{3,2,1,0:T(8,128)} reshape(f32[2,2,4,256,4,256]{5,4,3,2,1,0:T(4,128)} %copy.60) | data formatting | bytes 33554432 | tf_op jit(solution)/shard_map/while/body/eval_jaxpr/reshape | solution.py:76
  378.8 10.3 %slice_add_fusion.2 = (f32[1,1,1024,1024]{3,2,1,0:T(8,128)S(1)}, f32[1,1,1024,1024]{3,2,1,0:T(8,128)}) fusion(f32[2,2,1024,1024]{3,2,1,0:T(8,128)} %reshape.244), kind=kLoop, calls=%fused_computation.7.clone.1 | loop fusion | flops 2097152 | bytes 25165824 | tf_op jit(solution)/shard_map/while/body/eval_jaxpr/add | solution.py:77
  389.1 7.0 %fusion.34 = f32[2,2,1024,1024]{3,2,1,0:T(8,128)} fusion(f32[2,2,1024,1024]{3,2,1,0:T(8,128)} %get-tuple-element.124, s32[]{:T(128)} %get-tuple-element.123, f32[1,1,1024,1024]{3,2,1,0:T(8,128)} %get-tuple-element.117, f32[1,1,1024,1024]{3,2,1,0:T(8,128)S(1)} %get-tuple-element.118), kind=kLoop, calls=%fused_computation.5.clone.1 | loop fusion | flops 4194304 | bytes 16777728 | tf_op jit(solution)/shard_map/while/body/eval_jaxpr/jit(dynamic_update_index_in_dim)/dynamic_update_slice | solution.py:80
  396.2 5.4 %copy.36 = f32[16,1,512,128]{3,2,1,0:T(8,128)} copy(f32[16,1,512,128]{2,3,0,1:T(8,128)} %bitcast.63) | data formatting | bytes 8388608
  (21 shorter events, 0.1 us)
Async XLA Ops:
  7.2 52.6 %copy-start = (f32[256,1024]{1,0:T(8,128)S(1)}, f32[256,1024]{1,0:T(8,128)}, u32[]{:S(2)}) copy-start(f32[256,1024]{1,0:T(8,128)} %param.10) | copy-start | bytes 3145732
  50.9 8.9 %copy-start.3 = (s32[256]{0:T(256)S(1)}, s32[256]{0:T(256)}, u32[]{:S(2)}) copy-start(s32[256]{0:T(256)} %param.11) | copy-start | bytes 3076
  50.9 108.5 %all-to-all-start.1 = ((bf16[32,16,2,16,256]{4,3,2,1,0:T(8,128)(2,1)}), bf16[32,16,2,16,256]{4,3,2,1,0:T(8,128)(2,1)}, u32[]{:S(2)}, u32[]{:S(2)}) async-start(bf16[32,16,2,16,256]{4,3,2,1,0:T(8,128)(2,1)} %select_select_fusion), calls=%async_computation.1 | async-start | bytes 16777216 | tf_op jit(solution)/shard_map/all_to_all | solution.py:94
  59.7 336.5 %reduce-scatter.2.cloned.1.call-start = ((), (), s32[]{:S(2)}) async-start(), calls=%async_computation.3 | async-start | bytes 20971520 | tf_op jit(solution)/shard_map/reduce_scatter | solution.py:102
  159.4 8.1 %copy-start.2 = (bf16[16,1,256,512]{2,3,1,0:T(8,128)(2,1)S(1)}, bf16[16,1,256,512]{2,3,1,0:T(8,128)(2,1)}, u32[]{:S(2)}) copy-start(bf16[16,1,256,512]{2,3,1,0:T(8,128)(2,1)} %get-tuple-element.90) | copy-start | bytes 12582916
  178.4 0.7 copy-start.4
  188.9 65.6 %all-to-all-start = ((bf16[128,2,2,16,256]{4,3,2,1,0:T(8,128)(2,1)}), bf16[128,2,2,16,256]{4,3,2,1,0:T(8,128)(2,1)}, u32[]{:S(2)}, u32[]{:S(2)}) async-start(bf16[128,2,2,16,256]{4,3,2,1,0:T(8,128)(2,1)} %select_select_fusion.1), calls=%async_computation | async-start | bytes 8388608 | tf_op jit(solution)/shard_map/all_to_all | solution.py:68
  396.2 5.4 %copy-start.1 = (f32[256,1024]{1,0:T(8,128)S(1)}, f32[256,1024]{1,0:T(8,128)}, u32[]{:S(2)}) copy-start(f32[256,1024]{1,0:T(8,128)} %param.10) | copy-start | bytes 3145732
Sparse Core Ops, SparseCore 0:
  178.6 196.6 reduce-scatter.1
where the time goes:
time: 411 us; the launch traced here: 408 us
  local copies, waits for them, and re-layouts  131 us (32%)
  waiting for transfers between devices  116 us (28%)
  other arithmetic  86.1 us (21%)
  matrix products  38.9 us (9%)
  starting transfers between devices  21.8 us (5%)
  between operations  14.2 us (3%)
    all_to_all x1, waiting for transfers between devices, shards(): lax.all_to_all(leaving, 'chan', split_axis=0, concat_axis=3, tiled=True)  63.6 us
    all_to_all x1, waiting for transfers between devices, shards(): lax.all_to_all(outgoing, ('inp', 'chan'), split_axis=0, concat_axis=0, ti...  52.6 us
    reshape x2, local copies, waits for them, and re-layouts, correlate(): products = products.reshape(2, 2, all_inputs, all_inputs)  41.8 us
    transpose x2, local copies, waits for them, and re-layouts, correlate(): jnp.einsum('icpfa,jcqfb->pqiajb', block, block, preferred_element_type=jn...  38.9 us
    dot_general x2, matrix products, correlate(): jnp.einsum('icpfa,jcqfb->pqiajb', block, block, preferred_element_type=jn...  22.5 us
    gather x1, local copies, waits for them, and re-layouts, shards(): jnp.take(spectra, beam_channel, axis=0)  21.9 us
    add x2, other arithmetic, correlate(): real_part = products[0, 0] + products[1, 1]  20.9 us
    convert_element_type x1, other arithmetic, apply_weights(): imag_weight = (-jnp.sin(angle) * inverse).astype(jnp.bfloat16)  16.2 us
  transfers between devices with their start and end apart: 3, of which 2 were waited for; matrix products, arithmetic and copies ran while one was open for 46% of the time, Pallas kernels for 0%

commit v1 on v0

v1 whole, which is shorter than its diff:
```python
import functools
import math

import jax
import jax.numpy as jnp
import ml_dtypes
import numpy as np
from jax import lax
from jax.experimental import pallas as pl
from jax.experimental.pallas import tpu as pltpu
from jax.sharding import PartitionSpec as P

BF16 = jnp.bfloat16
F32 = jnp.float32
VMEM_LIMIT = 56 * 1024 * 1024


def fourier_table(length_total):
    half_count = length_total // 2
    rows = np.arange(half_count, dtype=np.int32)
    cols = np.arange(length_total, dtype=np.int32)
    turns = (rows[:, None] * cols[None, :] % length_total).astype(np.float32)
    turns = turns * np.float32(2.0 * math.pi / length_total)
    factor = np.float32(1.0 / math.sqrt(length_total))
    both = np.stack([np.cos(turns) * factor, -np.sin(turns) * factor], axis=1)
    return both.reshape(length_total, length_total).astype(ml_dtypes.bfloat16)


def frame_major(frames):
    count = frames * frames
    matrix = np.zeros((count, count), np.float32)
    for f in range(frames):
        for i in range(frames):
            matrix[f * frames + i, i * frames + f] = 1.0
    return matrix.astype(ml_dtypes.bfloat16)


def params(**more):
    return pltpu.CompilerParams(vmem_limit_bytes=VMEM_LIMIT, **more)


def vmem():
    return pl.BlockSpec(memory_space=pltpu.VMEM)


def smem():
    return pl.BlockSpec(memory_space=pltpu.SMEM)


def channelize_body(
    slots, owner_ref, x_ref, table_ref, perm_ref, gram_ref, spec_ref, xs, rows, taken
):
    frames, inputs, width = xs.shape
    channels = spec_ref.shape[0]
    gram_channels = owner_ref.shape[0]

    def clear(o, carry):
        taken[o] = 0
        return carry

    lax.fori_loop(0, taken.shape[0], clear, 0)

    group = frames * frames

    def reorder(b, carry):
        block = x_ref[pl.ds(pl.multiple_of(b * group, group), group), :]
        moved = jnp.dot(perm_ref[...], block, preferred_element_type=F32)
        moved = moved.astype(BF16).reshape(frames, frames, width)
        xs[:, pl.ds(pl.multiple_of(b * frames, frames), frames), :] = moved
        return carry

    lax.fori_loop(0, inputs // frames, reorder, 0, unroll=2)

    def transform(f, carry):
        out = lax.dot_general(
            table_ref[...], xs[f], (((1,), (1,)), ((), ())), preferred_element_type=F32
        )
        for half in range(inputs // 128):
            rows[half, pl.ds(f, 2 * channels, stride=frames), :] = out[
                :, half * 128 : half * 128 + 128
            ]
        return carry

    lax.fori_loop(0, frames, transform, 0)

    def fetch(k):
        start = pl.multiple_of(k * 2 * frames, 2 * frames)
        both = [rows[h, pl.ds(start, 2 * frames), :] for h in range(inputs // 128)]
        return jnp.concatenate(both, axis=1).astype(BF16).reshape(2, frames, inputs)

    def low(k, carry):
        owner = owner_ref[k]
        slot = taken[owner]
        taken[owner] = slot + 1
        value = fetch(k)
        spec_ref[k] = value
        gram_ref[owner * slots + slot] = value
        return carry

    lax.fori_loop(0, gram_channels, low, 0, unroll=4)

    def high(k, carry):
        spec_ref[k] = fetch(k)
        return carry

    lax.fori_loop(gram_channels, channels, high, 0, unroll=4)


def channelize(samples, gram_owner, owner_count, slots):
    inputs, frames, width = samples.shape
    channels = width // 2
    return pl.pallas_call(
        functools.partial(channelize_body, slots),
        out_shape=(
            jax.ShapeDtypeStruct((owner_count * slots, 2, frames, inputs), BF16),
            jax.ShapeDtypeStruct((channels, 2, frames, inputs), BF16),
        ),
        in_specs=[smem(), vmem(), vmem(), vmem()],
        out_specs=(vmem(), vmem()),
        scratch_shapes=[
            pltpu.VMEM((frames, inputs, width), BF16),
            pltpu.VMEM((inputs // 128, 2 * channels * frames, 128), F32),
            pltpu.SMEM((owner_count,), jnp.int32),
        ],
        compiler_params=params(),
        name="channelize",
    )(
        gram_owner,
        samples.reshape(inputs * frames, width),
        jnp.asarray(fourier_table(width)),
        jnp.asarray(frame_major(frames)),
    )


STEP = 16


def turn(a, b, c, s):
    return a * c - b * s, b * c + a * s


def beam_body(
    first, lanes_half, spec_ref, cos_ref, sin_ref, keep_ref, a_ref, a2_ref, b_ref, b2_ref,
    cm, sm, big_c, big_s, now_c, now_s, weights,
):
    step = pl.program_id(0)
    steps = pl.num_programs(0)
    inputs, lanes = cos_ref.shape
    frames = keep_ref.shape[1]
    tiles = lanes // 128
    half = STEP // 2

    @pl.when(step == 0)
    def _():
        def start(r, carry):
            rows = pl.ds(pl.multiple_of(r * 8, 8), 8)
            for t in range(tiles):
                cols = pl.ds(t * 128, 128)
                c1, s1 = cos_ref[rows, cols], sin_ref[rows, cols]
                c, s = c1, s1
                powers = [(c1, s1)]
                cm[0, rows, cols] = c
                sm[0, rows, cols] = s
                for m in range(2, half + 1):
                    x, y = powers[m // 2 - 1], powers[m - m // 2 - 1]
                    c, s = turn(x[0], x[1], y[0], y[1])
                    powers.append((c, s))
                    cm[m - 1, rows, cols] = c
                    sm[m - 1, rows, cols] = s
                c8, s8 = powers[half - 1]
                c16, s16 = turn(c8, s8, c8, s8)
                big_c[rows, cols] = c16
                big_s[rows, cols] = s16
                a, b = c8, s8
                if first:
                    c, s = c16, s16
                    done = STEP
                    while done < first:
                        c, s = turn(c, s, c, s)
                        done *= 2
                    a, b = turn(a, b, c, s)
                lane = lax.broadcasted_iota(jnp.int32, a.shape, 1)
                real = lane < lanes_half
                scale = 1.0 / 32.0
                now_c[rows, cols] = jnp.where(real, a, -b) * scale
                now_s[rows, cols] = jnp.where(real, b, a) * scale
            return carry

        lax.fori_loop(0, inputs // 8, start, 0)

    def make(r, carry):
        rows = pl.ds(pl.multiple_of(r * 16, 16), 16)
        for t in range(tiles):
            cols = pl.ds(t * 128, 128)
            a, b = now_c[rows, cols], now_s[rows, cols]
            weights[half, rows, cols] = a.astype(BF16)
            for m in range(1, half + 1):
                p = a * cm[m - 1, rows, cols]
                q = b * sm[m - 1, rows, cols]
                weights[half - m, rows, cols] = (p + q).astype(BF16)
                if m < half:
                    weights[half + m, rows, cols] = (p - q).astype(BF16)
            c16, s16 = big_c[rows, cols], big_s[rows, cols]
            now_c[rows, cols], now_s[rows, cols] = turn(a, b, c16, s16)
        return carry

    lax.fori_loop(0, inputs // 16, make, 0)

    lane = lax.broadcasted_iota(jnp.int32, (frames, 128), 1)
    sign = jnp.where(lane < lanes_half, -1.0, 1.0).astype(F32)
    outs = []
    for m in range(STEP):
        got = jnp.dot(spec_ref[m], weights[m], preferred_element_type=F32)
        parts = []
        for t in range(tiles):
            real = got[:frames, t * 128 : t * 128 + 128]
            imag = got[frames:, t * 128 : t * 128 + 128]
            parts.append((real + sign * pltpu.roll(imag, 64, 1)).astype(BF16))
        outs.append(parts)
    for m in range(STEP):
        keep_ref[step * STEP + m] = outs[m][0]

    @pl.when(step < steps // 2)
    def _():
        for m in range(STEP):
            at = step * STEP + m
            a_ref[0, at] = outs[m][1]
            a_ref[1, at] = outs[m][3]
            a2_ref[at] = outs[m][2]

    @pl.when(step >= steps // 2)
    def _():
        for m in range(STEP):
            at = (step - steps // 2) * STEP + m
            b_ref[0, at] = outs[m][2]
            b_ref[1, at] = outs[m][3]
            b2_ref[at] = outs[m][1]


def beamform(spectra, cosines, sines, first, count):
    channels, _, frames, inputs = spectra.shape
    lanes = cosines.shape[1]
    part = count // 2
    tile = (frames, 128)
    spectra = spectra.reshape(channels, 2 * frames, inputs)
    table = pltpu.VMEM((STEP // 2, inputs, lanes), F32)
    state = pltpu.VMEM((inputs, lanes), F32)
    whole = lambda *shape: pl.BlockSpec(shape, lambda j: (0,) * len(shape))
    flops = count * 2 * (2 * frames) * inputs * lanes
    return pl.pallas_call(
        functools.partial(beam_body, first, 64),
        grid=(count // STEP,),
        out_shape=(
            jax.ShapeDtypeStruct((count, *tile), BF16),
            jax.ShapeDtypeStruct((2, part, *tile), BF16),
            jax.ShapeDtypeStruct((part, *tile), BF16),
            jax.ShapeDtypeStruct((2, part, *tile), BF16),
            jax.ShapeDtypeStruct((part, *tile), BF16),
        ),
        in_specs=[
            pl.BlockSpec((STEP, 2 * frames, inputs), lambda j: (first // STEP + j, 0, 0)),
            whole(inputs, lanes),
            whole(inputs, lanes),
        ],
        out_specs=(
            whole(count, *tile),
            whole(2, part, *tile),
            whole(part, *tile),
            whole(2, part, *tile),
            whole(part, *tile),
        ),
        scratch_shapes=[
            table, table, state, state, state, state,
            pltpu.VMEM((STEP, inputs, lanes), BF16),
        ],
        compiler_params=params(dimension_semantics=("arbitrary",)),
        cost_estimate=pl.CostEstimate(
            flops=8 * flops, bytes_accessed=count * 2 * frames * inputs * 4, transcendentals=0
        ),
        name=f"beamform_{first}",
    )(spectra, cosines, sines)


def place_body(slots, chunks, owner_ref, *refs):
    ins, out_ref, taken = refs[:-2], refs[-2], refs[-1]

    def clear(o, carry):
        taken[o] = 0
        return carry

    lax.fori_loop(0, taken.shape[0], clear, 0)
    base = 0
    for c in range(chunks):
        keep, *rest = ins[c * 5 : c * 5 + 5]
        part = rest[0].shape[1]
        for h in range(2):
            near, far = rest[2 * h], rest[2 * h + 1]

            def body(n, carry, h=h, near=near, far=far, keep=keep, base=base, part=part):
                k = base + h * part + n
                owner = owner_ref[k]
                slot = taken[owner]
                taken[owner] = slot + 1
                total = keep[h * part + n].astype(F32) + near[0, n].astype(F32)
                total = total + far[n].astype(F32)
                out_ref[owner * slots + slot] = total.astype(BF16)
                return carry

            lax.fori_loop(0, part, body, 0, unroll=4)
        base += 2 * part


def place(beam_owner, groups, owner_count, slots):
    flat = [a for g in groups for a in g]
    tile = groups[0][0].shape[1:]
    return pl.pallas_call(
        functools.partial(place_body, slots, len(groups)),
        out_shape=jax.ShapeDtypeStruct((owner_count * slots, *tile), BF16),
        in_specs=[smem()] + [vmem()] * len(flat),
        out_specs=vmem(),
        scratch_shapes=[pltpu.SMEM((owner_count,), jnp.int32)],
        compiler_params=params(),
        name="place_beams",
    )(beam_owner, *flat)


def deliver_body(live_ref, x_ref, o_ref):
    slot = pl.program_id(0)
    sources, _, frames, lanes = x_ref.shape

    @pl.when(slot < live_ref[0])
    def _():
        o_ref[0] = x_ref[:, 0].astype(F32).reshape(sources * frames, lanes)

    @pl.when(slot >= live_ref[0])
    def _():
        o_ref[0] = jnp.zeros((sources * frames, lanes), F32)


def deliver(live, arrived, sources, slots):
    _, frames, lanes = arrived.shape
    return pl.pallas_call(
        deliver_body,
        grid=(slots,),
        out_shape=jax.ShapeDtypeStruct((slots, sources * frames, lanes), F32),
        in_specs=[
            smem(),
            pl.BlockSpec((sources, 1, frames, lanes), lambda s: (0, s, 0, 0)),
        ],
        out_specs=pl.BlockSpec((1, sources * frames, lanes), lambda s: (s, 0, 0)),
        compiler_params=params(dimension_semantics=("arbitrary",)),
        name="deliver_beams",
    )(live, arrived.reshape(sources, slots, frames, lanes))


def gram_body(scale, groups, live_ref, x_ref, o_ref):
    slot, row = pl.program_id(0), pl.program_id(1)
    sources, _, _, frames, inputs = x_ref.shape
    each = sources // groups
    depth = each * frames
    over = (((0,), (0,)), ((), ()))

    @pl.when(slot < live_ref[0])
    def _():
        mine = pl.ds(row * each, each)
        r_a = x_ref[mine, 0, 0].reshape(depth, inputs)
        m_a = x_ref[mine, 0, 1].reshape(depth, inputs)
        left_re = jnp.concatenate([r_a, m_a], axis=0)
        left_im = jnp.concatenate([m_a, -r_a], axis=0)
        for b in range(groups):
            r_b = x_ref[b * each : b * each + each, 0, 0].reshape(depth, inputs)
            m_b = x_ref[b * each : b * each + each, 0, 1].reshape(depth, inputs)
            right = jnp.concatenate([r_b, m_b], axis=0)
            cols = pl.ds(b * inputs, inputs)
            re = lax.dot_general(left_re, right, over, preferred_element_type=F32)
            im = lax.dot_general(left_im, right, over, preferred_element_type=F32)
            o_ref[0, 0, :, cols] = re * scale
            o_ref[0, 1, :, cols] = im * scale

    @pl.when(slot >= live_ref[0])
    def _():
        o_ref[...] = jnp.zeros_like(o_ref)


def gram(live, arrived, groups, sources, slots):
    _, _, frames, inputs = arrived.shape
    total = groups * inputs
    scale = 1.0 / (sources // groups * frames)
    return pl.pallas_call(
        functools.partial(gram_body, scale, groups),
        grid=(slots, groups),
        out_shape=jax.ShapeDtypeStruct((slots, 2, total, total), F32),
        in_specs=[
            smem(),
            pl.BlockSpec((sources, 1, 2, frames, inputs), lambda s, a: (0, s, 0, 0, 0)),
        ],
        out_specs=pl.BlockSpec((1, 2, inputs, total), lambda s, a: (s, 0, a, 0)),
        compiler_params=params(dimension_semantics=("arbitrary", "arbitrary")),
        cost_estimate=pl.CostEstimate(
            flops=slots * 8 * total * total * (sources // groups) * frames,
            bytes_accessed=slots * 12 * total * total,
            transcendentals=0,
        ),
        name="gram",
    )(live, arrived.reshape(sources, slots, 2, frames, inputs))


def shards(samples, gram_owner, beam_owner, delays, sections):
    input_count, frame_count, length_total = samples.shape
    half_count = length_total // 2
    inp_count = lax.axis_size("inp")
    chan_count = lax.axis_size("chan")
    inp_here = lax.axis_index("inp")
    chan_here = lax.axis_index("chan")
    owner_count = inp_count * chan_count
    gram_slots = 2 * gram_owner.shape[0] // owner_count
    beam_slots = 2 * half_count // chan_count
    beam_total = delays.shape[0]
    section_width = beam_total // inp_count

    outgoing, spectra = channelize(samples, gram_owner, owner_count, gram_slots)
    arrived = lax.all_to_all(outgoing, ("inp", "chan"), split_axis=0, concat_axis=0, tiled=True)

    order = jnp.stack([inp_here, inp_here ^ 1, 3 - inp_here, 3 - (inp_here ^ 1)])
    beams = sections.reshape(inp_count, section_width)[order].reshape(-1)
    delay_cols = lax.dynamic_slice_in_dim(delays, inp_here * input_count, input_count, 1)
    theta = jnp.take(delay_cols, beams, axis=0) * (2.0 * math.pi / length_total)
    theta = theta.T.reshape(input_count, inp_count, 1, section_width)

    def lanes_of(values):
        shape = (input_count, inp_count, 2, section_width)
        return jnp.broadcast_to(values, shape).reshape(input_count, 2 * beam_total)

    cosines, sines = lanes_of(jnp.cos(theta)), lanes_of(jnp.sin(theta))

    side = [(z, z ^ 1) for z in range(inp_count)]
    back = [(z, 3 - z) for z in range(inp_count)]
    chunk = half_count // 2
    groups = []
    for first in range(0, half_count, chunk):
        keep, a, a2, b, b2 = beamform(spectra, cosines, sines, first, chunk)
        a_in = lax.ppermute(a, "inp", side)
        b_in = lax.ppermute(b, "inp", back)
        a_sum = (a2.astype(F32) + a_in[1].astype(F32)).astype(BF16)
        b_sum = (b2.astype(F32) + b_in[1].astype(F32)).astype(BF16)
        a_far = lax.ppermute(a_sum, "inp", back)
        b_far = lax.ppermute(b_sum, "inp", side)
        groups.append((keep, a_in, a_far, b_in, b_far))
    leaving = place(beam_owner, groups, chan_count, beam_slots)
    leaving, arrived = lax.optimization_barrier((leaving, arrived))
    beams_in = lax.all_to_all(leaving, "chan", split_axis=0, concat_axis=0, tiled=True)

    here = inp_here * chan_count + chan_here
    gram_live = jnp.sum((gram_owner == here).astype(jnp.int32)).reshape(1)
    beam_live = jnp.sum((beam_owner == chan_here).astype(jnp.int32)).reshape(1)
    visibilities = gram(gram_live, arrived, inp_count, owner_count, gram_slots)
    formed = deliver(beam_live, beams_in, chan_count, beam_slots)
    return (visibilities, formed[:, None])


def solution(mesh):
    return jax.shard_map(
        shards,
        mesh=mesh,
        in_specs=(P("inp", "chan", None), P(), P(), P(), P()),
        out_specs=(P(("inp", "chan"), None, None, None), P("chan", "inp", None, None)),
        check_vma=False,
    )
```

time: 411 us -> 168 us (0.41)
  local copies, waits for them, and re-layouts: 131 us -> 5.92 us
  Pallas kernels: 0 us -> 87.9 us
  other arithmetic: 86.1 us -> 5.1 us
  waiting for transfers between devices: 116 us -> 41.8 us
  matrix products: 38.9 us -> 0 us
  between operations: 14.2 us -> 0.87 us
    pallas_call x0 -> x6, Pallas kernels: none -> 87.9 us  [the longest x2 42 us: beamform(): pl.pallas_call(functools.partial(beam_body, first, 64), grid=(count // ST...]
    all_to_all x1, waiting for transfers between devices: 52.6 us -> 0.01 us  [shards(): lax.all_to_all(outgoing, ('inp', 'chan'), split_axis=0, concat_axis=0, ti...]
    all_to_all x1, waiting for transfers between devices: 63.6 us -> 14.1 us  [shards(): lax.all_to_all(leaving, 'chan', split_axis=0, concat_axis=0, tiled=True)]
    reshape x2 -> x5, local copies, waits for them, and re-layouts: 41.8 us -> 2.25 us  [the longest x2 2 us: lanes_of(): return jnp.broadcast_to(values, shape).reshape(input_count, 2 * beam_total)]
    transpose x2 -> x0, local copies, waits for them, and re-layouts: 38.9 us -> none  [correlate(): jnp.einsum('icpfa,jcqfb->pqiajb', block, block, preferred_element_type=jn...]
    dot_general x4 -> x0, matrix products: 38.9 us -> none  [the longest x2 22.5 us: correlate(): jnp.einsum('icpfa,jcqfb->pqiajb', block, block, preferred_element_type=jn...]
    ppermute x0 -> x8, waiting for transfers between devices: none -> 27.6 us  [the longest x2 19.2 us: shards(): b_in = lax.ppermute(b, 'inp', back)]
    gather x3 -> x2, local copies, waits for them, and re-layouts: 27.9 us -> 1.53 us  [the longest x1 0.97 us: shards(): theta = jnp.take(delay_cols, beams, axis=0) * (2.0 * math.pi / length_total)]
  transfers between devices with their start and end apart: 3 -> 10, of which waited for: 2 -> 7; matrix products, arithmetic and copies ran while one was open for 46% -> 5% of each run, Pallas kernels for 0% -> 36%
where the time goes in v1:
time: 168 us; the launch traced here: 167 us
  Pallas kernels  87.9 us (52%)
  waiting for transfers between devices  41.8 us (25%)
  starting transfers between devices  25.2 us (15%)
  local copies, waits for them, and re-layouts  5.92 us (4%)
  other arithmetic  5.1 us (3%)
    pallas_call x2, Pallas kernels, beamform(): pl.pallas_call(functools.partial(beam_body, first, 64), grid=(count // ST...  42 us
    ppermute x2, waiting for transfers between devices, shards(): b_in = lax.ppermute(b, 'inp', back)  19.2 us
    pallas_call x1, Pallas kernels, channelize(): pl.pallas_call(functools.partial(channelize_body, slots), out_shape=(jax....  17.9 us
    all_to_all x1, waiting for transfers between devices, shards(): lax.all_to_all(leaving, 'chan', split_axis=0, concat_axis=0, tiled=True)  14.1 us
    pallas_call x1, Pallas kernels, gram(): pl.pallas_call(functools.partial(gram_body, scale, groups), grid=(slots,...  12.4 us
    all_to_all x1, starting transfers between devices, shards(): lax.all_to_all(outgoing, ('inp', 'chan'), split_axis=0, concat_axis=0, ti...  11.9 us
    pallas_call x1, Pallas kernels, deliver(): pl.pallas_call(deliver_body, grid=(slots,), out_shape=jax.ShapeDtypeStruc...  10.5 us
    all_to_all x1, starting transfers between devices, shards(): lax.all_to_all(leaving, 'chan', split_axis=0, concat_axis=0, tiled=True)  8.06 us
  transfers between devices with their start and end apart: 10, of which 7 were waited for; matrix products, arithmetic and copies ran while one was open for 5% of the time, Pallas kernels for 36%

profile of v1, /device:TPU:1, one launch (start us, length us, event | category | flops | bytes accessed | tf_op | source)
XLA Modules:
  0.0 166.7 jit_solution(15427762213396034695)
XLA Ops:
  0.6 0.0 copy-start
  0.6 17.9 %channelize.1 = (bf16[256,2,16,256]{3,2,1,0:T(8,128)(2,1)}, bf16[256,2,16,256]{3,2,1,0:T(8,128)(2,1)}) custom-call(s32[128]{0:T(128)} %owner_ref.2, bf16[4096,512]{1,0:T(8,128)(2,1)} %bitcast.45, bf16[512,512]{1,0:T(8,128)(2,1)} %constant.44.clone.table_ref, bf16[256,256]{1,0:T(8,128)(2,1)} %constant.45.clone.perm_ref), custom_call_target="tpu_custom_call" | custom-call | tf_op jit(solution)/shard_map/channelize/pallas_call | solution.py:112
  18.6 11.9 %all-to-all-start = ((bf16[256,2,16,256]{3,2,1,0:T(8,128)(2,1)}), bf16[256,2,16,256]{3,2,1,0:T(8,128)(2,1)}, u32[]{:S(2)}, u32[]{:S(2)}) async-start(bf16[256,2,16,256]{3,2,1,0:T(8,128)(2,1)} %get-tuple-element.27), calls=%async_computation | async-start | bytes 8388608 | tf_op jit(solution)/shard_map/all_to_all | solution.py:422
  30.5 0.0 copy-done.13
  30.5 0.1 reshape.260
  30.6 0.1 fusion.8
  30.7 0.6 gather_fusion
  31.2 0.1 reshape.262
  31.3 0.1 reshape.261
  31.4 0.0 copy-done
  31.5 1.0 gather_fusion.1
  32.5 1.1 fusion.4
  33.6 1.0 copy.12.cos_ref
  34.7 1.0 copy.13.sin_ref
  35.7 21.2 %beamform_128.1 = (bf16[128,16,128]{2,1,0:T(8,128)(2,1)}, bf16[2,64,16,128]{3,2,1,0:T(8,128)(2,1)}, bf16[64,16,128]{2,1,0:T(8,128)(2,1)}, bf16[2,64,16,128]{3,2,1,0:T(8,128)(2,1)}, bf16[64,16,128]{2,1,0:T(8,128)(2,1)}) custom-call(bf16[256,32,256]{2,1,0:T(8,128)(2,1)} %bitcast.52, f32[256,512]{1,0:T(8,128)} %copy.12.cos_ref, f32[256,512]{1,0:T(8,128)} %copy.13.sin_ref), custom_call_target="tpu_custom_call" | custom-call | flops 8589934592 | bytes 4194304 | tf_op jit(solution)/shard_map/beamform_128/pallas_call | solution.py:250
  56.9 3.3 %collective-permute-start.6 = (bf16[2,64,16,128]{3,2,1,0:T(8,128)(2,1)}, bf16[2,64,16,128]{3,2,1,0:T(8,128)(2,1)S(1)}, u32[]{:S(2)}, u32[]{:S(2)}) collective-permute-start(bf16[2,64,16,128]{3,2,1,0:T(8,128)(2,1)} %get-tuple-element.25), channel_id=1, source_target_pairs={{0,96},{32,64},{64,32},{96,0},{1,97},{33,65},{65,33},{97,1},{2,98}... | collective-permute-start | bytes 1572872 | tf_op jit(solution)/shard_map/ppermute | solution.py:443
  60.2 0.0 collective-permute-start.4
  60.2 20.8 %beamform_0.1 = (bf16[128,16,128]{2,1,0:T(8,128)(2,1)}, bf16[2,64,16,128]{3,2,1,0:T(8,128)(2,1)}, bf16[64,16,128]{2,1,0:T(8,128)(2,1)}, bf16[2,64,16,128]{3,2,1,0:T(8,128)(2,1)}, bf16[64,16,128]{2,1,0:T(8,128)(2,1)}) custom-call(bf16[256,32,256]{2,1,0:T(8,128)(2,1)} %bitcast.53, f32[256,512]{1,0:T(8,128)} %copy.12.cos_ref, f32[256,512]{1,0:T(8,128)} %copy.13.sin_ref), custom_call_target="tpu_custom_call" | custom-call | flops 8589934592 | bytes 4194304 | tf_op jit(solution)/shard_map/beamform_0/pallas_call | solution.py:250
  81.0 0.3 collective-permute-start.2
  81.3 1.1 collective-permute-start
  82.4 8.4 %collective-permute-done.6.refs_8_ = bf16[2,64,16,128]{3,2,1,0:T(8,128)(2,1)S(1)} collective-permute-done((bf16[2,64,16,128]{3,2,1,0:T(8,128)(2,1)}, bf16[2,64,16,128]{3,2,1,0:T(8,128)(2,1)S(1)}, u32[]{:S(2)}, u32[]{:S(2)}) %collective-permute-start.6) | collective-permute-done | bytes 524320 | tf_op jit(solution)/shard_map/ppermute | solution.py:443
  90.8 0.1 fusion
  90.8 0.1 collective-permute-start.7
  90.9 0.0 collective-permute-done.4.refs_6_
  91.0 0.1 fusion.1
  91.1 0.2 collective-permute-start.5
  91.2 10.8 %collective-permute-done.2.refs_3_ = bf16[2,64,16,128]{3,2,1,0:T(8,128)(2,1)S(1)} collective-permute-done((bf16[2,64,16,128]{3,2,1,0:T(8,128)(2,1)}, bf16[2,64,16,128]{3,2,1,0:T(8,128)(2,1)S(1)}, u32[]{:S(2)}, u32[]{:S(2)}) %collective-permute-start.2) | collective-permute-done | bytes 524320 | tf_op jit(solution)/shard_map/ppermute | solution.py:443
  102.0 1.2 fusion.2
  103.2 0.1 collective-permute-start.3
  103.3 0.0 collective-permute-done.refs_1_
  103.3 0.0 copy-start.5
  103.3 1.2 fusion.3
  104.5 0.2 collective-permute-start.1
  104.7 1.0 collective-permute-done.7.refs_9_
  105.7 1.9 %collective-permute-done.5.refs_7_ = bf16[64,16,128]{2,1,0:T(8,128)(2,1)S(1)} collective-permute-done((bf16[64,16,128]{2,1,0:T(8,128)(2,1)S(1)}, bf16[64,16,128]{2,1,0:T(8,128)(2,1)S(1)}, u32[]{:S(2)}, u32[]{:S(2)}) %collective-permute-start.5) | collective-permute-done | bytes 262176 | tf_op jit(solution)/shard_map/ppermute | solution.py:446
  107.6 3.1 %collective-permute-done.3.refs_4_ = bf16[64,16,128]{2,1,0:T(8,128)(2,1)S(1)} collective-permute-done((bf16[64,16,128]{2,1,0:T(8,128)(2,1)S(1)}, bf16[64,16,128]{2,1,0:T(8,128)(2,1)S(1)}, u32[]{:S(2)}, u32[]{:S(2)}) %collective-permute-start.3) | collective-permute-done | bytes 262176 | tf_op jit(solution)/shard_map/ppermute | solution.py:447
  110.8 2.4 %collective-permute-done.1.refs_2_ = bf16[64,16,128]{2,1,0:T(8,128)(2,1)S(1)} collective-permute-done((bf16[64,16,128]{2,1,0:T(8,128)(2,1)S(1)}, bf16[64,16,128]{2,1,0:T(8,128)(2,1)S(1)}, u32[]{:S(2)}, u32[]{:S(2)}) %collective-permute-start.1) | collective-permute-done | bytes 262176 | tf_op jit(solution)/shard_map/ppermute | solution.py:446
  113.2 0.6 copy-done.11
  113.9 5.1 %place_beams.1 = bf16[512,16,128]{2,1,0:T(8,128)(2,1)} custom-call(s32[256]{0:T(256)} %owner_ref.3, bf16[128,16,128]{2,1,0:T(8,128)(2,1)} %get-tuple-element.17.refs_0_, bf16[2,64,16,128]{3,2,1,0:T(8,128)(2,1)} %copy-done.5, bf16[64,16,128]{2,1,0:T(8,128)(2,1)} %copy-done.11, bf16[2,64,16,128]{3,2,1,0:T(8,128)(2,1)} %copy-done.4, ...), custom_call_target="tpu_custom_call" | custom-call | tf_op jit(solution)/shard_map/place_beams/pallas_call | solution.py:316
  119.0 0.0 all-to-all-done
  119.0 8.1 %all-to-all-start.1 = ((bf16[512,16,128]{2,1,0:T(8,128)(2,1)}), bf16[512,16,128]{2,1,0:T(8,128)(2,1)S(1)}, u32[]{:S(2)}, u32[]{:S(2)}) async-start(bf16[512,16,128]{2,1,0:T(8,128)(2,1)} %place_beams.1), calls=%async_computation.1 | async-start | bytes 4194304 | tf_op jit(solution)/shard_map/all_to_all | solution.py:451
  127.0 0.0 copy-done.14
  127.1 0.6 fusion.7
  127.7 0.7 fusion.6
  128.4 12.4 %gram.1 = f32[2,2,1024,1024]{3,2,1,0:T(8,128)} custom-call(s32[1]{0:T(128)} %bitcast.live_ref, bf16[128,2,2,16,256]{4,3,2,1,0:T(8,128)(2,1)} %bitcast.19.x_ref), custom_call_target="tpu_custom_call" | custom-call | flops 8589934592 | bytes 25165824 | tf_op jit(solution)/shard_map/gram/pallas_call | solution.py:389
  140.8 14.1 %all-to-all-done.1 = bf16[512,16,128]{2,1,0:T(8,128)(2,1)S(1)} async-done(((bf16[512,16,128]{2,1,0:T(8,128)(2,1)}), bf16[512,16,128]{2,1,0:T(8,128)(2,1)S(1)}, u32[]{:S(2)}, u32[]{:S(2)}) %all-to-all-start.1) | async-done | bytes 2097184 | tf_op jit(solution)/shard_map/all_to_all | solution.py:451
  154.9 1.3 copy-done.1
  156.2 10.5 %deliver_beams.1 = f32[16,512,128]{2,1,0:T(8,128)} custom-call(s32[1]{0:T(128)} %bitcast.20.live_ref, bf16[32,16,16,128]{3,2,1,0:T(8,128)(2,1)} %bitcast.44), custom_call_target="tpu_custom_call" | custom-call | tf_op jit(solution)/shard_map/deliver_beams/pallas_call | solution.py:342
  (30 shorter events, 0.2 us)
Async XLA Ops:
  0.6 30.8 %copy-start = (f32[256,1024]{1,0:T(8,128)S(1)}, f32[256,1024]{1,0:T(8,128)}, u32[]{:S(2)}) copy-start(f32[256,1024]{1,0:T(8,128)} %param.10) | copy-start | bytes 3145732
  18.6 11.9 %copy-start.13 = (s32[256]{0:T(256)S(1)}, s32[256]{0:T(256)}, u32[]{:S(2)}) copy-start(s32[256]{0:T(256)} %param.11) | copy-start | bytes 3076
  18.6 100.4 %all-to-all-start = ((bf16[256,2,16,256]{3,2,1,0:T(8,128)(2,1)}), bf16[256,2,16,256]{3,2,1,0:T(8,128)(2,1)}, u32[]{:S(2)}, u32[]{:S(2)}) async-start(bf16[256,2,16,256]{3,2,1,0:T(8,128)(2,1)} %get-tuple-element.27), calls=%async_computation | async-start | bytes 8388608 | tf_op jit(solution)/shard_map/all_to_all | solution.py:422
  56.9 33.8 %collective-permute-start.6 = (bf16[2,64,16,128]{3,2,1,0:T(8,128)(2,1)}, bf16[2,64,16,128]{3,2,1,0:T(8,128)(2,1)S(1)}, u32[]{:S(2)}, u32[]{:S(2)}) collective-permute-start(bf16[2,64,16,128]{3,2,1,0:T(8,128)(2,1)} %get-tuple-element.25), channel_id=1, source_target_pairs={{0,96},{32,64},{64,32},{96,0},{1,97},{33,65},{65,33},{97,1},{2,98}... | collective-permute-start | bytes 1572872 | tf_op jit(solution)/shard_map/ppermute | solution.py:443
  60.2 30.6 %copy-start.7 = (bf16[64,16,128]{2,1,0:T(8,128)(2,1)S(1)}, bf16[64,16,128]{2,1,0:T(8,128)(2,1)}, u32[]{:S(2)}) copy-start(bf16[64,16,128]{2,1,0:T(8,128)(2,1)} %get-tuple-element.26) | copy-start | bytes 786436
  60.2 30.8 %copy-start.6 = (bf16[64,16,128]{2,1,0:T(8,128)(2,1)S(1)}, bf16[64,16,128]{2,1,0:T(8,128)(2,1)}, u32[]{:S(2)}) copy-start(bf16[64,16,128]{2,1,0:T(8,128)(2,1)} %get-tuple-element.24) | copy-start | bytes 786436
  60.2 30.8 %collective-permute-start.4 = (bf16[2,64,16,128]{3,2,1,0:T(8,128)(2,1)}, bf16[2,64,16,128]{3,2,1,0:T(8,128)(2,1)S(1)}, u32[]{:S(2)}, u32[]{:S(2)}) collective-permute-start(bf16[2,64,16,128]{3,2,1,0:T(8,128)(2,1)} %get-tuple-element.23), channel_id=1, source_target_pairs={{0,32},{32,0},{64,96},{96,64},{1,33},{33,1},{65,97},{97,65},{2,34}... | collective-permute-start | bytes 1572872 | tf_op jit(solution)/shard_map/ppermute | solution.py:442
  81.0 21.0 %collective-permute-start.2 = (bf16[2,64,16,128]{3,2,1,0:T(8,128)(2,1)}, bf16[2,64,16,128]{3,2,1,0:T(8,128)(2,1)S(1)}, u32[]{:S(2)}, u32[]{:S(2)}) collective-permute-start(bf16[2,64,16,128]{3,2,1,0:T(8,128)(2,1)} %get-tuple-element.20), channel_id=1, source_target_pairs={{0,96},{32,64},{64,32},{96,0},{1,97},{33,65},{65,33},{97,1},{2,98}... | collective-permute-start | bytes 1572872 | tf_op jit(solution)/shard_map/ppermute | solution.py:443
  81.3 22.0 %collective-permute-start = (bf16[2,64,16,128]{3,2,1,0:T(8,128)(2,1)}, bf16[2,64,16,128]{3,2,1,0:T(8,128)(2,1)S(1)}, u32[]{:S(2)}, u32[]{:S(2)}) collective-permute-start(bf16[2,64,16,128]{3,2,1,0:T(8,128)(2,1)} %get-tuple-element.18), channel_id=1, source_target_pairs={{0,32},{32,0},{64,96},{96,64},{1,33},{33,1},{65,97},{97,65},{2,34}... | collective-permute-start | bytes 1572872 | tf_op jit(solution)/shard_map/ppermute | solution.py:442
  90.8 22.4 %copy-start.2 = (bf16[2,64,16,128]{3,2,1,0:T(8,128)(2,1)}, bf16[2,64,16,128]{3,2,1,0:T(8,128)(2,1)S(1)}, u32[]{:S(2)}) copy-start(bf16[2,64,16,128]{3,2,1,0:T(8,128)(2,1)S(1)} %collective-permute-done.6.refs_8_) | copy-start | bytes 1572868
  90.8 14.8 %collective-permute-start.7 = (bf16[64,16,128]{2,1,0:T(8,128)(2,1)S(1)}, bf16[64,16,128]{2,1,0:T(8,128)(2,1)S(1)}, u32[]{:S(2)}, u32[]{:S(2)}) collective-permute-start(bf16[64,16,128]{2,1,0:T(8,128)(2,1)S(1)} %fusion), channel_id=1, source_target_pairs={{0,32},{32,0},{64,96},{96,64},{1,33},{33,1},{65,97},{97,65},{2,34}... | collective-permute-start | bytes 786440 | tf_op jit(solution)/shard_map/ppermute | solution.py:447
  91.0 22.2 %copy-start.3 = (bf16[2,64,16,128]{3,2,1,0:T(8,128)(2,1)}, bf16[2,64,16,128]{3,2,1,0:T(8,128)(2,1)S(1)}, u32[]{:S(2)}) copy-start(bf16[2,64,16,128]{3,2,1,0:T(8,128)(2,1)S(1)} %collective-permute-done.4.refs_6_) | copy-start | bytes 1572868
  91.1 16.6 %collective-permute-start.5 = (bf16[64,16,128]{2,1,0:T(8,128)(2,1)S(1)}, bf16[64,16,128]{2,1,0:T(8,128)(2,1)S(1)}, u32[]{:S(2)}, u32[]{:S(2)}) collective-permute-start(bf16[64,16,128]{2,1,0:T(8,128)(2,1)S(1)} %fusion.1), channel_id=1, source_target_pairs={{0,96},{32,64},{64,32},{96,0},{1,97},{33,65},{65,33},{97,1},{2,98}... | collective-permute-start | bytes 786440 | tf_op jit(solution)/shard_map/ppermute | solution.py:446
  102.0 11.2 %copy-start.4 = (bf16[2,64,16,128]{3,2,1,0:T(8,128)(2,1)}, bf16[2,64,16,128]{3,2,1,0:T(8,128)(2,1)S(1)}, u32[]{:S(2)}) copy-start(bf16[2,64,16,128]{3,2,1,0:T(8,128)(2,1)S(1)} %collective-permute-done.2.refs_3_) | copy-start | bytes 1572868
  103.2 7.6 %collective-permute-start.3 = (bf16[64,16,128]{2,1,0:T(8,128)(2,1)S(1)}, bf16[64,16,128]{2,1,0:T(8,128)(2,1)S(1)}, u32[]{:S(2)}, u32[]{:S(2)}) collective-permute-start(bf16[64,16,128]{2,1,0:T(8,128)(2,1)S(1)} %fusion.2), channel_id=1, source_target_pairs={{0,32},{32,0},{64,96},{96,64},{1,33},{33,1},{65,97},{97,65},{2,34}... | collective-permute-start | bytes 786440 | tf_op jit(solution)/shard_map/ppermute | solution.py:447
  103.3 9.9 %copy-start.5 = (bf16[2,64,16,128]{3,2,1,0:T(8,128)(2,1)}, bf16[2,64,16,128]{3,2,1,0:T(8,128)(2,1)S(1)}, u32[]{:S(2)}) copy-start(bf16[2,64,16,128]{3,2,1,0:T(8,128)(2,1)S(1)} %collective-permute-done.refs_1_) | copy-start | bytes 1572868
  104.5 8.6 %collective-permute-start.1 = (bf16[64,16,128]{2,1,0:T(8,128)(2,1)S(1)}, bf16[64,16,128]{2,1,0:T(8,128)(2,1)S(1)}, u32[]{:S(2)}, u32[]{:S(2)}) collective-permute-start(bf16[64,16,128]{2,1,0:T(8,128)(2,1)S(1)} %fusion.3), channel_id=1, source_target_pairs={{0,96},{32,64},{64,32},{96,0},{1,97},{33,65},{65,33},{97,1},{2,98}... | collective-permute-start | bytes 786440 | tf_op jit(solution)/shard_map/ppermute | solution.py:446
  105.7 7.5 %copy-start.8 = (bf16[64,16,128]{2,1,0:T(8,128)(2,1)}, bf16[64,16,128]{2,1,0:T(8,128)(2,1)S(1)}, u32[]{:S(2)}) copy-start(bf16[64,16,128]{2,1,0:T(8,128)(2,1)S(1)} %collective-permute-done.7.refs_9_) | copy-start | bytes 786436
  107.6 5.6 %copy-start.9 = (bf16[64,16,128]{2,1,0:T(8,128)(2,1)}, bf16[64,16,128]{2,1,0:T(8,128)(2,1)S(1)}, u32[]{:S(2)}) copy-start(bf16[64,16,128]{2,1,0:T(8,128)(2,1)S(1)} %collective-permute-done.5.refs_7_) | copy-start | bytes 786436
  110.8 2.4 %copy-start.10 = (bf16[64,16,128]{2,1,0:T(8,128)(2,1)}, bf16[64,16,128]{2,1,0:T(8,128)(2,1)S(1)}, u32[]{:S(2)}) copy-start(bf16[64,16,128]{2,1,0:T(8,128)(2,1)S(1)} %collective-permute-done.3.refs_4_) | copy-start | bytes 786436
  113.2 0.7 copy-start.11
  113.9 13.2 %copy-start.14 = (s32[128]{0:T(128)S(1)}, s32[128]{0:T(128)}, u32[]{:S(2)}) copy-start(s32[128]{0:T(128)} %owner_ref.2) | copy-start | bytes 1540
  113.9 13.8 %copy-start.12 = (s32[256]{0:T(256)S(1)}, s32[256]{0:T(256)}, u32[]{:S(2)}) copy-start(s32[256]{0:T(256)} %owner_ref.3) | copy-start | bytes 3076
  119.0 35.9 %all-to-all-start.1 = ((bf16[512,16,128]{2,1,0:T(8,128)(2,1)}), bf16[512,16,128]{2,1,0:T(8,128)(2,1)S(1)}, u32[]{:S(2)}, u32[]{:S(2)}) async-start(bf16[512,16,128]{2,1,0:T(8,128)(2,1)} %place_beams.1), calls=%async_computation.1 | async-start | bytes 4194304 | tf_op jit(solution)/shard_map/all_to_all | solution.py:451
  154.9 1.3 copy-start.1

commit v2 on v1

--- a/solution.py
+++ b/solution.py
@@ -47,20 +47,30 @@
     return pl.BlockSpec(memory_space=pltpu.SMEM)
 
 
+CHUNKS = 4
+PIECE = 32
+
+
 def channelize_body(
-    slots, owner_ref, x_ref, table_ref, perm_ref, gram_ref, spec_ref, xs, rows, taken
+    slots, owner_ref, x_hbm, table_ref, perm_ref, gram_hbm, spec_hbm,
+    x_ref, xs, rows, spec, taken, in_sem, gram_sem, spec_sem,
 ):
     frames, inputs, width = xs.shape
-    channels = spec_ref.shape[0]
+    channels = spec.shape[0]
     gram_channels = owner_ref.shape[0]
+    group = frames * frames
+    piece = inputs * frames // CHUNKS
+    loads = []
+    for c in range(CHUNKS):
+        part = pl.ds(c * piece, piece)
+        loads.append(pltpu.make_async_copy(x_hbm.at[part], x_ref.at[part], in_sem.at[c]))
+        loads[-1].start()
 
     def clear(o, carry):
         taken[o] = 0
         return carry
 
     lax.fori_loop(0, taken.shape[0], clear, 0)
-
-    group = frames * frames
 
     def reorder(b, carry):
         block = x_ref[pl.ds(pl.multiple_of(b * group, group), group), :]
@@ -69,19 +79,10 @@
         xs[:, pl.ds(pl.multiple_of(b * frames, frames), frames), :] = moved
         return carry
 
-    lax.fori_loop(0, inputs // frames, reorder, 0, unroll=2)
-
-    def transform(f, carry):
-        out = lax.dot_general(
-            table_ref[...], xs[f], (((1,), (1,)), ((), ())), preferred_element_type=F32
-        )
-        for half in range(inputs // 128):
-            rows[half, pl.ds(f, 2 * channels, stride=frames), :] = out[
-                :, half * 128 : half * 128 + 128
-            ]
-        return carry
-
-    lax.fori_loop(0, frames, transform, 0)
+    blocks = piece // group
+    for c in range(CHUNKS):
+        loads[c].wait()
+        lax.fori_loop(c * blocks, (c + 1) * blocks, reorder, 0, unroll=True)
 
     def fetch(k):
         start = pl.multiple_of(k * 2 * frames, 2 * frames)
@@ -92,35 +93,63 @@
         owner = owner_ref[k]
         slot = taken[owner]
         taken[owner] = slot + 1
-        value = fetch(k)
-        spec_ref[k] = value
-        gram_ref[owner * slots + slot] = value
+        spec[k] = fetch(k)
+        pltpu.make_async_copy(spec.at[k], gram_hbm.at[owner * slots + slot], gram_sem).start()
         return carry
 
-    lax.fori_loop(0, gram_channels, low, 0, unroll=4)
-
     def high(k, carry):
-        spec_ref[k] = fetch(k)
+        spec[k] = fetch(k)
         return carry
 
-    lax.fori_loop(gram_channels, channels, high, 0, unroll=4)
+    saves = []
+    for start in range(0, channels, gram_channels):
+        count = min(gram_channels, channels - start)
+
+        def transform(f, carry, start=start, count=count):
+            out = lax.dot_general(
+                table_ref[2 * start : 2 * (start + count)],
+                xs[f],
+                (((1,), (1,)), ((), ())),
+                preferred_element_type=F32,
+            )
+            for h in range(inputs // 128):
+                at = pl.ds(f + 2 * start * frames, 2 * count, stride=frames)
+                rows[h, at, :] = out[:, h * 128 : h * 128 + 128]
+            return carry
+
+        lax.fori_loop(0, frames, transform, 0, unroll=4)
+        for k in range(start, start + count, PIECE):
+            lax.fori_loop(k, k + PIECE, high if start else low, 0, unroll=4)
+            part = pl.ds(k, PIECE)
+            saves.append(pltpu.make_async_copy(spec.at[part], spec_hbm.at[part], spec_sem.at[k // PIECE]))
+            saves[-1].start()
+    all_low = pl.ds(0, gram_channels)
+    pltpu.make_async_copy(spec.at[all_low], gram_hbm.at[all_low], gram_sem).wait()
+    for save in saves:
+        save.wait()
 
 
 def channelize(samples, gram_owner, owner_count, slots):
     inputs, frames, width = samples.shape
     channels = width // 2
+    anywhere = pl.BlockSpec(memory_space=pl.ANY)
     return pl.pallas_call(
         functools.partial(channelize_body, slots),
         out_shape=(
             jax.ShapeDtypeStruct((owner_count * slots, 2, frames, inputs), BF16),
             jax.ShapeDtypeStruct((channels, 2, frames, inputs), BF16),
         ),
-        in_specs=[smem(), vmem(), vmem(), vmem()],
-        out_specs=(vmem(), vmem()),
+        in_specs=[smem(), anywhere, vmem(), vmem()],
+        out_specs=(anywhere, anywhere),
         scratch_shapes=[
+            pltpu.VMEM((inputs * frames, width), BF16),
             pltpu.VMEM((frames, inputs, width), BF16),
             pltpu.VMEM((inputs // 128, 2 * channels * frames, 128), F32),
+            pltpu.VMEM((channels, 2, frames, inputs), BF16),
             pltpu.SMEM((owner_count,), jnp.int32),
+            pltpu.SemaphoreType.DMA((CHUNKS,)),
+            pltpu.SemaphoreType.DMA(()),
+            pltpu.SemaphoreType.DMA((channels // PIECE,)),
         ],
         compiler_params=params(),
         name="channelize",
@@ -132,6 +161,50 @@
     )
 
 
+def small_turn(angle):
+    square = angle * angle
+    cosine = sine = jnp.zeros_like(angle)
+    for n in range(6, 0, -1):
+        cosine = (cosine + (-1.0) ** n / math.factorial(2 * n)) * square
+        sine = (sine + (-1.0) ** n / math.factorial(2 * n + 1)) * square
+    return 1.0 + cosine, angle + angle * sine
+
+
+def phase_body(factor, half, inp_ref, section_ref, delay_ref, cos_ref, sin_ref, turned):
+    here = inp_ref[0]
+    near = jnp.bitwise_xor(here, 1)
+    for q, device in enumerate((here, near, 3 - here, 3 - near)):
+
+        def row(t, carry, q=q, device=device):
+            beam = section_ref[device * half + t]
+            turned[pl.ds(q * half + t, 1), :] = delay_ref[pl.ds(beam, 1), :]
+            return carry
+
+        lax.fori_loop(0, half, row, 0, unroll=8)
+    for q in range(turned.shape[0] // half):
+        cosines, sines = small_turn(turned[q * half : q * half + half] * factor)
+        for source, target in ((cosines, cos_ref), (sines, sin_ref)):
+            rows = jnp.concatenate([source, source], axis=0).T
+            target[:, q * 2 * half : (q + 1) * 2 * half] = rows
+
+
+def phases(inp_here, sections, delays, inputs, half, factor):
+    beams = delays.shape[0]
+    return pl.pallas_call(
+        functools.partial(phase_body, factor, half),
+        grid_spec=pltpu.PrefetchScalarGridSpec(
+            num_scalar_prefetch=2,
+            grid=(1,),
+            in_specs=[pl.BlockSpec((beams, inputs), lambda g, inp, sec: (0, inp[0]))],
+            out_specs=[pl.BlockSpec((inputs, 2 * beams), lambda g, inp, sec: (0, 0))] * 2,
+            scratch_shapes=[pltpu.VMEM((beams, inputs), F32)],
+        ),
+        out_shape=[jax.ShapeDtypeStruct((inputs, 2 * beams), F32)] * 2,
+        compiler_params=params(),
+        name="phases",
+    )(inp_here.reshape(1), sections, delays)
+
+
 STEP = 16
 
 
@@ -140,101 +213,109 @@
 
 
 def beam_body(
-    first, lanes_half, spec_ref, cos_ref, sin_ref, keep_ref, a_ref, a2_ref, b_ref, b2_ref,
-    cm, sm, big_c, big_s, now_c, now_s, weights,
+    first, half, spec_ref, cos_ref, sin_ref, keep_ref, a_ref, a2_ref, b_ref, b2_ref,
+    big_c, big_s, now_c, now_s, even, odd, stage,
 ):
     step = pl.program_id(0)
-    steps = pl.num_programs(0)
+    last = pl.num_programs(0) - 1
     inputs, lanes = cos_ref.shape
     frames = keep_ref.shape[1]
     tiles = lanes // 128
-    half = STEP // 2
 
     @pl.when(step == 0)
     def _():
         def start(r, carry):
-            rows = pl.ds(pl.multiple_of(r * 8, 8), 8)
+            rows = pl.ds(pl.multiple_of(r * 16, 16), 16)
             for t in range(tiles):
                 cols = pl.ds(t * 128, 128)
-                c1, s1 = cos_ref[rows, cols], sin_ref[rows, cols]
-                c, s = c1, s1
-                powers = [(c1, s1)]
-                cm[0, rows, cols] = c
-                sm[0, rows, cols] = s
-                for m in range(2, half + 1):
-                    x, y = powers[m // 2 - 1], powers[m - m // 2 - 1]
-                    c, s = turn(x[0], x[1], y[0], y[1])
-                    powers.append((c, s))
-                    cm[m - 1, rows, cols] = c
-                    sm[m - 1, rows, cols] = s
-                c8, s8 = powers[half - 1]
-                c16, s16 = turn(c8, s8, c8, s8)
-                big_c[rows, cols] = c16
-                big_s[rows, cols] = s16
-                a, b = c8, s8
-                if first:
-                    c, s = c16, s16
-                    done = STEP
-                    while done < first:
-                        c, s = turn(c, s, c, s)
-                        done *= 2
-                    a, b = turn(a, b, c, s)
-                lane = lax.broadcasted_iota(jnp.int32, a.shape, 1)
-                real = lane < lanes_half
+                c, s = cos_ref[rows, cols], sin_ref[rows, cols]
+                done = 1
+                while done < STEP // 2:
+                    c, s = turn(c, s, c, s)
+                    done *= 2
+                mid = c, s
+                c, s = turn(c, s, c, s)
+                done *= 2
+                big_c[rows, cols] = c
+                big_s[rows, cols] = s
+                while done < first:
+                    c, s = turn(c, s, c, s)
+                    done *= 2
+                c, s = turn(*mid, c, s) if first else mid
+                lane = lax.broadcasted_iota(jnp.int32, c.shape, 1)
                 scale = 1.0 / 32.0
-                now_c[rows, cols] = jnp.where(real, a, -b) * scale
-                now_s[rows, cols] = jnp.where(real, b, a) * scale
+                now_c[rows, cols] = jnp.where(lane < half, c, -s) * scale
+                now_s[rows, cols] = jnp.where(lane < half, s, c) * scale
             return carry
 
-        lax.fori_loop(0, inputs // 8, start, 0)
-
-    def make(r, carry):
+        lax.fori_loop(0, inputs // 16, start, 0)
+
+    def make(r, weights):
         rows = pl.ds(pl.multiple_of(r * 16, 16), 16)
-        for t in range(tiles):
-            cols = pl.ds(t * 128, 128)
-            a, b = now_c[rows, cols], now_s[rows, cols]
-            weights[half, rows, cols] = a.astype(BF16)
-            for m in range(1, half + 1):
-                p = a * cm[m - 1, rows, cols]
-                q = b * sm[m - 1, rows, cols]
-                weights[half - m, rows, cols] = (p + q).astype(BF16)
-                if m < half:
-                    weights[half + m, rows, cols] = (p - q).astype(BF16)
-            c16, s16 = big_c[rows, cols], big_s[rows, cols]
-            now_c[rows, cols], now_s[rows, cols] = turn(a, b, c16, s16)
-        return carry
-
-    lax.fori_loop(0, inputs // 16, make, 0)
+        a, b = now_c[rows], now_s[rows]
+        c1, s1 = cos_ref[rows], sin_ref[rows]
+        twice = c1 + c1
+        p, q = a * c1, b * s1
+        below, above = (a, p + q), (a, p - q)
+        mid = STEP // 2
+        weights[mid, rows] = a.astype(BF16)
+        for m in range(1, mid + 1):
+            weights[mid - m, rows] = below[1].astype(BF16)
+            if m < mid:
+                weights[mid + m, rows] = above[1].astype(BF16)
+                below = below[1], twice * below[1] - below[0]
+                above = above[1], twice * above[1] - above[0]
+        now_c[rows], now_s[rows] = turn(a, b, big_c[rows], big_s[rows])
 
     lane = lax.broadcasted_iota(jnp.int32, (frames, 128), 1)
-    sign = jnp.where(lane < lanes_half, -1.0, 1.0).astype(F32)
-    outs = []
-    for m in range(STEP):
+    sign = jnp.where(lane < half, -1.0, 1.0).astype(F32)
+
+    def form(m, weights):
         got = jnp.dot(spec_ref[m], weights[m], preferred_element_type=F32)
         parts = []
         for t in range(tiles):
             real = got[:frames, t * 128 : t * 128 + 128]
             imag = got[frames:, t * 128 : t * 128 + 128]
-            parts.append((real + sign * pltpu.roll(imag, 64, 1)).astype(BF16))
-        outs.append(parts)
-    for m in range(STEP):
-        keep_ref[step * STEP + m] = outs[m][0]
-
-    @pl.when(step < steps // 2)
-    def _():
-        for m in range(STEP):
-            at = step * STEP + m
-            a_ref[0, at] = outs[m][1]
-            a_ref[1, at] = outs[m][3]
-            a2_ref[at] = outs[m][2]
-
-    @pl.when(step >= steps // 2)
-    def _():
-        for m in range(STEP):
-            at = (step - steps // 2) * STEP + m
-            b_ref[0, at] = outs[m][2]
-            b_ref[1, at] = outs[m][3]
-            b2_ref[at] = outs[m][1]
+            parts.append((real + sign * pltpu.roll(imag, half, 1)).astype(BF16))
+        keep_ref[m] = parts[0]
+        for t in range(1, tiles):
+            stage[t - 1, m] = parts[t]
+
+    @pl.when(step == 0)
+    def _():
+        @pl.loop(0, inputs // 16, unroll=2)
+        def _(r):
+            make(r, even)
+
+    @pl.when((step > 0) & (step < last) & (step % 2 == 1))
+    def _():
+        @pl.loop(0, STEP, unroll=True)
+        def _(r):
+            form(r, even)
+            make(r, odd)
+
+    @pl.when((step > 0) & (step < last) & (step % 2 == 0))
+    def _():
+        @pl.loop(0, STEP, unroll=True)
+        def _(r):
+            form(r, odd)
+            make(r, even)
+
+    @pl.when(step == last)
+    def _():
+        @pl.loop(0, STEP, unroll=True)
+        def _(r):
+            form(r, odd)
+
+    middle = last // 2
+
+    @pl.when((step > 0) & (step <= middle))
+    def _():
+        a_ref[0], a_ref[1], a2_ref[...] = stage[0], stage[2], stage[1]
+
+    @pl.when(step > middle)
+    def _():
+        b_ref[0], b_ref[1], b2_ref[...] = stage[1], stage[2], stage[0]
 
 
 def beamform(spectra, cosines, sines, first, count):
@@ -242,14 +323,18 @@
     lanes = cosines.shape[1]
     part = count // 2
     tile = (frames, 128)
+    steps = count // STEP
+    assert steps % 2 == 0 and inputs // 16 == STEP
     spectra = spectra.reshape(channels, 2 * frames, inputs)
-    table = pltpu.VMEM((STEP // 2, inputs, lanes), F32)
     state = pltpu.VMEM((inputs, lanes), F32)
+    at = lambda j: jnp.maximum(j - 1, 0)
+    low = lambda j: jnp.minimum(at(j), steps // 2 - 1)
+    high = lambda j: jnp.maximum(at(j) - steps // 2, 0)
     whole = lambda *shape: pl.BlockSpec(shape, lambda j: (0,) * len(shape))
     flops = count * 2 * (2 * frames) * inputs * lanes
     return pl.pallas_call(
         functools.partial(beam_body, first, 64),
-        grid=(count // STEP,),
+        grid=(steps + 1,),
         out_shape=(
             jax.ShapeDtypeStruct((count, *tile), BF16),
             jax.ShapeDtypeStruct((2, part, *tile), BF16),
@@ -258,20 +343,22 @@
             jax.ShapeDtypeStruct((part, *tile), BF16),
         ),
         in_specs=[
-            pl.BlockSpec((STEP, 2 * frames, inputs), lambda j: (first // STEP + j, 0, 0)),
+            pl.BlockSpec((STEP, 2 * frames, inputs), lambda j: (first // STEP + at(j), 0, 0)),
             whole(inputs, lanes),
             whole(inputs, lanes),
         ],
         out_specs=(
-            whole(count, *tile),
-            whole(2, part, *tile),
-            whole(part, *tile),
-            whole(2, part, *tile),
-            whole(part, *tile),
+            pl.BlockSpec((STEP, *tile), lambda j: (at(j), 0, 0)),
+            pl.BlockSpec((2, STEP, *tile), lambda j: (0, low(j), 0, 0)),
+            pl.BlockSpec((STEP, *tile), lambda j: (low(j), 0, 0)),
+            pl.BlockSpec((2, STEP, *tile), lambda j: (0, high(j), 0, 0)),
+            pl.BlockSpec((STEP, *tile), lambda j: (high(j), 0, 0)),
         ),
         scratch_shapes=[
-            table, table, state, state, state, state,
+            state, state, state, state,
             pltpu.VMEM((STEP, inputs, lanes), BF16),
+            pltpu.VMEM((STEP, inputs, lanes), BF16),
+            pltpu.VMEM((lanes // 128 - 1, STEP, *tile), BF16),
         ],
         compiler_params=params(dimension_semantics=("arbitrary",)),
         cost_estimate=pl.CostEstimate(
@@ -306,18 +393,24 @@
                 out_ref[owner * slots + slot] = total.astype(BF16)
                 return carry
 
-            lax.fori_loop(0, part, body, 0, unroll=4)
+            lax.fori_loop(0, part, body, 0, unroll=8)
         base += 2 * part
 
 
 def place(beam_owner, groups, owner_count, slots):
     flat = [a for g in groups for a in g]
     tile = groups[0][0].shape[1:]
+
+    def first_of(a):
+        shape = (1, *a.shape[1:]) if a.ndim == 4 else a.shape
+        return pl.BlockSpec(shape, lambda g: (0,) * len(shape))
+
     return pl.pallas_call(
         functools.partial(place_body, slots, len(groups)),
+        grid=(1,),
         out_shape=jax.ShapeDtypeStruct((owner_count * slots, *tile), BF16),
-        in_specs=[smem()] + [vmem()] * len(flat),
-        out_specs=vmem(),
+        in_specs=[smem()] + [first_of(a) for a in flat],
+        out_specs=pl.BlockSpec((owner_count * slots, *tile), lambda g: (0, 0, 0)),
         scratch_shapes=[pltpu.SMEM((owner_count,), jnp.int32)],
         compiler_params=params(),
         name="place_beams",
@@ -325,29 +418,31 @@
 
 
 def deliver_body(live_ref, x_ref, o_ref):
-    slot = pl.program_id(0)
-    sources, _, frames, lanes = x_ref.shape
-
-    @pl.when(slot < live_ref[0])
-    def _():
-        o_ref[0] = x_ref[:, 0].astype(F32).reshape(sources * frames, lanes)
-
-    @pl.when(slot >= live_ref[0])
-    def _():
-        o_ref[0] = jnp.zeros((sources * frames, lanes), F32)
+    sources, each, frames, lanes = x_ref.shape
+    for s in range(each):
+        slot = pl.program_id(0) * each + s
+
+        @pl.when(slot < live_ref[0])
+        def _():
+            o_ref[s] = x_ref[:, s].astype(F32).reshape(sources * frames, lanes)
+
+        @pl.when(slot >= live_ref[0])
+        def _():
+            o_ref[s] = jnp.zeros((sources * frames, lanes), F32)
 
 
 def deliver(live, arrived, sources, slots):
     _, frames, lanes = arrived.shape
+    each = 4
     return pl.pallas_call(
         deliver_body,
-        grid=(slots,),
+        grid=(slots // each,),
         out_shape=jax.ShapeDtypeStruct((slots, sources * frames, lanes), F32),
         in_specs=[
             smem(),
-            pl.BlockSpec((sources, 1, frames, lanes), lambda s: (0, s, 0, 0)),
+            pl.BlockSpec((sources, each, frames, lanes), lambda s: (0, s, 0, 0)),
         ],
-        out_specs=pl.BlockSpec((1, sources * frames, lanes), lambda s: (s, 0, 0)),
+        out_specs=pl.BlockSpec((each, sources * frames, lanes), lambda s: (s, 0, 0)),
         compiler_params=params(dimension_semantics=("arbitrary",)),
         name="deliver_beams",
     )(live, arrived.reshape(sources, slots, frames, lanes))
@@ -415,23 +510,14 @@
     owner_count = inp_count * chan_count
     gram_slots = 2 * gram_owner.shape[0] // owner_count
     beam_slots = 2 * half_count // chan_count
-    beam_total = delays.shape[0]
-    section_width = beam_total // inp_count
+    section_width = delays.shape[0] // inp_count
 
     outgoing, spectra = channelize(samples, gram_owner, owner_count, gram_slots)
     arrived = lax.all_to_all(outgoing, ("inp", "chan"), split_axis=0, concat_axis=0, tiled=True)
 
-    order = jnp.stack([inp_here, inp_here ^ 1, 3 - inp_here, 3 - (inp_here ^ 1)])
-    beams = sections.reshape(inp_count, section_width)[order].reshape(-1)
-    delay_cols = lax.dynamic_slice_in_dim(delays, inp_here * input_count, input_count, 1)
-    theta = jnp.take(delay_cols, beams, axis=0) * (2.0 * math.pi / length_total)
-    theta = theta.T.reshape(input_count, inp_count, 1, section_width)
-
-    def lanes_of(values):
-        shape = (input_count, inp_count, 2, section_width)
-        return jnp.broadcast_to(values, shape).reshape(input_count, 2 * beam_total)
-
-    cosines, sines = lanes_of(jnp.cos(theta)), lanes_of(jnp.sin(theta))
+    cosines, sines = phases(
+        inp_here, sections, delays, input_count, section_width, 2.0 * math.pi / length_total
+    )
 
     side = [(z, z ^ 1) for z in range(inp_count)]
     back = [(z, 3 - z) for z in range(inp_count)]

time: 168 us -> 156 us (0.929)
  Pallas kernels: 87.9 us -> 64.1 us
  waiting for transfers between devices: 41.8 us -> 56.9 us
  local copies, waits for them, and re-layouts: 5.92 us -> 2.04 us
    pallas_call x4 -> x5, Pallas kernels: 57.6 us -> 40.4 us  [the longest x2 26.8 us: beamform(): pl.pallas_call(functools.partial(beam_body, first, 64), grid=(steps + 1,)...]
    ppermute x2, waiting for transfers between devices: 19.2 us -> 34.5 us  [shards(): b_in = lax.ppermute(b, 'inp', back)]
    pallas_call x1, Pallas kernels: 17.9 us -> 11.4 us  [channelize(): pl.pallas_call(functools.partial(channelize_body, slots), out_shape=(jax....]
    reshape x5 -> x0, local copies, waits for them, and re-layouts: 2.25 us -> none  [the longest x2 2 us: lanes_of(): return jnp.broadcast_to(values, shape).reshape(input_count, 2 * beam_total)]
  transfers between devices with their start and end apart: 10 -> 10, of which waited for: 7 -> 7; matrix products, arithmetic and copies ran while one was open for 5% -> 3% of each run, Pallas kernels for 36% -> 31%
where the time goes in v2:
time: 156 us; the launch traced here: 154 us
  Pallas kernels  64.1 us (41%)
  waiting for transfers between devices  56.9 us (36%)
  starting transfers between devices  26.4 us (17%)
  other arithmetic  3.86 us (2%)
  local copies, waits for them, and re-layouts  2.04 us (1%)
    ppermute x2, waiting for transfers between devices, shards(): b_in = lax.ppermute(b, 'inp', back)  34.5 us
    pallas_call x2, Pallas kernels, beamform(): pl.pallas_call(functools.partial(beam_body, first, 64), grid=(steps + 1,)...  26.8 us
    all_to_all x1, waiting for transfers between devices, shards(): lax.all_to_all(leaving, 'chan', split_axis=0, concat_axis=0, tiled=True)  14.1 us
    pallas_call x1, Pallas kernels, gram(): pl.pallas_call(functools.partial(gram_body, scale, groups), grid=(slots,...  12.4 us
    all_to_all x1, starting transfers between devices, shards(): lax.all_to_all(outgoing, ('inp', 'chan'), split_axis=0, concat_axis=0, ti...  12 us
    pallas_call x1, Pallas kernels, channelize(): pl.pallas_call(functools.partial(channelize_body, slots), out_shape=(jax....  11.4 us
    all_to_all x1, starting transfers between devices, shards(): lax.all_to_all(leaving, 'chan', split_axis=0, concat_axis=0, tiled=True)  8.14 us
    pallas_call x1, Pallas kernels, deliver(): pl.pallas_call(deliver_body, grid=(slots // each,), out_shape=jax.ShapeDt...  4.98 us
  transfers between devices with their start and end apart: 10, of which 7 were waited for; matrix products, arithmetic and copies ran while one was open for 3% of the time, Pallas kernels for 31%

profile of v2, /device:TPU:1, one launch (start us, length us, event | category | flops | bytes accessed | tf_op | source)
XLA Modules:
  0.0 154.1 jit_solution(6375987491207396776)
XLA Ops:
  0.6 11.4 %channelize.1 = (bf16[256,2,16,256]{3,2,1,0:T(8,128)(2,1)}, bf16[256,2,16,256]{3,2,1,0:T(8,128)(2,1)}) custom-call(s32[128]{0:T(128)} %owner_ref.2, bf16[4096,512]{1,0:T(8,128)(2,1)} %bitcast.31, bf16[512,512]{1,0:T(8,128)(2,1)} %constant.17.clone.table_ref, bf16[256,256]{1,0:T(8,128)(2,1)} %constant.18.clone.perm_ref), custom_call_target="tpu_custom_call" | custom-call | tf_op jit(solution)/shard_map/channelize/pallas_call | solution.py:136
  12.0 12.0 %all-to-all-start = ((bf16[256,2,16,256]{3,2,1,0:T(8,128)(2,1)}), bf16[256,2,16,256]{3,2,1,0:T(8,128)(2,1)}, u32[]{:S(2)}, u32[]{:S(2)}) async-start(bf16[256,2,16,256]{3,2,1,0:T(8,128)(2,1)} %get-tuple-element.31), calls=%async_computation | async-start | bytes 8388608 | tf_op jit(solution)/shard_map/all_to_all | solution.py:516
  24.0 4.0 %phases.1 = (f32[256,512]{1,0:T(8,128)}, f32[256,512]{1,0:T(8,128)}) custom-call(s32[1]{0:T(128)} %bitcast.3.inp_ref, s32[256]{0:T(256)} %section_ref.1, f32[256,1024]{1,0:T(8,128)} %delay_ref.1), custom_call_target="tpu_custom_call" | custom-call | tf_op jit(solution)/shard_map/phases/pallas_call | solution.py:193
  28.0 13.6 %beamform_128.1 = (bf16[128,16,128]{2,1,0:T(8,128)(2,1)}, bf16[2,64,16,128]{3,2,1,0:T(8,128)(2,1)}, bf16[64,16,128]{2,1,0:T(8,128)(2,1)}, bf16[2,64,16,128]{3,2,1,0:T(8,128)(2,1)}, bf16[64,16,128]{2,1,0:T(8,128)(2,1)}) custom-call(bf16[256,32,256]{2,1,0:T(8,128)(2,1)} %bitcast.33, f32[256,512]{1,0:T(8,128)} %get-tuple-element.19.cos_ref, ...), custom_call_target="tpu_custom_call" | custom-call | flops 8589934592 | bytes 4194304 | tf_op jit(solution)/shard_map/beamform_128/pallas_call | solution.py:335
  41.5 3.3 %collective-permute-start.6 = (bf16[2,64,16,128]{3,2,1,0:T(8,128)(2,1)}, bf16[2,64,16,128]{3,2,1,0:T(8,128)(2,1)S(1)}, u32[]{:S(2)}, u32[]{:S(2)}) collective-permute-start(bf16[2,64,16,128]{3,2,1,0:T(8,128)(2,1)} %get-tuple-element.29), channel_id=1, source_target_pairs={{0,96},{32,64},{64,32},{96,0},{1,97},{33,65},{65,33},{97,1},{2,98}... | collective-permute-start | bytes 1572872 | tf_op jit(solution)/shard_map/ppermute | solution.py:529
  44.8 0.0 copy-start.6
  44.8 0.0 copy-start.5
  44.8 0.0 collective-permute-start.4
  44.8 13.2 %beamform_0.1 = (bf16[128,16,128]{2,1,0:T(8,128)(2,1)}, bf16[2,64,16,128]{3,2,1,0:T(8,128)(2,1)}, bf16[64,16,128]{2,1,0:T(8,128)(2,1)}, bf16[2,64,16,128]{3,2,1,0:T(8,128)(2,1)}, bf16[64,16,128]{2,1,0:T(8,128)(2,1)}) custom-call(bf16[256,32,256]{2,1,0:T(8,128)(2,1)} %bitcast.34, f32[256,512]{1,0:T(8,128)} %get-tuple-element.19.cos_ref, ...), custom_call_target="tpu_custom_call" | custom-call | flops 8589934592 | bytes 4194304 | tf_op jit(solution)/shard_map/beamform_0/pallas_call | solution.py:335
  58.0 0.3 collective-permute-start.2
  58.4 1.1 collective-permute-start
  59.5 24.1 %collective-permute-done.6.refs_8_ = bf16[2,64,16,128]{3,2,1,0:T(8,128)(2,1)S(1)} collective-permute-done((bf16[2,64,16,128]{3,2,1,0:T(8,128)(2,1)}, bf16[2,64,16,128]{3,2,1,0:T(8,128)(2,1)S(1)}, u32[]{:S(2)}, u32[]{:S(2)}) %collective-permute-start.6) | collective-permute-done | bytes 524320 | tf_op jit(solution)/shard_map/ppermute | solution.py:529
  83.6 0.0 copy-done.6
  83.6 0.1 fusion
  83.7 0.6 collective-permute-start.7
  84.3 0.0 collective-permute-done.4.refs_6_
  84.3 0.0 copy-done.5
  84.3 0.1 fusion.1
  84.4 0.1 collective-permute-start.5
  84.5 10.4 %collective-permute-done.2.refs_3_ = bf16[2,64,16,128]{3,2,1,0:T(8,128)(2,1)S(1)} collective-permute-done((bf16[2,64,16,128]{3,2,1,0:T(8,128)(2,1)}, bf16[2,64,16,128]{3,2,1,0:T(8,128)(2,1)S(1)}, u32[]{:S(2)}, u32[]{:S(2)}) %collective-permute-start.2) | collective-permute-done | bytes 524320 | tf_op jit(solution)/shard_map/ppermute | solution.py:529
  94.8 1.2 fusion.2
  96.0 0.8 collective-permute-start.3
  96.8 0.0 collective-permute-done.refs_1_
  96.8 1.2 fusion.3
  98.0 0.1 collective-permute-start.1
  98.1 0.3 collective-permute-done.7.refs_9_
  98.4 2.1 %collective-permute-done.5.refs_7_ = bf16[64,16,128]{2,1,0:T(8,128)(2,1)S(1)} collective-permute-done((bf16[64,16,128]{2,1,0:T(8,128)(2,1)S(1)}, bf16[64,16,128]{2,1,0:T(8,128)(2,1)S(1)}, u32[]{:S(2)}, u32[]{:S(2)}) %collective-permute-start.5) | collective-permute-done | bytes 262176 | tf_op jit(solution)/shard_map/ppermute | solution.py:532
  100.5 3.3 %collective-permute-done.3.refs_4_ = bf16[64,16,128]{2,1,0:T(8,128)(2,1)S(1)} collective-permute-done((bf16[64,16,128]{2,1,0:T(8,128)(2,1)S(1)}, bf16[64,16,128]{2,1,0:T(8,128)(2,1)S(1)}, u32[]{:S(2)}, u32[]{:S(2)}) %collective-permute-start.3) | collective-permute-done | bytes 262176 | tf_op jit(solution)/shard_map/ppermute | solution.py:533
  103.8 2.7 %collective-permute-done.1.refs_2_ = bf16[64,16,128]{2,1,0:T(8,128)(2,1)S(1)} collective-permute-done((bf16[64,16,128]{2,1,0:T(8,128)(2,1)S(1)}, bf16[64,16,128]{2,1,0:T(8,128)(2,1)S(1)}, u32[]{:S(2)}, u32[]{:S(2)}) %collective-permute-start.1) | collective-permute-done | bytes 262176 | tf_op jit(solution)/shard_map/ppermute | solution.py:532
  106.5 0.0 copy-done.1
  106.5 0.0 copy-done.2
  106.5 0.0 copy-done.3
  106.5 0.0 copy-done.4
  106.5 0.0 copy-done.7
  106.5 0.0 copy-done.8
  106.5 0.0 copy-done.9
  106.5 0.7 copy-done.10
  107.2 4.6 %place_beams.1 = bf16[512,16,128]{2,1,0:T(8,128)(2,1)} custom-call(s32[256]{0:T(256)} %owner_ref.3, bf16[128,16,128]{2,1,0:T(8,128)(2,1)} %get-tuple-element.21.refs_0_, bf16[2,64,16,128]{3,2,1,0:T(8,128)(2,1)} %copy-done.4, bf16[64,16,128]{2,1,0:T(8,128)(2,1)} %copy-done.10, bf16[2,64,16,128]{3,2,1,0:T(8,128)(2,1)} %copy-done.3, ...), custom_call_target="tpu_custom_call" | custom-call | tf_op jit(solution)/shard_map/place_beams/pallas_call | solution.py:408
  111.8 0.0 all-to-all-done
  111.8 8.1 %all-to-all-start.1 = ((bf16[512,16,128]{2,1,0:T(8,128)(2,1)}), bf16[512,16,128]{2,1,0:T(8,128)(2,1)S(1)}, u32[]{:S(2)}, u32[]{:S(2)}) async-start(bf16[512,16,128]{2,1,0:T(8,128)(2,1)} %place_beams.1), calls=%async_computation.1 | async-start | bytes 4194304 | tf_op jit(solution)/shard_map/all_to_all | solution.py:537
  120.0 0.0 copy-done.12
  120.0 0.6 fusion.5
  120.6 0.0 copy-done.11
  120.6 0.7 fusion.4
  121.3 12.4 %gram.1 = f32[2,2,1024,1024]{3,2,1,0:T(8,128)} custom-call(s32[1]{0:T(128)} %bitcast.live_ref, bf16[128,2,2,16,256]{4,3,2,1,0:T(8,128)(2,1)} %bitcast.8.x_ref), custom_call_target="tpu_custom_call" | custom-call | flops 8589934592 | bytes 25165824 | tf_op jit(solution)/shard_map/gram/pallas_call | solution.py:484
  133.7 14.1 %all-to-all-done.1 = bf16[512,16,128]{2,1,0:T(8,128)(2,1)S(1)} async-done(((bf16[512,16,128]{2,1,0:T(8,128)(2,1)}), bf16[512,16,128]{2,1,0:T(8,128)(2,1)S(1)}, u32[]{:S(2)}, u32[]{:S(2)}) %all-to-all-start.1) | async-done | bytes 2097184 | tf_op jit(solution)/shard_map/all_to_all | solution.py:537
  147.8 1.3 copy-done
  149.1 5.0 %deliver_beams.1 = f32[16,512,128]{2,1,0:T(8,128)} custom-call(s32[1]{0:T(128)} %bitcast.9.live_ref, bf16[32,16,16,128]{3,2,1,0:T(8,128)(2,1)} %bitcast.30), custom_call_target="tpu_custom_call" | custom-call | tf_op jit(solution)/shard_map/deliver_beams/pallas_call | solution.py:437
  (11 shorter events, 0.0 us)
Async XLA Ops:
  12.0 99.8 %all-to-all-start = ((bf16[256,2,16,256]{3,2,1,0:T(8,128)(2,1)}), bf16[256,2,16,256]{3,2,1,0:T(8,128)(2,1)}, u32[]{:S(2)}, u32[]{:S(2)}) async-start(bf16[256,2,16,256]{3,2,1,0:T(8,128)(2,1)} %get-tuple-element.31), calls=%async_computation | async-start | bytes 8388608 | tf_op jit(solution)/shard_map/all_to_all | solution.py:516
  41.5 42.1 %collective-permute-start.6 = (bf16[2,64,16,128]{3,2,1,0:T(8,128)(2,1)}, bf16[2,64,16,128]{3,2,1,0:T(8,128)(2,1)S(1)}, u32[]{:S(2)}, u32[]{:S(2)}) collective-permute-start(bf16[2,64,16,128]{3,2,1,0:T(8,128)(2,1)} %get-tuple-element.29), channel_id=1, source_target_pairs={{0,96},{32,64},{64,32},{96,0},{1,97},{33,65},{65,33},{97,1},{2,98}... | collective-permute-start | bytes 1572872 | tf_op jit(solution)/shard_map/ppermute | solution.py:529
  44.8 38.8 %copy-start.6 = (bf16[64,16,128]{2,1,0:T(8,128)(2,1)S(1)}, bf16[64,16,128]{2,1,0:T(8,128)(2,1)}, u32[]{:S(2)}) copy-start(bf16[64,16,128]{2,1,0:T(8,128)(2,1)} %get-tuple-element.30) | copy-start | bytes 786436
  44.8 39.5 %copy-start.5 = (bf16[64,16,128]{2,1,0:T(8,128)(2,1)S(1)}, bf16[64,16,128]{2,1,0:T(8,128)(2,1)}, u32[]{:S(2)}) copy-start(bf16[64,16,128]{2,1,0:T(8,128)(2,1)} %get-tuple-element.28) | copy-start | bytes 786436
  44.8 39.5 %collective-permute-start.4 = (bf16[2,64,16,128]{3,2,1,0:T(8,128)(2,1)}, bf16[2,64,16,128]{3,2,1,0:T(8,128)(2,1)S(1)}, u32[]{:S(2)}, u32[]{:S(2)}) collective-permute-start(bf16[2,64,16,128]{3,2,1,0:T(8,128)(2,1)} %get-tuple-element.27), channel_id=1, source_target_pairs={{0,32},{32,0},{64,96},{96,64},{1,33},{33,1},{65,97},{97,65},{2,34}... | collective-permute-start | bytes 1572872 | tf_op jit(solution)/shard_map/ppermute | solution.py:528
  58.0 36.8 %collective-permute-start.2 = (bf16[2,64,16,128]{3,2,1,0:T(8,128)(2,1)}, bf16[2,64,16,128]{3,2,1,0:T(8,128)(2,1)S(1)}, u32[]{:S(2)}, u32[]{:S(2)}) collective-permute-start(bf16[2,64,16,128]{3,2,1,0:T(8,128)(2,1)} %get-tuple-element.24), channel_id=1, source_target_pairs={{0,96},{32,64},{64,32},{96,0},{1,97},{33,65},{65,33},{97,1},{2,98}... | collective-permute-start | bytes 1572872 | tf_op jit(solution)/shard_map/ppermute | solution.py:529
  58.4 38.5 %collective-permute-start = (bf16[2,64,16,128]{3,2,1,0:T(8,128)(2,1)}, bf16[2,64,16,128]{3,2,1,0:T(8,128)(2,1)S(1)}, u32[]{:S(2)}, u32[]{:S(2)}) collective-permute-start(bf16[2,64,16,128]{3,2,1,0:T(8,128)(2,1)} %get-tuple-element.22), channel_id=1, source_target_pairs={{0,32},{32,0},{64,96},{96,64},{1,33},{33,1},{65,97},{97,65},{2,34}... | collective-permute-start | bytes 1572872 | tf_op jit(solution)/shard_map/ppermute | solution.py:528
  83.6 22.9 %copy-start.1 = (bf16[2,64,16,128]{3,2,1,0:T(8,128)(2,1)}, bf16[2,64,16,128]{3,2,1,0:T(8,128)(2,1)S(1)}, u32[]{:S(2)}) copy-start(bf16[2,64,16,128]{3,2,1,0:T(8,128)(2,1)S(1)} %collective-permute-done.6.refs_8_) | copy-start | bytes 1572868
  83.7 14.7 %collective-permute-start.7 = (bf16[64,16,128]{2,1,0:T(8,128)(2,1)S(1)}, bf16[64,16,128]{2,1,0:T(8,128)(2,1)S(1)}, u32[]{:S(2)}, u32[]{:S(2)}) collective-permute-start(bf16[64,16,128]{2,1,0:T(8,128)(2,1)S(1)} %fusion), channel_id=1, source_target_pairs={{0,32},{32,0},{64,96},{96,64},{1,33},{33,1},{65,97},{97,65},{2,34}... | collective-permute-start | bytes 786440 | tf_op jit(solution)/shard_map/ppermute | solution.py:533
  84.3 22.2 %copy-start.2 = (bf16[2,64,16,128]{3,2,1,0:T(8,128)(2,1)}, bf16[2,64,16,128]{3,2,1,0:T(8,128)(2,1)S(1)}, u32[]{:S(2)}) copy-start(bf16[2,64,16,128]{3,2,1,0:T(8,128)(2,1)S(1)} %collective-permute-done.4.refs_6_) | copy-start | bytes 1572868
  84.4 16.1 %collective-permute-start.5 = (bf16[64,16,128]{2,1,0:T(8,128)(2,1)S(1)}, bf16[64,16,128]{2,1,0:T(8,128)(2,1)S(1)}, u32[]{:S(2)}, u32[]{:S(2)}) collective-permute-start(bf16[64,16,128]{2,1,0:T(8,128)(2,1)S(1)} %fusion.1), channel_id=1, source_target_pairs={{0,96},{32,64},{64,32},{96,0},{1,97},{33,65},{65,33},{97,1},{2,98}... | collective-permute-start | bytes 786440 | tf_op jit(solution)/shard_map/ppermute | solution.py:532
  94.8 11.6 %copy-start.3 = (bf16[2,64,16,128]{3,2,1,0:T(8,128)(2,1)}, bf16[2,64,16,128]{3,2,1,0:T(8,128)(2,1)S(1)}, u32[]{:S(2)}) copy-start(bf16[2,64,16,128]{3,2,1,0:T(8,128)(2,1)S(1)} %collective-permute-done.2.refs_3_) | copy-start | bytes 1572868
  96.0 7.7 %collective-permute-start.3 = (bf16[64,16,128]{2,1,0:T(8,128)(2,1)S(1)}, bf16[64,16,128]{2,1,0:T(8,128)(2,1)S(1)}, u32[]{:S(2)}, u32[]{:S(2)}) collective-permute-start(bf16[64,16,128]{2,1,0:T(8,128)(2,1)S(1)} %fusion.2), channel_id=1, source_target_pairs={{0,32},{32,0},{64,96},{96,64},{1,33},{33,1},{65,97},{97,65},{2,34}... | collective-permute-start | bytes 786440 | tf_op jit(solution)/shard_map/ppermute | solution.py:533
  96.8 9.7 %copy-start.4 = (bf16[2,64,16,128]{3,2,1,0:T(8,128)(2,1)}, bf16[2,64,16,128]{3,2,1,0:T(8,128)(2,1)S(1)}, u32[]{:S(2)}) copy-start(bf16[2,64,16,128]{3,2,1,0:T(8,128)(2,1)S(1)} %collective-permute-done.refs_1_) | copy-start | bytes 1572868
  98.0 8.4 %collective-permute-start.1 = (bf16[64,16,128]{2,1,0:T(8,128)(2,1)S(1)}, bf16[64,16,128]{2,1,0:T(8,128)(2,1)S(1)}, u32[]{:S(2)}, u32[]{:S(2)}) collective-permute-start(bf16[64,16,128]{2,1,0:T(8,128)(2,1)S(1)} %fusion.3), channel_id=1, source_target_pairs={{0,96},{32,64},{64,32},{96,0},{1,97},{33,65},{65,33},{97,1},{2,98}... | collective-permute-start | bytes 786440 | tf_op jit(solution)/shard_map/ppermute | solution.py:532
  98.4 8.1 %copy-start.7 = (bf16[64,16,128]{2,1,0:T(8,128)(2,1)}, bf16[64,16,128]{2,1,0:T(8,128)(2,1)S(1)}, u32[]{:S(2)}) copy-start(bf16[64,16,128]{2,1,0:T(8,128)(2,1)S(1)} %collective-permute-done.7.refs_9_) | copy-start | bytes 786436
  100.5 6.0 %copy-start.8 = (bf16[64,16,128]{2,1,0:T(8,128)(2,1)}, bf16[64,16,128]{2,1,0:T(8,128)(2,1)S(1)}, u32[]{:S(2)}) copy-start(bf16[64,16,128]{2,1,0:T(8,128)(2,1)S(1)} %collective-permute-done.5.refs_7_) | copy-start | bytes 786436
  103.8 2.7 %copy-start.9 = (bf16[64,16,128]{2,1,0:T(8,128)(2,1)}, bf16[64,16,128]{2,1,0:T(8,128)(2,1)S(1)}, u32[]{:S(2)}) copy-start(bf16[64,16,128]{2,1,0:T(8,128)(2,1)S(1)} %collective-permute-done.3.refs_4_) | copy-start | bytes 786436
  106.5 0.7 copy-start.10
  107.2 12.8 %copy-start.12 = (s32[128]{0:T(128)S(1)}, s32[128]{0:T(128)}, u32[]{:S(2)}) copy-start(s32[128]{0:T(128)} %owner_ref.2) | copy-start | bytes 1540
  107.2 13.4 %copy-start.11 = (s32[256]{0:T(256)S(1)}, s32[256]{0:T(256)}, u32[]{:S(2)}) copy-start(s32[256]{0:T(256)} %owner_ref.3) | copy-start | bytes 3076
  111.8 36.0 %all-to-all-start.1 = ((bf16[512,16,128]{2,1,0:T(8,128)(2,1)}), bf16[512,16,128]{2,1,0:T(8,128)(2,1)S(1)}, u32[]{:S(2)}, u32[]{:S(2)}) async-start(bf16[512,16,128]{2,1,0:T(8,128)(2,1)} %place_beams.1), calls=%async_computation.1 | async-start | bytes 4194304 | tf_op jit(solution)/shard_map/all_to_all | solution.py:537
  147.8 1.3 copy-start

commit v3 on v2

--- a/solution.py
+++ b/solution.py
@@ -52,7 +52,7 @@
 
 
 def channelize_body(
-    slots, owner_ref, x_hbm, table_ref, perm_ref, gram_hbm, spec_hbm,
+    slots, groups, owner_ref, inp_ref, x_hbm, table_ref, perm_ref, gram_hbm, more_hbm, spec_hbm,
     x_ref, xs, rows, spec, taken, in_sem, gram_sem, spec_sem,
 ):
     frames, inputs, width = xs.shape
@@ -94,7 +94,18 @@
         slot = taken[owner]
         taken[owner] = slot + 1
         spec[k] = fetch(k)
-        pltpu.make_async_copy(spec.at[k], gram_hbm.at[owner * slots + slot], gram_sem).start()
+
+        @pl.when(slot == 0)
+        def _():
+            pltpu.make_async_copy(spec.at[k], gram_hbm.at[owner], gram_sem).start()
+
+        @pl.when(slot > 0)
+        def _():
+            chans = taken.shape[0] // groups
+            ahead = lax.rem(lax.div(owner, chans) - inp_ref[0] + groups, groups)
+            at = (lax.rem(owner, chans) * groups + ahead) * (slots - 1) + slot - 1
+            pltpu.make_async_copy(spec.at[k], more_hbm.at[at], gram_sem).start()
+
         return carry
 
     def high(k, carry):
@@ -129,18 +140,19 @@
         save.wait()
 
 
-def channelize(samples, gram_owner, owner_count, slots):
+def channelize(samples, gram_owner, inp_here, owner_count, groups, slots):
     inputs, frames, width = samples.shape
     channels = width // 2
     anywhere = pl.BlockSpec(memory_space=pl.ANY)
     return pl.pallas_call(
-        functools.partial(channelize_body, slots),
+        functools.partial(channelize_body, slots, groups),
         out_shape=(
-            jax.ShapeDtypeStruct((owner_count * slots, 2, frames, inputs), BF16),
+            jax.ShapeDtypeStruct((owner_count, 2, frames, inputs), BF16),
+            jax.ShapeDtypeStruct((owner_count * (slots - 1), 2, frames, inputs), BF16),
             jax.ShapeDtypeStruct((channels, 2, frames, inputs), BF16),
         ),
-        in_specs=[smem(), anywhere, vmem(), vmem()],
-        out_specs=(anywhere, anywhere),
+        in_specs=[smem(), smem(), anywhere, vmem(), vmem()],
+        out_specs=(anywhere, anywhere, anywhere),
         scratch_shapes=[
             pltpu.VMEM((inputs * frames, width), BF16),
             pltpu.VMEM((frames, inputs, width), BF16),
@@ -155,6 +167,7 @@
         name="channelize",
     )(
         gram_owner,
+        inp_here.reshape(1),
         samples.reshape(inputs * frames, width),
         jnp.asarray(fourier_table(width)),
         jnp.asarray(frame_major(frames)),
@@ -170,7 +183,9 @@
     return 1.0 + cosine, angle + angle * sine
 
 
-def phase_body(factor, half, inp_ref, section_ref, delay_ref, cos_ref, sin_ref, turned):
+def phase_body(
+    factor, half, inp_ref, section_ref, delay_ref, cos_ref, sin_ref, turned
+):
     here = inp_ref[0]
     near = jnp.bitwise_xor(here, 1)
     for q, device in enumerate((here, near, 3 - here, 3 - near)):
@@ -195,8 +210,11 @@
         grid_spec=pltpu.PrefetchScalarGridSpec(
             num_scalar_prefetch=2,
             grid=(1,),
-            in_specs=[pl.BlockSpec((beams, inputs), lambda g, inp, sec: (0, inp[0]))],
-            out_specs=[pl.BlockSpec((inputs, 2 * beams), lambda g, inp, sec: (0, 0))] * 2,
+            in_specs=[pl.BlockSpec((beams, inputs), lambda g, inp, *_: (0, inp[0]))],
+            out_specs=[
+                pl.BlockSpec((inputs, 2 * beams), lambda g, *_: (0, 0)),
+                pl.BlockSpec((inputs, 2 * beams), lambda g, *_: (0, 0)),
+            ],
             scratch_shapes=[pltpu.VMEM((beams, inputs), F32)],
         ),
         out_shape=[jax.ShapeDtypeStruct((inputs, 2 * beams), F32)] * 2,
@@ -206,6 +224,7 @@
 
 
 STEP = 16
+CHANNEL_CHUNKS = ((0, 128), (128, 128))
 
 
 def turn(a, b, c, s):
@@ -238,10 +257,12 @@
                 done *= 2
                 big_c[rows, cols] = c
                 big_s[rows, cols] = s
-                while done < first:
+                while done <= first:
+                    if first & done:
+                        mid = turn(*mid, c, s)
                     c, s = turn(c, s, c, s)
                     done *= 2
-                c, s = turn(*mid, c, s) if first else mid
+                c, s = mid
                 lane = lax.broadcasted_iota(jnp.int32, c.shape, 1)
                 scale = 1.0 / 32.0
                 now_c[rows, cols] = jnp.where(lane < half, c, -s) * scale
@@ -368,53 +389,63 @@
     )(spectra, cosines, sines)
 
 
-def place_body(slots, chunks, owner_ref, *refs):
-    ins, out_ref, taken = refs[:-2], refs[-2], refs[-1]
+def place_body(first, slots, owner_ref, keep, a_near, a_far, b_near, b_far, *rest):
+    out_hbm, total, taken, sem = rest[-4:]
+    part = a_far.shape[0]
 
     def clear(o, carry):
         taken[o] = 0
         return carry
 
-    lax.fori_loop(0, taken.shape[0], clear, 0)
-    base = 0
-    for c in range(chunks):
-        keep, *rest = ins[c * 5 : c * 5 + 5]
-        part = rest[0].shape[1]
-        for h in range(2):
-            near, far = rest[2 * h], rest[2 * h + 1]
-
-            def body(n, carry, h=h, near=near, far=far, keep=keep, base=base, part=part):
-                k = base + h * part + n
-                owner = owner_ref[k]
-                slot = taken[owner]
-                taken[owner] = slot + 1
-                total = keep[h * part + n].astype(F32) + near[0, n].astype(F32)
-                total = total + far[n].astype(F32)
-                out_ref[owner * slots + slot] = total.astype(BF16)
-                return carry
-
-            lax.fori_loop(0, part, body, 0, unroll=8)
-        base += 2 * part
-
-
-def place(beam_owner, groups, owner_count, slots):
-    flat = [a for g in groups for a in g]
-    tile = groups[0][0].shape[1:]
+    lax.fori_loop(0, taken.shape[0], clear, 0, unroll=8)
+
+    def count(k, carry):
+        taken[owner_ref[k]] = taken[owner_ref[k]] + 1
+        return carry
+
+    if first:
+        lax.fori_loop(0, first, count, 0, unroll=8)
+    for h, (near, far) in enumerate(((a_near, a_far), (b_near, b_far))):
+
+        def body(n, carry, h=h, near=near, far=far):
+            k = h * part + n
+            owner = owner_ref[first + k]
+            slot = taken[owner]
+            taken[owner] = slot + 1
+            value = keep[k].astype(F32) + near[0, n].astype(F32) + far[n].astype(F32)
+            total[k] = value.astype(BF16)
+            pltpu.make_async_copy(total.at[k], out_hbm.at[owner * slots + slot], sem).start()
+            return carry
+
+        lax.fori_loop(0, part, body, 0, unroll=8)
+    pltpu.make_async_copy(total, out_hbm.at[pl.ds(0, 2 * part)], sem).wait()
+
+
+def place(beam_owner, first, group, owner_count, slots, before):
+    tile = group[0].shape[1:]
+    count = group[0].shape[0]
+    anywhere = pl.BlockSpec(memory_space=pl.ANY)
 
     def first_of(a):
         shape = (1, *a.shape[1:]) if a.ndim == 4 else a.shape
         return pl.BlockSpec(shape, lambda g: (0,) * len(shape))
 
+    more = [] if before is None else [before]
     return pl.pallas_call(
-        functools.partial(place_body, slots, len(groups)),
+        functools.partial(place_body, first, slots),
         grid=(1,),
         out_shape=jax.ShapeDtypeStruct((owner_count * slots, *tile), BF16),
-        in_specs=[smem()] + [first_of(a) for a in flat],
-        out_specs=pl.BlockSpec((owner_count * slots, *tile), lambda g: (0, 0, 0)),
-        scratch_shapes=[pltpu.SMEM((owner_count,), jnp.int32)],
+        in_specs=[smem()] + [first_of(a) for a in group] + [anywhere] * len(more),
+        out_specs=anywhere,
+        scratch_shapes=[
+            pltpu.VMEM((count, *tile), BF16),
+            pltpu.SMEM((owner_count,), jnp.int32),
+            pltpu.SemaphoreType.DMA(()),
+        ],
+        input_output_aliases={6: 0} if more else {},
         compiler_params=params(),
-        name="place_beams",
-    )(beam_owner, *flat)
+        name=f"place_beams_{first}",
+    )(beam_owner, *group, *more)
 
 
 def deliver_body(live_ref, x_ref, o_ref):
@@ -448,56 +479,73 @@
     )(live, arrived.reshape(sources, slots, frames, lanes))
 
 
-def gram_body(scale, groups, live_ref, x_ref, o_ref):
-    slot, row = pl.program_id(0), pl.program_id(1)
-    sources, _, _, frames, inputs = x_ref.shape
-    each = sources // groups
-    depth = each * frames
+def gram_body(scale, slot, blocks, here_ref, live_ref, *refs):
+    ins, o_ref, xs = refs[:blocks], refs[-2], refs[-1]
+    row = pl.program_id(0)
+    groups, _, depth, inputs = xs.shape
     over = (((0,), (0,)), ((), ()))
 
-    @pl.when(slot < live_ref[0])
-    def _():
-        mine = pl.ds(row * each, each)
-        r_a = x_ref[mine, 0, 0].reshape(depth, inputs)
-        m_a = x_ref[mine, 0, 1].reshape(depth, inputs)
+    @pl.when(live_ref[0] > slot)
+    def _():
+        @pl.when(row == 0)
+        def _():
+            for n, ref in enumerate(ins):
+                parts = groups // blocks
+                value = ref[...].reshape(parts, -1, 2, *ref.shape[-2:])
+                for d in range(parts):
+                    for p in range(2):
+                        xs[n * parts + d, p] = value[d, :, p].reshape(depth, inputs)
+
+        r_a, m_a = xs[row, 0], xs[row, 1]
         left_re = jnp.concatenate([r_a, m_a], axis=0)
         left_im = jnp.concatenate([m_a, -r_a], axis=0)
-        for b in range(groups):
-            r_b = x_ref[b * each : b * each + each, 0, 0].reshape(depth, inputs)
-            m_b = x_ref[b * each : b * each + each, 0, 1].reshape(depth, inputs)
-            right = jnp.concatenate([r_b, m_b], axis=0)
-            cols = pl.ds(b * inputs, inputs)
+        for d in range(groups):
+            right = xs[d].reshape(2 * depth, inputs)
+            block = lax.rem(here_ref[0] - d + groups, groups) if blocks > 1 else d
+            cols = pl.ds(pl.multiple_of(block * inputs, inputs), inputs)
             re = lax.dot_general(left_re, right, over, preferred_element_type=F32)
             im = lax.dot_general(left_im, right, over, preferred_element_type=F32)
             o_ref[0, 0, :, cols] = re * scale
             o_ref[0, 1, :, cols] = im * scale
 
-    @pl.when(slot >= live_ref[0])
+    @pl.when(live_ref[0] <= slot)
     def _():
         o_ref[...] = jnp.zeros_like(o_ref)
 
 
-def gram(live, arrived, groups, sources, slots):
-    _, _, frames, inputs = arrived.shape
+def gram(here, live, arrays, groups, slot, slots, before):
+    frames, inputs = arrays[-1].shape[-2:]
     total = groups * inputs
-    scale = 1.0 / (sources // groups * frames)
+    blocks = len(arrays)
+    depth = arrays[-1].shape[0] * frames * blocks // groups
+    back = lambda a, here: lax.rem(here[0] - a + groups, groups) if blocks > 1 else a
+    whole = lambda x: pl.BlockSpec(x.shape, lambda a, *_: (0,) * x.ndim)
+    first = [whole(arrays[0])]
+    if blocks > 1:
+        chans, _, _, *rest = arrays[0].shape
+        first = [pl.BlockSpec((chans, 1, 1, *rest), lambda a, *_: (0, 0, slot - 1, 0, 0, 0))]
+    more = [] if before is None else [before]
     return pl.pallas_call(
-        functools.partial(gram_body, scale, groups),
-        grid=(slots, groups),
+        functools.partial(gram_body, 1.0 / depth, slot, blocks),
+        grid_spec=pltpu.PrefetchScalarGridSpec(
+            num_scalar_prefetch=2,
+            grid=(groups,),
+            in_specs=first
+            + [whole(x) for x in arrays[1:]]
+            + [pl.BlockSpec(memory_space=pl.ANY)] * len(more),
+            out_specs=pl.BlockSpec(
+                (1, 2, inputs, total), lambda a, here, live: (slot, 0, back(a, here), 0)
+            ),
+            scratch_shapes=[pltpu.VMEM((groups, 2, depth, inputs), BF16)],
+        ),
         out_shape=jax.ShapeDtypeStruct((slots, 2, total, total), F32),
-        in_specs=[
-            smem(),
-            pl.BlockSpec((sources, 1, 2, frames, inputs), lambda s, a: (0, s, 0, 0, 0)),
-        ],
-        out_specs=pl.BlockSpec((1, 2, inputs, total), lambda s, a: (s, 0, a, 0)),
-        compiler_params=params(dimension_semantics=("arbitrary", "arbitrary")),
+        input_output_aliases={2 + blocks: 0} if more else {},
+        compiler_params=params(dimension_semantics=("arbitrary",)),
         cost_estimate=pl.CostEstimate(
-            flops=slots * 8 * total * total * (sources // groups) * frames,
-            bytes_accessed=slots * 12 * total * total,
-            transcendentals=0,
+            flops=8 * total * total * depth, bytes_accessed=12 * total * total, transcendentals=0
         ),
-        name="gram",
-    )(live, arrived.reshape(sources, slots, 2, frames, inputs))
+        name=f"gram_{slot}",
+    )(here, live, *arrays, *more)
 
 
 def shards(samples, gram_owner, beam_owner, delays, sections):
@@ -512,7 +560,9 @@
     beam_slots = 2 * half_count // chan_count
     section_width = delays.shape[0] // inp_count
 
-    outgoing, spectra = channelize(samples, gram_owner, owner_count, gram_slots)
+    outgoing, later, spectra = channelize(
+        samples, gram_owner, inp_here, owner_count, inp_count, gram_slots
+    )
     arrived = lax.all_to_all(outgoing, ("inp", "chan"), split_axis=0, concat_axis=0, tiled=True)
 
     cosines, sines = phases(
@@ -521,25 +571,47 @@
 
     side = [(z, z ^ 1) for z in range(inp_count)]
     back = [(z, 3 - z) for z in range(inp_count)]
-    chunk = half_count // 2
-    groups = []
-    for first in range(0, half_count, chunk):
-        keep, a, a2, b, b2 = beamform(spectra, cosines, sines, first, chunk)
-        a_in = lax.ppermute(a, "inp", side)
-        b_in = lax.ppermute(b, "inp", back)
+    parts = []
+    near = []
+    for first, count in CHANNEL_CHUNKS:
+        keep, a, a2, b, b2 = beamform(spectra, cosines, sines, first, count)
+        spectra, keep = lax.optimization_barrier((spectra, keep))
+        parts.append((keep, a, a2, b, b2))
+        if first + count < half_count:
+            near.append((lax.ppermute(a, "inp", side), lax.ppermute(b, "inp", back)))
+    later, arrived, parts, near = lax.optimization_barrier((later, arrived, parts, near))
+    later = lax.all_to_all(later, "chan", split_axis=0, concat_axis=0, tiled=True)
+    later = later.reshape(chan_count, inp_count, gram_slots - 1, *later.shape[1:])
+    near.append((lax.ppermute(parts[-1][1], "inp", side), lax.ppermute(parts[-1][3], "inp", back)))
+    far = []
+    for n, (_, _, a2, _, b2) in enumerate(parts):
+        a_in, b_in = near[n]
+        if far:
+            a_in, b_in, far[-1] = lax.optimization_barrier((a_in, b_in, far[-1]))
         a_sum = (a2.astype(F32) + a_in[1].astype(F32)).astype(BF16)
         b_sum = (b2.astype(F32) + b_in[1].astype(F32)).astype(BF16)
-        a_far = lax.ppermute(a_sum, "inp", back)
-        b_far = lax.ppermute(b_sum, "inp", side)
-        groups.append((keep, a_in, a_far, b_in, b_far))
-    leaving = place(beam_owner, groups, chan_count, beam_slots)
-    leaving, arrived = lax.optimization_barrier((leaving, arrived))
+        far.append((lax.ppermute(a_sum, "inp", back), lax.ppermute(b_sum, "inp", side)))
+        near[n] = (a_in, b_in)
+    leaving = None
+    for (first, _), (keep, *_), (a_in, b_in), (a_far, b_far) in zip(CHANNEL_CHUNKS, parts, near, far):
+        group = (keep, a_in, a_far, b_in, b_far)
+        leaving = place(beam_owner, first, group, chan_count, beam_slots, leaving)
+    leaving, later = lax.optimization_barrier((leaving, later))
     beams_in = lax.all_to_all(leaving, "chan", split_axis=0, concat_axis=0, tiled=True)
 
     here = inp_here * chan_count + chan_here
     gram_live = jnp.sum((gram_owner == here).astype(jnp.int32)).reshape(1)
     beam_live = jnp.sum((beam_owner == chan_here).astype(jnp.int32)).reshape(1)
-    visibilities = gram(gram_live, arrived, inp_count, owner_count, gram_slots)
+    at = inp_here.reshape(1)
+    visibilities = gram(at, gram_live, [arrived], inp_count, 0, gram_slots, None)
+    for slot in range(1, gram_slots):
+        moved = [
+            lax.ppermute(later[:, d, slot - 1], "inp", [(z, (z + d) % inp_count) for z in range(inp_count)])
+            for d in range(1, inp_count)
+        ]
+        visibilities = gram(
+            at, gram_live, [later, *moved], inp_count, slot, gram_slots, visibilities
+        )
     formed = deliver(beam_live, beams_in, chan_count, beam_slots)
     return (visibilities, formed[:, None])
 

time: 156 us -> 155 us (level)
  waiting for transfers between devices: 56.9 us -> 36.5 us
  starting transfers between devices: 26.4 us -> 38.3 us
  Pallas kernels: 64.1 us -> 71.5 us
    all_to_all x1, waiting for transfers between devices: 14.1 us -> 0.01 us  [shards(): lax.all_to_all(leaving, 'chan', split_axis=0, concat_axis=0, tiled=True)]
    pallas_call x3 -> x5, Pallas kernels: 28.4 us -> 35.8 us  [the longest x2 17.9 us: gram(): pl.pallas_call(functools.partial(gram_body, 1.0 / depth, slot, blocks), g...]
    ppermute x8 -> x11, waiting for transfers between devices: 42.8 us -> 36.5 us  [the longest x2 15.7 us: shards(): lax.ppermute(b_sum, 'inp', side)]
    all_to_all x0 -> x1, starting transfers between devices: none -> 5.99 us  [shards(): lax.all_to_all(later, 'chan', split_axis=0, concat_axis=0, tiled=True)]
    ppermute x8 -> x11, starting transfers between devices: 6.31 us -> 11.3 us  [the longest x2 3.56 us: shards(): near.append((lax.ppermute(a, 'inp', side), lax.ppermute(b, 'inp', back)))]
  transfers between devices with their start and end apart: 10 -> 14, of which waited for: 7 -> 8; matrix products, arithmetic and copies ran while one was open for 3% -> 2% of each run, Pallas kernels for 31% -> 35%
where the time goes in v3:
time: 155 us; the launch traced here: 154 us
  Pallas kernels  71.5 us (46%)
  starting transfers between devices  38.3 us (25%)
  waiting for transfers between devices  36.5 us (24%)
  other arithmetic  3.45 us (2%)
  local copies, waits for them, and re-layouts  3.26 us (2%)
    pallas_call x2, Pallas kernels, beamform(): pl.pallas_call(functools.partial(beam_body, first, 64), grid=(steps + 1,)...  26.8 us
    pallas_call x2, Pallas kernels, gram(): pl.pallas_call(functools.partial(gram_body, 1.0 / depth, slot, blocks), g...  17.9 us
    ppermute x2, waiting for transfers between devices, shards(): lax.ppermute(b_sum, 'inp', side)  15.7 us
    ppermute x3, waiting for transfers between devices, shards(): lax.ppermute(later[:, d, slot - 1], 'inp', [(z, (z + d) % inp_count) for...  13.7 us
    pallas_call x1, Pallas kernels, channelize(): pl.pallas_call(functools.partial(channelize_body, slots, groups), out_sha...  12.1 us
    all_to_all x1, starting transfers between devices, shards(): lax.all_to_all(outgoing, ('inp', 'chan'), split_axis=0, concat_axis=0, ti...  11.5 us
    all_to_all x1, starting transfers between devices, shards(): lax.all_to_all(leaving, 'chan', split_axis=0, concat_axis=0, tiled=True)  9.51 us
    all_to_all x1, starting transfers between devices, shards(): lax.all_to_all(later, 'chan', split_axis=0, concat_axis=0, tiled=True)  5.99 us
  transfers between devices with their start and end apart: 14, of which 8 were waited for; matrix products, arithmetic and copies ran while one was open for 2% of the time, Pallas kernels for 35%

profile of v3, /device:TPU:1, one launch (start us, length us, event | category | flops | bytes accessed | tf_op | source)
XLA Modules:
  0.0 153.8 jit_solution(17026284499974068441)
XLA Ops:
  0.6 12.1 %channelize.1 = (bf16[128,2,16,256]{3,2,1,0:T(8,128)(2,1)}, bf16[128,2,16,256]{3,2,1,0:T(8,128)(2,1)}, bf16[256,2,16,256]{3,2,1,0:T(8,128)(2,1)}) custom-call(s32[128]{0:T(128)} %owner_ref.3, s32[1]{0:T(128)} %bitcast.inp_ref.here_ref, bf16[4096,512]{1,0:T(8,128)(2,1)} %bitcast.33, bf16[512,512]{1,0:T(8,128)(2,1)} %constant.17.clone.table_ref, ...), custom_call_target="tpu_custom_call" | custom-call | tf_op jit(solution)/shard_map/channelize/pallas_call | solution.py:147
  12.8 11.5 %all-to-all-start = ((bf16[128,2,16,256]{3,2,1,0:T(8,128)(2,1)}), bf16[128,2,16,256]{3,2,1,0:T(8,128)(2,1)S(1)}, u32[]{:S(2)}, u32[]{:S(2)}) async-start(bf16[128,2,16,256]{3,2,1,0:T(8,128)(2,1)} %get-tuple-element.39), calls=%async_computation | async-start | bytes 4194304 | tf_op jit(solution)/shard_map/all_to_all | solution.py:566
  24.3 4.0 %phases.1 = (f32[256,512]{1,0:T(8,128)}, f32[256,512]{1,0:T(8,128)}) custom-call(s32[1]{0:T(128)} %bitcast.inp_ref.here_ref, s32[256]{0:T(256)} %section_ref.1, f32[256,1024]{1,0:T(8,128)} %delay_ref.1), custom_call_target="tpu_custom_call" | custom-call | tf_op jit(solution)/shard_map/phases/pallas_call | solution.py:208
  28.3 13.2 %beamform_0.1 = (bf16[128,16,128]{2,1,0:T(8,128)(2,1)}, bf16[2,64,16,128]{3,2,1,0:T(8,128)(2,1)}, bf16[64,16,128]{2,1,0:T(8,128)(2,1)}, bf16[2,64,16,128]{3,2,1,0:T(8,128)(2,1)}, bf16[64,16,128]{2,1,0:T(8,128)(2,1)}) custom-call(bf16[256,32,256]{2,1,0:T(8,128)(2,1)} %bitcast.34, f32[256,512]{1,0:T(8,128)} %get-tuple-element.41.cos_ref, ...), custom_call_target="tpu_custom_call" | custom-call | flops 8589934592 | bytes 4194304 | tf_op jit(solution)/shard_map/beamform_0/pallas_call | solution.py:356
  41.5 1.5 collective-permute-start
  43.0 2.1 %collective-permute-start.1 = (bf16[2,64,16,128]{3,2,1,0:T(8,128)(2,1)}, bf16[2,64,16,128]{3,2,1,0:T(8,128)(2,1)S(1)}, u32[]{:S(2)}, u32[]{:S(2)}) collective-permute-start(bf16[2,64,16,128]{3,2,1,0:T(8,128)(2,1)} %get-tuple-element.47), channel_id=1, source_target_pairs={{0,96},{32,64},{64,32},{96,0},{1,97},{33,65},{65,33},{97,1},{2,98}... | collective-permute-start | bytes 1572872 | tf_op jit(solution)/shard_map/ppermute | solution.py:581
  45.0 13.6 %beamform_128.1 = (bf16[128,16,128]{2,1,0:T(8,128)(2,1)}, bf16[2,64,16,128]{3,2,1,0:T(8,128)(2,1)}, bf16[64,16,128]{2,1,0:T(8,128)(2,1)}, bf16[2,64,16,128]{3,2,1,0:T(8,128)(2,1)}, bf16[64,16,128]{2,1,0:T(8,128)(2,1)}) custom-call(bf16[256,32,256]{2,1,0:T(8,128)(2,1)} %bitcast.35, f32[256,512]{1,0:T(8,128)} %get-tuple-element.41.cos_ref, ...), custom_call_target="tpu_custom_call" | custom-call | flops 8589934592 | bytes 4194304 | tf_op jit(solution)/shard_map/beamform_128/pallas_call | solution.py:356
  58.6 2.8 %collective-permute-done.a_near = bf16[2,64,16,128]{3,2,1,0:T(8,128)(2,1)S(1)} collective-permute-done((bf16[2,64,16,128]{3,2,1,0:T(8,128)(2,1)}, bf16[2,64,16,128]{3,2,1,0:T(8,128)(2,1)S(1)}, u32[]{:S(2)}, u32[]{:S(2)}) %collective-permute-start) | collective-permute-done | bytes 524320 | tf_op jit(solution)/shard_map/ppermute | solution.py:581
  61.4 2.1 %collective-permute-done.1.b_near = bf16[2,64,16,128]{3,2,1,0:T(8,128)(2,1)S(1)} collective-permute-done((bf16[2,64,16,128]{3,2,1,0:T(8,128)(2,1)}, bf16[2,64,16,128]{3,2,1,0:T(8,128)(2,1)S(1)}, u32[]{:S(2)}, u32[]{:S(2)}) %collective-permute-start.1) | collective-permute-done | bytes 524320 | tf_op jit(solution)/shard_map/ppermute | solution.py:581
  63.4 0.0 all-to-all-done.refs_0_
  63.5 1.3 copy-done.1
  64.8 6.0 %all-to-all-start.1 = ((bf16[128,2,16,256]{3,2,1,0:T(8,128)(2,1)}), bf16[128,2,16,256]{3,2,1,0:T(8,128)(2,1)S(1)}, u32[]{:S(2)}, u32[]{:S(2)}) async-start(bf16[128,2,16,256]{3,2,1,0:T(8,128)(2,1)} %get-tuple-element.70), calls=%async_computation.1 | async-start | bytes 4194304 | tf_op jit(solution)/shard_map/all_to_all | solution.py:583
  70.8 0.1 collective-permute-start.2
  71.0 1.2 collective-permute-start.3
  72.1 1.0 fusion.2
  73.2 0.3 collective-permute-start.5
  73.5 1.0 fusion.3
  74.5 2.3 %collective-permute-start.4 = (bf16[64,16,128]{2,1,0:T(8,128)(2,1)S(1)}, bf16[64,16,128]{2,1,0:T(8,128)(2,1)S(1)}, u32[]{:S(2)}, u32[]{:S(2)}) collective-permute-start(bf16[64,16,128]{2,1,0:T(8,128)(2,1)S(1)} %fusion.3), channel_id=1, source_target_pairs={{0,96},{32,64},{64,32},{96,0},{1,97},{33,65},{65,33},{97,1},{2,98}... | collective-permute-start | bytes 786440 | tf_op jit(solution)/shard_map/ppermute | solution.py:593
  76.8 13.2 %collective-permute-done.5.b_far = bf16[64,16,128]{2,1,0:T(8,128)(2,1)S(1)} collective-permute-done((bf16[64,16,128]{2,1,0:T(8,128)(2,1)S(1)}, bf16[64,16,128]{2,1,0:T(8,128)(2,1)S(1)}, u32[]{:S(2)}, u32[]{:S(2)}) %collective-permute-start.5) | collective-permute-done | bytes 262176 | tf_op jit(solution)/shard_map/ppermute | solution.py:593
  90.0 1.0 collective-permute-done.4.a_far
  91.0 0.0 collective-permute-done.3.b_near
  91.1 0.0 copy-start.5
  91.1 0.1 fusion
  91.2 0.2 collective-permute-start.7
  91.4 0.1 fusion.1
  91.4 1.1 collective-permute-start.6
  92.5 2.6 %place_beams_0.1.rest_0_ = bf16[512,16,128]{2,1,0:T(8,128)(2,1)} custom-call(s32[256]{0:T(256)} %owner_ref.5, bf16[128,16,128]{2,1,0:T(8,128)(2,1)} %get-tuple-element.67.keep, bf16[2,64,16,128]{3,2,1,0:T(8,128)(2,1)} %copy-done.2, bf16[64,16,128]{2,1,0:T(8,128)(2,1)} %copy-done.12, bf16[2,64,16,128]{3,2,1,0:T(8,128)(2,1)} %copy-done.3, ...), custom_call_target="tpu_custom_call" | custom-call | tf_op jit(solution)/shard_map/place_beams_0/pallas_call | solution.py:434
  95.2 2.5 %collective-permute-done.7.b_far = bf16[64,16,128]{2,1,0:T(8,128)(2,1)S(1)} collective-permute-done((bf16[64,16,128]{2,1,0:T(8,128)(2,1)S(1)}, bf16[64,16,128]{2,1,0:T(8,128)(2,1)S(1)}, u32[]{:S(2)}, u32[]{:S(2)}) %collective-permute-start.7) | collective-permute-done | bytes 262176 | tf_op jit(solution)/shard_map/ppermute | solution.py:593
  97.7 1.2 collective-permute-done.6.a_far
  98.9 0.7 copy-done.14
  99.6 3.2 %place_beams_128.1 = bf16[512,16,128]{2,1,0:T(8,128)(2,1)} custom-call(s32[256]{0:T(256)} %owner_ref.5, bf16[128,16,128]{2,1,0:T(8,128)(2,1)} %get-tuple-element.56.keep, bf16[2,64,16,128]{3,2,1,0:T(8,128)(2,1)} %copy-done.4, bf16[64,16,128]{2,1,0:T(8,128)(2,1)} %copy-done.14, bf16[2,64,16,128]{3,2,1,0:T(8,128)(2,1)} %copy-done.5, ...), custom_call_target="tpu_custom_call", output_to_operand_aliasing={{}: (6, {})} | custom-call | tf_op jit(solution)/shard_map/place_beams_128/pallas_call | solution.py:434
  102.8 0.0 copy-start
  102.8 9.5 %all-to-all-start.2 = ((bf16[512,16,128]{2,1,0:T(8,128)(2,1)}), bf16[512,16,128]{2,1,0:T(8,128)(2,1)}, u32[]{:S(2)}, u32[]{:S(2)}) async-start(bf16[512,16,128]{2,1,0:T(8,128)(2,1)} %place_beams_128.1), calls=%async_computation.2 | async-start | bytes 4194304 | tf_op jit(solution)/shard_map/all_to_all | solution.py:600
  112.3 0.0 copy-start.16
  112.3 0.0 copy-start.15
  112.4 0.2 slice_bitcast_fusion
  112.5 1.1 collective-permute-start.10
  113.6 0.5 collective-permute-start.8
  114.1 1.0 collective-permute-start.9
  115.1 0.6 fusion.5
  115.7 0.6 fusion.4
  116.3 8.9 %gram_0.1.refs_4_ = f32[2,2,1024,1024]{3,2,1,0:T(8,128)} custom-call(s32[1]{0:T(128)} %bitcast.inp_ref.here_ref, s32[1]{0:T(128)} %bitcast.1.live_ref, bf16[128,2,16,256]{3,2,1,0:T(8,128)(2,1)} %copy-done.1), custom_call_target="tpu_custom_call" | custom-call | flops 4294967296 | bytes 12582912 | tf_op jit(solution)/shard_map/gram_0/pallas_call | solution.py:528
  125.3 0.7 collective-permute-done.10.refs_3_
  125.9 13.0 %collective-permute-done.8.refs_1_ = bf16[32,2,16,256]{3,2,1,0:T(8,128)(2,1)S(1)} collective-permute-done((bf16[32,2,16,256]{3,2,1,0:T(8,128)(2,1)S(1)}, bf16[32,2,16,256]{3,2,1,0:T(8,128)(2,1)S(1)}, u32[]{:S(2)}, u32[]{:S(2)}) %collective-permute-start.8) | collective-permute-done | bytes 524320 | tf_op jit(solution)/shard_map/ppermute | solution.py:609
  139.0 0.8 copy-done.7
  139.8 0.2 copy-done.8
  140.0 9.0 %gram_1.1 = f32[2,2,1024,1024]{3,2,1,0:T(8,128)} custom-call(s32[1]{0:T(128)} %bitcast.inp_ref.here_ref, s32[1]{0:T(128)} %bitcast.1.live_ref, bf16[32,4,1,2,16,256]{5,4,3,2,1,0:T(8,128)(2,1)} %bitcast.31, bf16[32,2,16,256]{3,2,1,0:T(8,128)(2,1)} %copy-done.7, bf16[32,2,16,256]{3,2,1,0:T(8,128)(2,1)} %copy-done.8, ...), custom_call_target="tpu_custom_call", output_to_operand_aliasing={{}: (6, {})} | custom-call | flops 4294967296 | bytes 12582912 | tf_op jit(solution)/shard_map/gram_1/pallas_call | solution.py:528
  148.9 4.9 %deliver_beams.1 = f32[16,512,128]{2,1,0:T(8,128)} custom-call(s32[1]{0:T(128)} %bitcast.14.live_ref, bf16[32,16,16,128]{3,2,1,0:T(8,128)(2,1)} %bitcast.15.x_ref), custom_call_target="tpu_custom_call" | custom-call | tf_op jit(solution)/shard_map/deliver_beams/pallas_call | solution.py:468
  (30 shorter events, 0.1 us)
Async XLA Ops:
  12.8 50.7 %all-to-all-start = ((bf16[128,2,16,256]{3,2,1,0:T(8,128)(2,1)}), bf16[128,2,16,256]{3,2,1,0:T(8,128)(2,1)S(1)}, u32[]{:S(2)}, u32[]{:S(2)}) async-start(bf16[128,2,16,256]{3,2,1,0:T(8,128)(2,1)} %get-tuple-element.39), calls=%async_computation | async-start | bytes 4194304 | tf_op jit(solution)/shard_map/all_to_all | solution.py:566
  41.5 19.9 %collective-permute-start = (bf16[2,64,16,128]{3,2,1,0:T(8,128)(2,1)}, bf16[2,64,16,128]{3,2,1,0:T(8,128)(2,1)S(1)}, u32[]{:S(2)}, u32[]{:S(2)}) collective-permute-start(bf16[2,64,16,128]{3,2,1,0:T(8,128)(2,1)} %get-tuple-element.45), channel_id=1, source_target_pairs={{0,32},{32,0},{64,96},{96,64},{1,33},{33,1},{65,97},{97,65},{2,34}... | collective-permute-start | bytes 1572872 | tf_op jit(solution)/shard_map/ppermute | solution.py:581
  43.0 20.5 %collective-permute-start.1 = (bf16[2,64,16,128]{3,2,1,0:T(8,128)(2,1)}, bf16[2,64,16,128]{3,2,1,0:T(8,128)(2,1)S(1)}, u32[]{:S(2)}, u32[]{:S(2)}) collective-permute-start(bf16[2,64,16,128]{3,2,1,0:T(8,128)(2,1)} %get-tuple-element.47), channel_id=1, source_target_pairs={{0,96},{32,64},{64,32},{96,0},{1,97},{33,65},{65,33},{97,1},{2,98}... | collective-permute-start | bytes 1572872 | tf_op jit(solution)/shard_map/ppermute | solution.py:581
  61.4 31.1 %copy-start.2 = (bf16[2,64,16,128]{3,2,1,0:T(8,128)(2,1)}, bf16[2,64,16,128]{3,2,1,0:T(8,128)(2,1)S(1)}, u32[]{:S(2)}) copy-start(bf16[2,64,16,128]{3,2,1,0:T(8,128)(2,1)S(1)} %collective-permute-done.a_near) | copy-start | bytes 1572868
  63.4 29.1 %copy-start.3 = (bf16[2,64,16,128]{3,2,1,0:T(8,128)(2,1)}, bf16[2,64,16,128]{3,2,1,0:T(8,128)(2,1)S(1)}, u32[]{:S(2)}) copy-start(bf16[2,64,16,128]{3,2,1,0:T(8,128)(2,1)S(1)} %collective-permute-done.1.b_near) | copy-start | bytes 1572868
  63.5 1.4 copy-start.1
  63.5 27.6 %copy-start.10 = (bf16[64,16,128]{2,1,0:T(8,128)(2,1)S(1)}, bf16[64,16,128]{2,1,0:T(8,128)(2,1)}, u32[]{:S(2)}) copy-start(bf16[64,16,128]{2,1,0:T(8,128)(2,1)} %get-tuple-element.66) | copy-start | bytes 786436
  64.8 38.0 %all-to-all-start.1 = ((bf16[128,2,16,256]{3,2,1,0:T(8,128)(2,1)}), bf16[128,2,16,256]{3,2,1,0:T(8,128)(2,1)S(1)}, u32[]{:S(2)}, u32[]{:S(2)}) async-start(bf16[128,2,16,256]{3,2,1,0:T(8,128)(2,1)} %get-tuple-element.70), calls=%async_computation.1 | async-start | bytes 4194304 | tf_op jit(solution)/shard_map/all_to_all | solution.py:583
  70.8 20.6 %copy-start.9 = (bf16[64,16,128]{2,1,0:T(8,128)(2,1)S(1)}, bf16[64,16,128]{2,1,0:T(8,128)(2,1)}, u32[]{:S(2)}) copy-start(bf16[64,16,128]{2,1,0:T(8,128)(2,1)} %get-tuple-element.64) | copy-start | bytes 786436
  70.8 20.2 %collective-permute-start.2 = (bf16[2,64,16,128]{3,2,1,0:T(8,128)(2,1)}, bf16[2,64,16,128]{3,2,1,0:T(8,128)(2,1)S(1)}, u32[]{:S(2)}, u32[]{:S(2)}) collective-permute-start(bf16[2,64,16,128]{3,2,1,0:T(8,128)(2,1)} %get-tuple-element.57), channel_id=1, source_target_pairs={{0,32},{32,0},{64,96},{96,64},{1,33},{33,1},{65,97},{97,65},{2,34}... | collective-permute-start | bytes 1572872 | tf_op jit(solution)/shard_map/ppermute | solution.py:585
  71.0 20.1 %collective-permute-start.3 = (bf16[2,64,16,128]{3,2,1,0:T(8,128)(2,1)}, bf16[2,64,16,128]{3,2,1,0:T(8,128)(2,1)S(1)}, u32[]{:S(2)}, u32[]{:S(2)}) collective-permute-start(bf16[2,64,16,128]{3,2,1,0:T(8,128)(2,1)} %get-tuple-element.58), channel_id=1, source_target_pairs={{0,96},{32,64},{64,32},{96,0},{1,97},{33,65},{65,33},{97,1},{2,98}... | collective-permute-start | bytes 1572872 | tf_op jit(solution)/shard_map/ppermute | solution.py:585
  73.2 16.8 %collective-permute-start.5 = (bf16[64,16,128]{2,1,0:T(8,128)(2,1)S(1)}, bf16[64,16,128]{2,1,0:T(8,128)(2,1)S(1)}, u32[]{:S(2)}, u32[]{:S(2)}) collective-permute-start(bf16[64,16,128]{2,1,0:T(8,128)(2,1)S(1)} %fusion.2), channel_id=1, source_target_pairs={{0,32},{32,0},{64,96},{96,64},{1,33},{33,1},{65,97},{97,65},{2,34}... | collective-permute-start | bytes 786440 | tf_op jit(solution)/shard_map/ppermute | solution.py:593
  74.5 16.5 %collective-permute-start.4 = (bf16[64,16,128]{2,1,0:T(8,128)(2,1)S(1)}, bf16[64,16,128]{2,1,0:T(8,128)(2,1)S(1)}, u32[]{:S(2)}, u32[]{:S(2)}) collective-permute-start(bf16[64,16,128]{2,1,0:T(8,128)(2,1)S(1)} %fusion.3), channel_id=1, source_target_pairs={{0,96},{32,64},{64,32},{96,0},{1,97},{33,65},{65,33},{97,1},{2,98}... | collective-permute-start | bytes 786440 | tf_op jit(solution)/shard_map/ppermute | solution.py:593
  90.0 2.5 %copy-start.11 = (bf16[64,16,128]{2,1,0:T(8,128)(2,1)}, bf16[64,16,128]{2,1,0:T(8,128)(2,1)S(1)}, u32[]{:S(2)}) copy-start(bf16[64,16,128]{2,1,0:T(8,128)(2,1)S(1)} %collective-permute-done.5.b_far) | copy-start | bytes 786436
  91.0 1.5 copy-start.12
  91.0 4.1 %copy-start.4 = (bf16[2,64,16,128]{3,2,1,0:T(8,128)(2,1)}, bf16[2,64,16,128]{3,2,1,0:T(8,128)(2,1)S(1)}, u32[]{:S(2)}) copy-start(bf16[2,64,16,128]{3,2,1,0:T(8,128)(2,1)S(1)} %collective-permute-done.2.a_near) | copy-start | bytes 1572868
  91.1 4.1 %copy-start.5 = (bf16[2,64,16,128]{3,2,1,0:T(8,128)(2,1)}, bf16[2,64,16,128]{3,2,1,0:T(8,128)(2,1)S(1)}, u32[]{:S(2)}) copy-start(bf16[2,64,16,128]{3,2,1,0:T(8,128)(2,1)S(1)} %collective-permute-done.3.b_near) | copy-start | bytes 1572868
  91.2 6.5 %collective-permute-start.7 = (bf16[64,16,128]{2,1,0:T(8,128)(2,1)S(1)}, bf16[64,16,128]{2,1,0:T(8,128)(2,1)S(1)}, u32[]{:S(2)}, u32[]{:S(2)}) collective-permute-start(bf16[64,16,128]{2,1,0:T(8,128)(2,1)S(1)} %fusion), channel_id=1, source_target_pairs={{0,32},{32,0},{64,96},{96,64},{1,33},{33,1},{65,97},{97,65},{2,34}... | collective-permute-start | bytes 786440 | tf_op jit(solution)/shard_map/ppermute | solution.py:593
  91.4 7.4 %collective-permute-start.6 = (bf16[64,16,128]{2,1,0:T(8,128)(2,1)S(1)}, bf16[64,16,128]{2,1,0:T(8,128)(2,1)S(1)}, u32[]{:S(2)}, u32[]{:S(2)}) collective-permute-start(bf16[64,16,128]{2,1,0:T(8,128)(2,1)S(1)} %fusion.1), channel_id=1, source_target_pairs={{0,96},{32,64},{64,32},{96,0},{1,97},{33,65},{65,33},{97,1},{2,98}... | collective-permute-start | bytes 786440 | tf_op jit(solution)/shard_map/ppermute | solution.py:593
  97.7 1.2 copy-start.13
  98.9 0.7 copy-start.14
  102.8 9.6 %copy-start = (bf16[128,2,16,256]{3,2,1,0:T(8,128)(2,1)}, bf16[128,2,16,256]{3,2,1,0:T(8,128)(2,1)S(1)}, u32[]{:S(2)}) copy-start(bf16[128,2,16,256]{3,2,1,0:T(8,128)(2,1)S(1)} %all-to-all-done.1) | copy-start | bytes 6291460
  102.8 46.1 %all-to-all-start.2 = ((bf16[512,16,128]{2,1,0:T(8,128)(2,1)}), bf16[512,16,128]{2,1,0:T(8,128)(2,1)}, u32[]{:S(2)}, u32[]{:S(2)}) async-start(bf16[512,16,128]{2,1,0:T(8,128)(2,1)} %place_beams_128.1), calls=%async_computation.2 | async-start | bytes 4194304 | tf_op jit(solution)/shard_map/all_to_all | solution.py:600
  112.3 2.7 %copy-start.16 = (s32[128]{0:T(128)S(1)}, s32[128]{0:T(128)}, u32[]{:S(2)}) copy-start(s32[128]{0:T(128)} %owner_ref.3) | copy-start | bytes 1540
  112.3 3.3 %copy-start.15 = (s32[256]{0:T(256)S(1)}, s32[256]{0:T(256)}, u32[]{:S(2)}) copy-start(s32[256]{0:T(256)} %owner_ref.5) | copy-start | bytes 3076
  112.5 13.4 %collective-permute-start.10 = (bf16[32,2,16,256]{3,2,1,0:T(8,128)(2,1)S(1)}, bf16[32,2,16,256]{3,2,1,0:T(8,128)(2,1)S(1)}, u32[]{:S(2)}, u32[]{:S(2)}) collective-permute-start(bf16[32,2,16,256]{3,2,1,0:T(8,128)(2,1)S(1)} %get-tuple-element.78), channel_id=1, source_target_pairs={{0,96},{32,0},{64,32},{96,64},{1,97},{33,1},{65,33},{97,65},{2,98}... | collective-permute-start | bytes 1572872 | tf_op jit(solution)/shard_map/ppermute | solution.py:609
  113.6 25.3 %collective-permute-start.8 = (bf16[32,2,16,256]{3,2,1,0:T(8,128)(2,1)S(1)}, bf16[32,2,16,256]{3,2,1,0:T(8,128)(2,1)S(1)}, u32[]{:S(2)}, u32[]{:S(2)}) collective-permute-start(bf16[32,2,16,256]{3,2,1,0:T(8,128)(2,1)S(1)} %get-tuple-element.80), channel_id=1, source_target_pairs={{0,32},{32,64},{64,96},{96,0},{1,33},{33,65},{65,97},{97,1},{2,34}... | collective-permute-start | bytes 1572872 | tf_op jit(solution)/shard_map/ppermute | solution.py:609
  114.1 24.9 %collective-permute-start.9 = (bf16[32,2,16,256]{3,2,1,0:T(8,128)(2,1)S(1)}, bf16[32,2,16,256]{3,2,1,0:T(8,128)(2,1)S(1)}, u32[]{:S(2)}, u32[]{:S(2)}) collective-permute-start(bf16[32,2,16,256]{3,2,1,0:T(8,128)(2,1)S(1)} %get-tuple-element.79), channel_id=1, source_target_pairs={{0,64},{32,96},{64,0},{96,32},{1,65},{33,97},{65,1},{97,33},{2,66}... | collective-permute-start | bytes 1572872 | tf_op jit(solution)/shard_map/ppermute | solution.py:609
  125.9 13.0 %copy-start.6 = (bf16[32,2,16,256]{3,2,1,0:T(8,128)(2,1)}, bf16[32,2,16,256]{3,2,1,0:T(8,128)(2,1)S(1)}, u32[]{:S(2)}) copy-start(bf16[32,2,16,256]{3,2,1,0:T(8,128)(2,1)S(1)} %collective-permute-done.10.refs_3_) | copy-start | bytes 1572868
  139.0 0.8 copy-start.7
  139.0 1.0 copy-start.8

commit v4 on v3

--- a/solution.py
+++ b/solution.py
@@ -52,7 +52,7 @@
 
 
 def channelize_body(
-    slots, groups, owner_ref, inp_ref, x_hbm, table_ref, perm_ref, gram_hbm, more_hbm, spec_hbm,
+    groups, owner_ref, inp_ref, x_hbm, table_ref, perm_ref, gram_hbm, more_hbm, spec_hbm,
     x_ref, xs, rows, spec, taken, in_sem, gram_sem, spec_sem,
 ):
     frames, inputs, width = xs.shape
@@ -97,14 +97,16 @@
 
         @pl.when(slot == 0)
         def _():
-            pltpu.make_async_copy(spec.at[k], gram_hbm.at[owner], gram_sem).start()
+            both = gram_hbm.at[owner, pl.ds(0, 2)]
+            pltpu.make_async_copy(spec.at[k], both, gram_sem).start()
 
         @pl.when(slot > 0)
         def _():
             chans = taken.shape[0] // groups
             ahead = lax.rem(lax.div(owner, chans) - inp_ref[0] + groups, groups)
-            at = (lax.rem(owner, chans) * groups + ahead) * (slots - 1) + slot - 1
-            pltpu.make_async_copy(spec.at[k], more_hbm.at[at], gram_sem).start()
+            at = lax.rem(owner, chans) * groups + ahead
+            pltpu.make_async_copy(spec.at[k, 0], gram_hbm.at[owner, 2], gram_sem).start()
+            pltpu.make_async_copy(spec.at[k, 1], more_hbm.at[at], gram_sem).start()
 
         return carry
 
@@ -128,27 +130,27 @@
                 rows[h, at, :] = out[:, h * 128 : h * 128 + 128]
             return carry
 
-        lax.fori_loop(0, frames, transform, 0, unroll=4)
+        lax.fori_loop(0, frames, transform, 0, unroll=16)
         for k in range(start, start + count, PIECE):
             lax.fori_loop(k, k + PIECE, high if start else low, 0, unroll=4)
             part = pl.ds(k, PIECE)
             saves.append(pltpu.make_async_copy(spec.at[part], spec_hbm.at[part], spec_sem.at[k // PIECE]))
             saves[-1].start()
     all_low = pl.ds(0, gram_channels)
-    pltpu.make_async_copy(spec.at[all_low], gram_hbm.at[all_low], gram_sem).wait()
+    pltpu.make_async_copy(spec.at[all_low], spec_hbm.at[all_low], gram_sem).wait()
     for save in saves:
         save.wait()
 
 
-def channelize(samples, gram_owner, inp_here, owner_count, groups, slots):
+def channelize(samples, gram_owner, inp_here, owner_count, groups):
     inputs, frames, width = samples.shape
     channels = width // 2
     anywhere = pl.BlockSpec(memory_space=pl.ANY)
     return pl.pallas_call(
-        functools.partial(channelize_body, slots, groups),
+        functools.partial(channelize_body, groups),
         out_shape=(
-            jax.ShapeDtypeStruct((owner_count, 2, frames, inputs), BF16),
-            jax.ShapeDtypeStruct((owner_count * (slots - 1), 2, frames, inputs), BF16),
+            jax.ShapeDtypeStruct((owner_count, 3, frames, inputs), BF16),
+            jax.ShapeDtypeStruct((owner_count, frames, inputs), BF16),
             jax.ShapeDtypeStruct((channels, 2, frames, inputs), BF16),
         ),
         in_specs=[smem(), smem(), anywhere, vmem(), vmem()],
@@ -224,6 +226,7 @@
 
 
 STEP = 16
+PAIR = 2 * STEP
 CHANNEL_CHUNKS = ((0, 128), (128, 128))
 
 
@@ -292,7 +295,7 @@
     sign = jnp.where(lane < half, -1.0, 1.0).astype(F32)
 
     def form(m, weights):
-        got = jnp.dot(spec_ref[m], weights[m], preferred_element_type=F32)
+        got = jnp.dot(spec_ref[m], weights[m % STEP], preferred_element_type=F32)
         parts = []
         for t in range(tiles):
             real = got[:frames, t * 128 : t * 128 + 128]
@@ -308,25 +311,25 @@
         def _(r):
             make(r, even)
 
-    @pl.when((step > 0) & (step < last) & (step % 2 == 1))
+    @pl.when(step > 0)
     def _():
         @pl.loop(0, STEP, unroll=True)
         def _(r):
             form(r, even)
             make(r, odd)
 
-    @pl.when((step > 0) & (step < last) & (step % 2 == 0))
+    @pl.when((step > 0) & (step < last))
     def _():
         @pl.loop(0, STEP, unroll=True)
         def _(r):
-            form(r, odd)
+            form(STEP + r, odd)
             make(r, even)
 
     @pl.when(step == last)
     def _():
         @pl.loop(0, STEP, unroll=True)
         def _(r):
-            form(r, odd)
+            form(STEP + r, odd)
 
     middle = last // 2
 
@@ -344,7 +347,7 @@
     lanes = cosines.shape[1]
     part = count // 2
     tile = (frames, 128)
-    steps = count // STEP
+    steps = count // PAIR
     assert steps % 2 == 0 and inputs // 16 == STEP
     spectra = spectra.reshape(channels, 2 * frames, inputs)
     state = pltpu.VMEM((inputs, lanes), F32)
@@ -364,22 +367,22 @@
             jax.ShapeDtypeStruct((part, *tile), BF16),
         ),
         in_specs=[
-            pl.BlockSpec((STEP, 2 * frames, inputs), lambda j: (first // STEP + at(j), 0, 0)),
+            pl.BlockSpec((PAIR, 2 * frames, inputs), lambda j: (first // PAIR + at(j), 0, 0)),
             whole(inputs, lanes),
             whole(inputs, lanes),
         ],
         out_specs=(
-            pl.BlockSpec((STEP, *tile), lambda j: (at(j), 0, 0)),
-            pl.BlockSpec((2, STEP, *tile), lambda j: (0, low(j), 0, 0)),
-            pl.BlockSpec((STEP, *tile), lambda j: (low(j), 0, 0)),
-            pl.BlockSpec((2, STEP, *tile), lambda j: (0, high(j), 0, 0)),
-            pl.BlockSpec((STEP, *tile), lambda j: (high(j), 0, 0)),
+            pl.BlockSpec((PAIR, *tile), lambda j: (at(j), 0, 0)),
+            pl.BlockSpec((2, PAIR, *tile), lambda j: (0, low(j), 0, 0)),
+            pl.BlockSpec((PAIR, *tile), lambda j: (low(j), 0, 0)),
+            pl.BlockSpec((2, PAIR, *tile), lambda j: (0, high(j), 0, 0)),
+            pl.BlockSpec((PAIR, *tile), lambda j: (high(j), 0, 0)),
         ),
         scratch_shapes=[
             state, state, state, state,
             pltpu.VMEM((STEP, inputs, lanes), BF16),
             pltpu.VMEM((STEP, inputs, lanes), BF16),
-            pltpu.VMEM((lanes // 128 - 1, STEP, *tile), BF16),
+            pltpu.VMEM((lanes // 128 - 1, PAIR, *tile), BF16),
         ],
         compiler_params=params(dimension_semantics=("arbitrary",)),
         cost_estimate=pl.CostEstimate(
@@ -479,30 +482,34 @@
     )(live, arrived.reshape(sources, slots, frames, lanes))
 
 
-def gram_body(scale, slot, blocks, here_ref, live_ref, *refs):
-    ins, o_ref, xs = refs[:blocks], refs[-2], refs[-1]
+def gram_body(scale, slot, here_ref, live_ref, direct_ref, *refs):
+    others, o_ref, xs = refs[:4], refs[-2], refs[-1]
     row = pl.program_id(0)
     groups, _, depth, inputs = xs.shape
     over = (((0,), (0,)), ((), ()))
 
+    def block(d):
+        return lax.rem(here_ref[0] - d + groups, groups) if slot else d
+
     @pl.when(live_ref[0] > slot)
     def _():
         @pl.when(row == 0)
         def _():
-            for n, ref in enumerate(ins):
-                parts = groups // blocks
-                value = ref[...].reshape(parts, -1, 2, *ref.shape[-2:])
-                for d in range(parts):
-                    for p in range(2):
-                        xs[n * parts + d, p] = value[d, :, p].reshape(depth, inputs)
+            each = direct_ref.shape[0] // groups
+            for d in range(groups):
+                mine = pl.ds(block(d) * each, each)
+                xs[d, 0] = direct_ref[mine, 0].reshape(depth, inputs)
+                if slot:
+                    xs[d, 1] = others[d][...].reshape(depth, inputs)
+                else:
+                    xs[d, 1] = direct_ref[mine, 1].reshape(depth, inputs)
 
         r_a, m_a = xs[row, 0], xs[row, 1]
         left_re = jnp.concatenate([r_a, m_a], axis=0)
         left_im = jnp.concatenate([m_a, -r_a], axis=0)
         for d in range(groups):
             right = xs[d].reshape(2 * depth, inputs)
-            block = lax.rem(here_ref[0] - d + groups, groups) if blocks > 1 else d
-            cols = pl.ds(pl.multiple_of(block * inputs, inputs), inputs)
+            cols = pl.ds(pl.multiple_of(block(d) * inputs, inputs), inputs)
             re = lax.dot_general(left_re, right, over, preferred_element_type=F32)
             im = lax.dot_general(left_im, right, over, preferred_element_type=F32)
             o_ref[0, 0, :, cols] = re * scale
@@ -513,33 +520,32 @@
         o_ref[...] = jnp.zeros_like(o_ref)
 
 
-def gram(here, live, arrays, groups, slot, slots, before):
-    frames, inputs = arrays[-1].shape[-2:]
+def gram(here, live, direct, later, moved, groups, slot, slots, before):
+    sources, _, frames, inputs = direct.shape
+    chans = sources // groups
     total = groups * inputs
-    blocks = len(arrays)
-    depth = arrays[-1].shape[0] * frames * blocks // groups
-    back = lambda a, here: lax.rem(here[0] - a + groups, groups) if blocks > 1 else a
-    whole = lambda x: pl.BlockSpec(x.shape, lambda a, *_: (0,) * x.ndim)
-    first = [whole(arrays[0])]
-    if blocks > 1:
-        chans, _, _, *rest = arrays[0].shape
-        first = [pl.BlockSpec((chans, 1, 1, *rest), lambda a, *_: (0, 0, slot - 1, 0, 0, 0))]
+    depth = chans * frames
+    back = lambda a, here: lax.rem(here[0] - a + groups, groups) if slot else a
+    specs = [pl.BlockSpec((sources, 2 - slot, frames, inputs), lambda a, *_: (0, 2 * slot, 0, 0))]
+    arrays = [direct]
+    if slot:
+        specs.append(pl.BlockSpec((chans, 1, frames, inputs), lambda a, *_: (0, 0, 0, 0)))
+        arrays += [later, *moved]
+        specs += [pl.BlockSpec(x.shape, lambda a, *_: (0, 0, 0)) for x in moved]
     more = [] if before is None else [before]
     return pl.pallas_call(
-        functools.partial(gram_body, 1.0 / depth, slot, blocks),
+        functools.partial(gram_body, 1.0 / depth, slot),
         grid_spec=pltpu.PrefetchScalarGridSpec(
             num_scalar_prefetch=2,
             grid=(groups,),
-            in_specs=first
-            + [whole(x) for x in arrays[1:]]
-            + [pl.BlockSpec(memory_space=pl.ANY)] * len(more),
+            in_specs=specs + [pl.BlockSpec(memory_space=pl.ANY)] * len(more),
             out_specs=pl.BlockSpec(
                 (1, 2, inputs, total), lambda a, here, live: (slot, 0, back(a, here), 0)
             ),
             scratch_shapes=[pltpu.VMEM((groups, 2, depth, inputs), BF16)],
         ),
         out_shape=jax.ShapeDtypeStruct((slots, 2, total, total), F32),
-        input_output_aliases={2 + blocks: 0} if more else {},
+        input_output_aliases={2 + len(arrays): 0} if more else {},
         compiler_params=params(dimension_semantics=("arbitrary",)),
         cost_estimate=pl.CostEstimate(
             flops=8 * total * total * depth, bytes_accessed=12 * total * total, transcendentals=0
@@ -561,7 +567,7 @@
     section_width = delays.shape[0] // inp_count
 
     outgoing, later, spectra = channelize(
-        samples, gram_owner, inp_here, owner_count, inp_count, gram_slots
+        samples, gram_owner, inp_here, owner_count, inp_count
     )
     arrived = lax.all_to_all(outgoing, ("inp", "chan"), split_axis=0, concat_axis=0, tiled=True)
 
@@ -581,7 +587,7 @@
             near.append((lax.ppermute(a, "inp", side), lax.ppermute(b, "inp", back)))
     later, arrived, parts, near = lax.optimization_barrier((later, arrived, parts, near))
     later = lax.all_to_all(later, "chan", split_axis=0, concat_axis=0, tiled=True)
-    later = later.reshape(chan_count, inp_count, gram_slots - 1, *later.shape[1:])
+    later = later.reshape(chan_count, inp_count, *later.shape[1:])
     near.append((lax.ppermute(parts[-1][1], "inp", side), lax.ppermute(parts[-1][3], "inp", back)))
     far = []
     for n, (_, _, a2, _, b2) in enumerate(parts):
@@ -603,14 +609,14 @@
     gram_live = jnp.sum((gram_owner == here).astype(jnp.int32)).reshape(1)
     beam_live = jnp.sum((beam_owner == chan_here).astype(jnp.int32)).reshape(1)
     at = inp_here.reshape(1)
-    visibilities = gram(at, gram_live, [arrived], inp_count, 0, gram_slots, None)
-    for slot in range(1, gram_slots):
-        moved = [
-            lax.ppermute(later[:, d, slot - 1], "inp", [(z, (z + d) % inp_count) for z in range(inp_count)])
-            for d in range(1, inp_count)
-        ]
+    moved = [
+        lax.ppermute(later[:, d], "inp", [(z, (z + d) % inp_count) for z in range(inp_count)])
+        for d in range(1, inp_count)
+    ]
+    visibilities = None
+    for slot in range(gram_slots):
         visibilities = gram(
-            at, gram_live, [later, *moved], inp_count, slot, gram_slots, visibilities
+            at, gram_live, arrived, later, moved, inp_count, slot, gram_slots, visibilities
         )
     formed = deliver(beam_live, beams_in, chan_count, beam_slots)
     return (visibilities, formed[:, None])

time: 155 us -> 154 us (level)
  Pallas kernels: 71.5 us -> 63.3 us
  other arithmetic: 3.45 us -> 6.44 us
  local copies, waits for them, and re-layouts: 3.26 us -> 5.45 us
    ppermute x2, waiting for transfers between devices: 4.85 us -> 15.3 us  [shards(): near.append((lax.ppermute(a, 'inp', side), lax.ppermute(b, 'inp', back)))]
    ppermute x2, waiting for transfers between devices: 15.7 us -> 6.65 us  [shards(): lax.ppermute(b_sum, 'inp', side)]
    pallas_call x3, Pallas kernels: 30 us -> 22.4 us  [the longest x2 11.6 us: gram(): pl.pallas_call(functools.partial(gram_body, 1.0 / depth, slot), grid_spec...]
    ppermute x3, waiting for transfers between devices: 13.7 us -> 6.92 us  [shards(): lax.ppermute(later[:, d], 'inp', [(z, (z + d) % inp_count) for z in range...]
    all_to_all x1, waiting for transfers between devices: 0.01 us -> 2.83 us  [shards(): lax.all_to_all(leaving, 'chan', split_axis=0, concat_axis=0, tiled=True)]
    ppermute x2, waiting for transfers between devices: 2.2 us -> 4.65 us  [shards(): lax.ppermute(a_sum, 'inp', back)]
    convert_element_type x2, other arithmetic: 1.09 us -> 3 us  [shards(): b_sum = (b2.astype(F32) + b_in[1].astype(F32)).astype(BF16)]
    unnamed x34 -> x24, local copies, waits for them, and re-layouts: 3.1 us -> 4.29 us
  transfers between devices with their start and end apart: 14 -> 14, of which waited for: 8 -> 8; matrix products, arithmetic and copies ran while one was open for 2% -> 5% of each run, Pallas kernels for 35% -> 31%
where the time goes in v4:
time: 154 us; the launch traced here: 152 us
  Pallas kernels  63.3 us (41%)
  starting transfers between devices  39.4 us (26%)
  waiting for transfers between devices  36.4 us (24%)
  other arithmetic  6.44 us (4%)
  local copies, waits for them, and re-layouts  5.45 us (4%)
    pallas_call x2, Pallas kernels, beamform(): pl.pallas_call(functools.partial(beam_body, first, 64), grid=(steps + 1,)...  26.2 us
    ppermute x2, waiting for transfers between devices, shards(): near.append((lax.ppermute(a, 'inp', side), lax.ppermute(b, 'inp', back)))  15.3 us
    pallas_call x2, Pallas kernels, gram(): pl.pallas_call(functools.partial(gram_body, 1.0 / depth, slot), grid_spec...  11.6 us
    all_to_all x1, starting transfers between devices, shards(): lax.all_to_all(outgoing, ('inp', 'chan'), split_axis=0, concat_axis=0, ti...  11.5 us
    pallas_call x1, Pallas kernels, channelize(): pl.pallas_call(functools.partial(channelize_body, groups), out_shape=(jax...  10.7 us
    all_to_all x1, starting transfers between devices, shards(): lax.all_to_all(leaving, 'chan', split_axis=0, concat_axis=0, tiled=True)  9.21 us
    all_to_all x1, starting transfers between devices, shards(): lax.all_to_all(later, 'chan', split_axis=0, concat_axis=0, tiled=True)  7.26 us
    ppermute x3, waiting for transfers between devices, shards(): lax.ppermute(later[:, d], 'inp', [(z, (z + d) % inp_count) for z in range...  6.92 us
  transfers between devices with their start and end apart: 14, of which 8 were waited for; matrix products, arithmetic and copies ran while one was open for 5% of the time, Pallas kernels for 31%

profile of v4, /device:TPU:1, one launch (start us, length us, event | category | flops | bytes accessed | tf_op | source)
XLA Modules:
  0.0 151.8 jit_solution(17089377708222103797)
XLA Ops:
  0.6 10.7 %channelize.1 = (bf16[128,3,16,256]{3,2,1,0:T(8,128)(2,1)}, bf16[128,16,256]{2,1,0:T(8,128)(2,1)}, bf16[256,2,16,256]{3,2,1,0:T(8,128)(2,1)}) custom-call(s32[128]{0:T(128)} %owner_ref.3, s32[1]{0:T(128)} %bitcast.inp_ref.here_ref, bf16[4096,512]{1,0:T(8,128)(2,1)} %bitcast.31, bf16[512,512]{1,0:T(8,128)(2,1)} %constant.17.clone.table_ref, ...), custom_call_target="tpu_custom_call" | custom-call | tf_op jit(solution)/shard_map/channelize/pallas_call | solution.py:149
  11.4 11.5 %all-to-all-start = ((bf16[128,3,16,256]{3,2,1,0:T(8,128)(2,1)}), bf16[128,3,16,256]{3,2,1,0:T(8,128)(2,1)S(1)}, u32[]{:S(2)}, u32[]{:S(2)}) async-start(bf16[128,3,16,256]{3,2,1,0:T(8,128)(2,1)} %get-tuple-element.39), calls=%async_computation | async-start | bytes 6291456 | tf_op jit(solution)/shard_map/all_to_all | solution.py:572
  22.9 4.0 %phases.1 = (f32[256,512]{1,0:T(8,128)}, f32[256,512]{1,0:T(8,128)}) custom-call(s32[1]{0:T(128)} %bitcast.inp_ref.here_ref, s32[256]{0:T(256)} %section_ref.1, f32[256,1024]{1,0:T(8,128)} %delay_ref.1), custom_call_target="tpu_custom_call" | custom-call | tf_op jit(solution)/shard_map/phases/pallas_call | solution.py:210
  26.9 12.9 %beamform_0.1 = (bf16[128,16,128]{2,1,0:T(8,128)(2,1)}, bf16[2,64,16,128]{3,2,1,0:T(8,128)(2,1)}, bf16[64,16,128]{2,1,0:T(8,128)(2,1)}, bf16[2,64,16,128]{3,2,1,0:T(8,128)(2,1)}, bf16[64,16,128]{2,1,0:T(8,128)(2,1)}) custom-call(bf16[256,32,256]{2,1,0:T(8,128)(2,1)} %bitcast.32, f32[256,512]{1,0:T(8,128)} %get-tuple-element.41.cos_ref, ...), custom_call_target="tpu_custom_call" | custom-call | flops 8589934592 | bytes 4194304 | tf_op jit(solution)/shard_map/beamform_0/pallas_call | solution.py:359
  39.8 1.5 collective-permute-start
  41.3 2.1 %collective-permute-start.1 = (bf16[2,64,16,128]{3,2,1,0:T(8,128)(2,1)}, bf16[2,64,16,128]{3,2,1,0:T(8,128)(2,1)}, u32[]{:S(2)}, u32[]{:S(2)}) collective-permute-start(bf16[2,64,16,128]{3,2,1,0:T(8,128)(2,1)} %get-tuple-element.47), channel_id=1, source_target_pairs={{0,96},{32,64},{64,32},{96,0},{1,97},{33,65},{65,33},{97,1},{2,98}... | collective-permute-start | bytes 1572872 | tf_op jit(solution)/shard_map/ppermute | solution.py:587
  43.3 13.3 %beamform_128.1 = (bf16[128,16,128]{2,1,0:T(8,128)(2,1)}, bf16[2,64,16,128]{3,2,1,0:T(8,128)(2,1)}, bf16[64,16,128]{2,1,0:T(8,128)(2,1)}, bf16[2,64,16,128]{3,2,1,0:T(8,128)(2,1)}, bf16[64,16,128]{2,1,0:T(8,128)(2,1)}) custom-call(bf16[256,32,256]{2,1,0:T(8,128)(2,1)} %bitcast.33, f32[256,512]{1,0:T(8,128)} %get-tuple-element.41.cos_ref, ...), custom_call_target="tpu_custom_call" | custom-call | flops 8589934592 | bytes 4194304 | tf_op jit(solution)/shard_map/beamform_128/pallas_call | solution.py:359
  56.7 13.8 %collective-permute-done.a_near = bf16[2,64,16,128]{3,2,1,0:T(8,128)(2,1)S(1)} collective-permute-done((bf16[2,64,16,128]{3,2,1,0:T(8,128)(2,1)}, bf16[2,64,16,128]{3,2,1,0:T(8,128)(2,1)S(1)}, u32[]{:S(2)}, u32[]{:S(2)}) %collective-permute-start) | collective-permute-done | bytes 524320 | tf_op jit(solution)/shard_map/ppermute | solution.py:587
  70.5 0.8 copy-done.2
  71.3 1.5 collective-permute-done.1.b_near
  72.8 0.0 all-to-all-done.direct_ref
  72.8 0.0 collective-permute-start.2
  72.8 1.7 %collective-permute-start.3 = (bf16[2,64,16,128]{3,2,1,0:T(8,128)(2,1)}, bf16[2,64,16,128]{3,2,1,0:T(8,128)(2,1)}, u32[]{:S(2)}, u32[]{:S(2)}) collective-permute-start(bf16[2,64,16,128]{3,2,1,0:T(8,128)(2,1)} %get-tuple-element.59), channel_id=1, source_target_pairs={{0,96},{32,64},{64,32},{96,0},{1,97},{33,65},{65,33},{97,1},{2,98}... | collective-permute-start | bytes 1572872 | tf_op jit(solution)/shard_map/ppermute | solution.py:591
  74.5 1.8 %fusion.2 = bf16[64,16,128]{2,1,0:T(8,128)(2,1)} fusion(bf16[64,16,128]{2,1,0:T(8,128)(2,1)} %get-tuple-element.62, bf16[2,64,16,128]{3,2,1,0:T(8,128)(2,1)} %collective-permute-done.1.b_near), kind=kLoop, calls=%fused_computation.5 | loop fusion | flops 524288 | bytes 786432 | tf_op jit(solution)/shard_map/convert_element_type | solution.py:598
  76.3 0.3 collective-permute-start.5
  76.6 7.3 %all-to-all-start.1 = ((bf16[128,16,256]{2,1,0:T(8,128)(2,1)}), bf16[128,16,256]{2,1,0:T(8,128)(2,1)}, u32[]{:S(2)}, u32[]{:S(2)}) async-start(bf16[128,16,256]{2,1,0:T(8,128)(2,1)} %get-tuple-element.71), calls=%async_computation.1 | async-start | bytes 2097152 | tf_op jit(solution)/shard_map/all_to_all | solution.py:589
  83.8 1.1 fusion.3
  85.0 1.7 %collective-permute-start.4 = (bf16[64,16,128]{2,1,0:T(8,128)(2,1)S(1)}, bf16[64,16,128]{2,1,0:T(8,128)(2,1)S(1)}, u32[]{:S(2)}, u32[]{:S(2)}) collective-permute-start(bf16[64,16,128]{2,1,0:T(8,128)(2,1)S(1)} %fusion.3), channel_id=1, source_target_pairs={{0,96},{32,64},{64,32},{96,0},{1,97},{33,65},{65,33},{97,1},{2,98}... | collective-permute-start | bytes 786440 | tf_op jit(solution)/shard_map/ppermute | solution.py:599
  86.6 5.2 %collective-permute-done.5.b_far = bf16[64,16,128]{2,1,0:T(8,128)(2,1)} collective-permute-done((bf16[64,16,128]{2,1,0:T(8,128)(2,1)}, bf16[64,16,128]{2,1,0:T(8,128)(2,1)}, u32[]{:S(2)}, u32[]{:S(2)}) %collective-permute-start.5) | collective-permute-done | bytes 262176 | tf_op jit(solution)/shard_map/ppermute | solution.py:599
  91.8 2.1 %collective-permute-done.4.a_far = bf16[64,16,128]{2,1,0:T(8,128)(2,1)S(1)} collective-permute-done((bf16[64,16,128]{2,1,0:T(8,128)(2,1)S(1)}, bf16[64,16,128]{2,1,0:T(8,128)(2,1)S(1)}, u32[]{:S(2)}, u32[]{:S(2)}) %collective-permute-start.4) | collective-permute-done | bytes 262176 | tf_op jit(solution)/shard_map/ppermute | solution.py:599
  93.9 0.0 collective-permute-done.2.a_near
  93.9 1.2 fusion
  95.1 0.6 collective-permute-start.7
  95.8 1.0 fusion.1
  96.8 1.1 collective-permute-start.6
  97.9 2.6 %place_beams_0.1.rest_0_ = bf16[512,16,128]{2,1,0:T(8,128)(2,1)} custom-call(s32[256]{0:T(256)} %owner_ref.5, bf16[128,16,128]{2,1,0:T(8,128)(2,1)} %get-tuple-element.68.keep, bf16[2,64,16,128]{3,2,1,0:T(8,128)(2,1)} %copy-done.2, bf16[64,16,128]{2,1,0:T(8,128)(2,1)} %copy-done.7, bf16[2,64,16,128]{3,2,1,0:T(8,128)(2,1)} %collective-permute-done.1.b_near, ...), custom_call_target="tpu_custom_call" | custom-call | tf_op jit(solution)/shard_map/place_beams_0/pallas_call | solution.py:437
  100.6 0.0 copy-start.11
  100.6 0.0 copy-start.10
  100.6 1.4 collective-permute-done.7.b_far
  102.0 2.6 %collective-permute-done.6.a_far = bf16[64,16,128]{2,1,0:T(8,128)(2,1)S(1)} collective-permute-done((bf16[64,16,128]{2,1,0:T(8,128)(2,1)S(1)}, bf16[64,16,128]{2,1,0:T(8,128)(2,1)S(1)}, u32[]{:S(2)}, u32[]{:S(2)}) %collective-permute-start.6) | collective-permute-done | bytes 262176 | tf_op jit(solution)/shard_map/ppermute | solution.py:599
  104.6 0.7 copy-done.9
  105.3 3.2 %place_beams_128.1 = bf16[512,16,128]{2,1,0:T(8,128)(2,1)} custom-call(s32[256]{0:T(256)} %owner_ref.5, bf16[128,16,128]{2,1,0:T(8,128)(2,1)} %get-tuple-element.57.keep, bf16[2,64,16,128]{3,2,1,0:T(8,128)(2,1)} %collective-permute-done.2.a_near, bf16[64,16,128]{2,1,0:T(8,128)(2,1)} %copy-done.9, ...), custom_call_target="tpu_custom_call", output_to_operand_aliasing={{}: (6, {})} | custom-call | tf_op jit(solution)/shard_map/place_beams_128/pallas_call | solution.py:437
  108.5 0.0 all-to-all-done.1
  108.5 9.2 %all-to-all-start.2 = ((bf16[512,16,128]{2,1,0:T(8,128)(2,1)}), bf16[512,16,128]{2,1,0:T(8,128)(2,1)S(1)}, u32[]{:S(2)}, u32[]{:S(2)}) async-start(bf16[512,16,128]{2,1,0:T(8,128)(2,1)} %place_beams_128.1), calls=%async_computation.2 | async-start | bytes 4194304 | tf_op jit(solution)/shard_map/all_to_all | solution.py:606
  117.7 0.7 fusion.5
  118.4 0.7 fusion.4
  119.0 1.2 slice_bitcast_fusion
  120.2 1.1 collective-permute-start.10
  121.4 0.4 collective-permute-start.8
  121.8 1.0 collective-permute-start.9
  122.8 5.8 %gram_0.1.refs_4_ = f32[2,2,1024,1024]{3,2,1,0:T(8,128)} custom-call(s32[1]{0:T(128)} %bitcast.inp_ref.here_ref, s32[1]{0:T(128)} %bitcast.1.live_ref, bf16[128,3,16,256]{3,2,1,0:T(8,128)(2,1)} %copy-done), custom_call_target="tpu_custom_call" | custom-call | flops 4294967296 | bytes 12582912 | tf_op jit(solution)/shard_map/gram_0/pallas_call | solution.py:536
  128.6 6.9 %collective-permute-done.8.refs_1_ = bf16[32,16,256]{2,1,0:T(8,128)(2,1)S(1)} collective-permute-done((bf16[32,16,256]{2,1,0:T(8,128)(2,1)S(1)}, bf16[32,16,256]{2,1,0:T(8,128)(2,1)S(1)}, u32[]{:S(2)}, u32[]{:S(2)}) %collective-permute-start.8) | collective-permute-done | bytes 262176 | tf_op jit(solution)/shard_map/ppermute | solution.py:613
  135.5 0.7 copy-done.4
  136.2 0.7 copy-done.5
  137.0 5.8 %gram_1.1 = f32[2,2,1024,1024]{3,2,1,0:T(8,128)} custom-call(s32[1]{0:T(128)} %bitcast.inp_ref.here_ref, s32[1]{0:T(128)} %bitcast.1.live_ref, bf16[128,3,16,256]{3,2,1,0:T(8,128)(2,1)} %copy-done, bf16[32,4,16,256]{3,2,1,0:T(8,128)(2,1)} %bitcast.9.refs_0_, bf16[32,16,256]{2,1,0:T(8,128)(2,1)} %copy-done.4, ...), custom_call_target="tpu_custom_call", output_to_operand_aliasing={{}: (7, {})} | custom-call | flops 4294967296 | bytes 12582912 | tf_op jit(solution)/shard_map/gram_1/pallas_call | solution.py:536
  142.7 2.8 %all-to-all-done.2 = bf16[512,16,128]{2,1,0:T(8,128)(2,1)S(1)} async-done(((bf16[512,16,128]{2,1,0:T(8,128)(2,1)}), bf16[512,16,128]{2,1,0:T(8,128)(2,1)S(1)}, u32[]{:S(2)}, u32[]{:S(2)}) %all-to-all-start.2) | async-done | bytes 2097184 | tf_op jit(solution)/shard_map/all_to_all | solution.py:606
  145.6 1.4 copy-done.1
  146.9 4.9 %deliver_beams.1 = f32[16,512,128]{2,1,0:T(8,128)} custom-call(s32[1]{0:T(128)} %bitcast.13.live_ref, bf16[32,16,16,128]{3,2,1,0:T(8,128)(2,1)} %bitcast.29), custom_call_target="tpu_custom_call" | custom-call | tf_op jit(solution)/shard_map/deliver_beams/pallas_call | solution.py:471
  (20 shorter events, 0.0 us)
Async XLA Ops:
  11.4 61.4 %all-to-all-start = ((bf16[128,3,16,256]{3,2,1,0:T(8,128)(2,1)}), bf16[128,3,16,256]{3,2,1,0:T(8,128)(2,1)S(1)}, u32[]{:S(2)}, u32[]{:S(2)}) async-start(bf16[128,3,16,256]{3,2,1,0:T(8,128)(2,1)} %get-tuple-element.39), calls=%async_computation | async-start | bytes 6291456 | tf_op jit(solution)/shard_map/all_to_all | solution.py:572
  39.8 30.7 %collective-permute-start = (bf16[2,64,16,128]{3,2,1,0:T(8,128)(2,1)}, bf16[2,64,16,128]{3,2,1,0:T(8,128)(2,1)S(1)}, u32[]{:S(2)}, u32[]{:S(2)}) collective-permute-start(bf16[2,64,16,128]{3,2,1,0:T(8,128)(2,1)} %get-tuple-element.45), channel_id=1, source_target_pairs={{0,32},{32,0},{64,96},{96,64},{1,33},{33,1},{65,97},{97,65},{2,34}... | collective-permute-start | bytes 1572872 | tf_op jit(solution)/shard_map/ppermute | solution.py:587
  41.3 31.5 %collective-permute-start.1 = (bf16[2,64,16,128]{3,2,1,0:T(8,128)(2,1)}, bf16[2,64,16,128]{3,2,1,0:T(8,128)(2,1)}, u32[]{:S(2)}, u32[]{:S(2)}) collective-permute-start(bf16[2,64,16,128]{3,2,1,0:T(8,128)(2,1)} %get-tuple-element.47), channel_id=1, source_target_pairs={{0,96},{32,64},{64,32},{96,0},{1,97},{33,65},{65,33},{97,1},{2,98}... | collective-permute-start | bytes 1572872 | tf_op jit(solution)/shard_map/ppermute | solution.py:587
  56.7 39.1 %copy-start.6 = (bf16[64,16,128]{2,1,0:T(8,128)(2,1)S(1)}, bf16[64,16,128]{2,1,0:T(8,128)(2,1)}, u32[]{:S(2)}) copy-start(bf16[64,16,128]{2,1,0:T(8,128)(2,1)} %get-tuple-element.65) | copy-start | bytes 786436
  70.5 0.8 copy-start.2
  72.8 27.7 %copy-start = (bf16[128,3,16,256]{3,2,1,0:T(8,128)(2,1)}, bf16[128,3,16,256]{3,2,1,0:T(8,128)(2,1)S(1)}, u32[]{:S(2)}) copy-start(bf16[128,3,16,256]{3,2,1,0:T(8,128)(2,1)S(1)} %all-to-all-done.direct_ref) | copy-start | bytes 9437188
  72.8 21.1 %collective-permute-start.2 = (bf16[2,64,16,128]{3,2,1,0:T(8,128)(2,1)}, bf16[2,64,16,128]{3,2,1,0:T(8,128)(2,1)}, u32[]{:S(2)}, u32[]{:S(2)}) collective-permute-start(bf16[2,64,16,128]{3,2,1,0:T(8,128)(2,1)} %get-tuple-element.58), channel_id=1, source_target_pairs={{0,32},{32,0},{64,96},{96,64},{1,33},{33,1},{65,97},{97,65},{2,34}... | collective-permute-start | bytes 1572872 | tf_op jit(solution)/shard_map/ppermute | solution.py:591
  72.8 21.1 %collective-permute-start.3 = (bf16[2,64,16,128]{3,2,1,0:T(8,128)(2,1)}, bf16[2,64,16,128]{3,2,1,0:T(8,128)(2,1)}, u32[]{:S(2)}, u32[]{:S(2)}) collective-permute-start(bf16[2,64,16,128]{3,2,1,0:T(8,128)(2,1)} %get-tuple-element.59), channel_id=1, source_target_pairs={{0,96},{32,64},{64,32},{96,0},{1,97},{33,65},{65,33},{97,1},{2,98}... | collective-permute-start | bytes 1572872 | tf_op jit(solution)/shard_map/ppermute | solution.py:591
  76.3 15.5 %collective-permute-start.5 = (bf16[64,16,128]{2,1,0:T(8,128)(2,1)}, bf16[64,16,128]{2,1,0:T(8,128)(2,1)}, u32[]{:S(2)}, u32[]{:S(2)}) collective-permute-start(bf16[64,16,128]{2,1,0:T(8,128)(2,1)} %fusion.2), channel_id=1, source_target_pairs={{0,32},{32,0},{64,96},{96,64},{1,33},{33,1},{65,97},{97,65},{2,34}... | collective-permute-start | bytes 786440 | tf_op jit(solution)/shard_map/ppermute | solution.py:599
  76.6 31.9 %all-to-all-start.1 = ((bf16[128,16,256]{2,1,0:T(8,128)(2,1)}), bf16[128,16,256]{2,1,0:T(8,128)(2,1)}, u32[]{:S(2)}, u32[]{:S(2)}) async-start(bf16[128,16,256]{2,1,0:T(8,128)(2,1)} %get-tuple-element.71), calls=%async_computation.1 | async-start | bytes 2097152 | tf_op jit(solution)/shard_map/all_to_all | solution.py:589
  85.0 9.0 %collective-permute-start.4 = (bf16[64,16,128]{2,1,0:T(8,128)(2,1)S(1)}, bf16[64,16,128]{2,1,0:T(8,128)(2,1)S(1)}, u32[]{:S(2)}, u32[]{:S(2)}) collective-permute-start(bf16[64,16,128]{2,1,0:T(8,128)(2,1)S(1)} %fusion.3), channel_id=1, source_target_pairs={{0,96},{32,64},{64,32},{96,0},{1,97},{33,65},{65,33},{97,1},{2,98}... | collective-permute-start | bytes 786440 | tf_op jit(solution)/shard_map/ppermute | solution.py:599
  93.9 4.0 %copy-start.7 = (bf16[64,16,128]{2,1,0:T(8,128)(2,1)}, bf16[64,16,128]{2,1,0:T(8,128)(2,1)S(1)}, u32[]{:S(2)}) copy-start(bf16[64,16,128]{2,1,0:T(8,128)(2,1)S(1)} %collective-permute-done.4.a_far) | copy-start | bytes 786436
  95.1 6.8 %collective-permute-start.7 = (bf16[64,16,128]{2,1,0:T(8,128)(2,1)S(1)}, bf16[64,16,128]{2,1,0:T(8,128)(2,1)S(1)}, u32[]{:S(2)}, u32[]{:S(2)}) collective-permute-start(bf16[64,16,128]{2,1,0:T(8,128)(2,1)S(1)} %fusion), channel_id=1, source_target_pairs={{0,32},{32,0},{64,96},{96,64},{1,33},{33,1},{65,97},{97,65},{2,34}... | collective-permute-start | bytes 786440 | tf_op jit(solution)/shard_map/ppermute | solution.py:599
  96.8 7.8 %collective-permute-start.6 = (bf16[64,16,128]{2,1,0:T(8,128)(2,1)S(1)}, bf16[64,16,128]{2,1,0:T(8,128)(2,1)S(1)}, u32[]{:S(2)}, u32[]{:S(2)}) collective-permute-start(bf16[64,16,128]{2,1,0:T(8,128)(2,1)S(1)} %fusion.1), channel_id=1, source_target_pairs={{0,96},{32,64},{64,32},{96,0},{1,97},{33,65},{65,33},{97,1},{2,98}... | collective-permute-start | bytes 786440 | tf_op jit(solution)/shard_map/ppermute | solution.py:599
  100.6 17.2 %copy-start.11 = (s32[128]{0:T(128)S(1)}, s32[128]{0:T(128)}, u32[]{:S(2)}) copy-start(s32[128]{0:T(128)} %owner_ref.3) | copy-start | bytes 1540
  100.6 17.8 %copy-start.10 = (s32[256]{0:T(256)S(1)}, s32[256]{0:T(256)}, u32[]{:S(2)}) copy-start(s32[256]{0:T(256)} %owner_ref.5) | copy-start | bytes 3076
  102.0 2.6 %copy-start.8 = (bf16[64,16,128]{2,1,0:T(8,128)(2,1)}, bf16[64,16,128]{2,1,0:T(8,128)(2,1)S(1)}, u32[]{:S(2)}) copy-start(bf16[64,16,128]{2,1,0:T(8,128)(2,1)S(1)} %collective-permute-done.7.b_far) | copy-start | bytes 786436
  104.6 0.7 copy-start.9
  108.5 37.1 %all-to-all-start.2 = ((bf16[512,16,128]{2,1,0:T(8,128)(2,1)}), bf16[512,16,128]{2,1,0:T(8,128)(2,1)S(1)}, u32[]{:S(2)}, u32[]{:S(2)}) async-start(bf16[512,16,128]{2,1,0:T(8,128)(2,1)} %place_beams_128.1), calls=%async_computation.2 | async-start | bytes 4194304 | tf_op jit(solution)/shard_map/all_to_all | solution.py:606
  120.2 8.4 %collective-permute-start.10 = (bf16[32,16,256]{2,1,0:T(8,128)(2,1)S(1)}, bf16[32,16,256]{2,1,0:T(8,128)(2,1)S(1)}, u32[]{:S(2)}, u32[]{:S(2)}) collective-permute-start(bf16[32,16,256]{2,1,0:T(8,128)(2,1)S(1)} %get-tuple-element.78), channel_id=1, source_target_pairs={{0,96},{32,0},{64,32},{96,64},{1,97},{33,1},{65,33},{97,65},{2,98}... | collective-permute-start | bytes 786440 | tf_op jit(solution)/shard_map/ppermute | solution.py:613
  121.4 14.2 %collective-permute-start.8 = (bf16[32,16,256]{2,1,0:T(8,128)(2,1)S(1)}, bf16[32,16,256]{2,1,0:T(8,128)(2,1)S(1)}, u32[]{:S(2)}, u32[]{:S(2)}) collective-permute-start(bf16[32,16,256]{2,1,0:T(8,128)(2,1)S(1)} %get-tuple-element.80), channel_id=1, source_target_pairs={{0,32},{32,64},{64,96},{96,0},{1,33},{33,65},{65,97},{97,1},{2,34}... | collective-permute-start | bytes 786440 | tf_op jit(solution)/shard_map/ppermute | solution.py:613
  121.8 13.8 %collective-permute-start.9 = (bf16[32,16,256]{2,1,0:T(8,128)(2,1)S(1)}, bf16[32,16,256]{2,1,0:T(8,128)(2,1)S(1)}, u32[]{:S(2)}, u32[]{:S(2)}) collective-permute-start(bf16[32,16,256]{2,1,0:T(8,128)(2,1)S(1)} %get-tuple-element.79), channel_id=1, source_target_pairs={{0,64},{32,96},{64,0},{96,32},{1,65},{33,97},{65,1},{97,33},{2,66}... | collective-permute-start | bytes 786440 | tf_op jit(solution)/shard_map/ppermute | solution.py:613
  128.6 6.9 %copy-start.3 = (bf16[32,16,256]{2,1,0:T(8,128)(2,1)}, bf16[32,16,256]{2,1,0:T(8,128)(2,1)S(1)}, u32[]{:S(2)}) copy-start(bf16[32,16,256]{2,1,0:T(8,128)(2,1)S(1)} %collective-permute-done.10.refs_3_) | copy-start | bytes 786436
  135.5 0.7 copy-start.4
  136.2 0.7 copy-start.5
  145.6 1.4 copy-start.1

commit v5 on v4

--- a/solution.py
+++ b/solution.py
@@ -451,8 +451,25 @@
     )(beam_owner, *group, *more)
 
 
-def deliver_body(live_ref, x_ref, o_ref):
-    sources, each, frames, lanes = x_ref.shape
+def deliver_body(live_ref, x_any, o_ref, held, sem):
+    _, sources, each, frames, lanes = held.shape
+    step = pl.program_id(0)
+
+    def fetch(n):
+        at = lax.rem(n, 2)
+        part = x_any.at[:, pl.ds(n * each, each)]
+        return pltpu.make_async_copy(part, held.at[at], sem.at[at])
+
+    @pl.when(step == 0)
+    def _():
+        fetch(step).start()
+
+    @pl.when(step + 1 < pl.num_programs(0))
+    def _():
+        fetch(step + 1).start()
+
+    fetch(step).wait()
+    x_ref = held.at[lax.rem(step, 2)]
     for s in range(each):
         slot = pl.program_id(0) * each + s
 
@@ -474,10 +491,16 @@
         out_shape=jax.ShapeDtypeStruct((slots, sources * frames, lanes), F32),
         in_specs=[
             smem(),
-            pl.BlockSpec((sources, each, frames, lanes), lambda s: (0, s, 0, 0)),
+            pl.BlockSpec(memory_space=pl.ANY),
         ],
         out_specs=pl.BlockSpec((each, sources * frames, lanes), lambda s: (s, 0, 0)),
-        compiler_params=params(dimension_semantics=("arbitrary",)),
+        scratch_shapes=[
+            pltpu.VMEM((2, sources, each, frames, lanes), BF16),
+            pltpu.SemaphoreType.DMA((2,)),
+        ],
+        compiler_params=pltpu.CompilerParams(
+            vmem_limit_bytes=VMEM_LIMIT // 4, dimension_semantics=("arbitrary",)
+        ),
         name="deliver_beams",
     )(live, arrived.reshape(sources, slots, frames, lanes))
 
@@ -585,10 +608,11 @@
         parts.append((keep, a, a2, b, b2))
         if first + count < half_count:
             near.append((lax.ppermute(a, "inp", side), lax.ppermute(b, "inp", back)))
+    last = parts[-1]
     later, arrived, parts, near = lax.optimization_barrier((later, arrived, parts, near))
     later = lax.all_to_all(later, "chan", split_axis=0, concat_axis=0, tiled=True)
     later = later.reshape(chan_count, inp_count, *later.shape[1:])
-    near.append((lax.ppermute(parts[-1][1], "inp", side), lax.ppermute(parts[-1][3], "inp", back)))
+    near.append((lax.ppermute(last[1], "inp", side), lax.ppermute(last[3], "inp", back)))
     far = []
     for n, (_, _, a2, _, b2) in enumerate(parts):
         a_in, b_in = near[n]

time: 154 us -> 149 us (0.968)
  waiting for transfers between devices: 36.4 us -> 32.5 us
    ppermute x2, waiting for transfers between devices: 6.65 us -> 2.96 us  [shards(): lax.ppermute(b_sum, 'inp', side)]
    ppermute x2, waiting for transfers between devices: 4.65 us -> 6.86 us  [shards(): lax.ppermute(a_sum, 'inp', back)]
    ppermute x2, starting transfers between devices: 2.8 us -> 4.37 us  [shards(): lax.ppermute(a_sum, 'inp', back)]
    unnamed x24 -> x22, local copies, waits for them, and re-layouts: 4.29 us -> 2.94 us
  transfers between devices with their start and end apart: 14 -> 14, of which waited for: 8 -> 8; matrix products, arithmetic and copies ran while one was open for 5% -> 5% of each run, Pallas kernels for 31% -> 33%
where the time goes in v5:
time: 149 us; the launch traced here: 147 us
  Pallas kernels  61.9 us (42%)
  starting transfers between devices  40.5 us (27%)
  waiting for transfers between devices  32.5 us (22%)
  other arithmetic  6.84 us (5%)
  local copies, waits for them, and re-layouts  4.1 us (3%)
    pallas_call x2, Pallas kernels, beamform(): pl.pallas_call(functools.partial(beam_body, first, 64), grid=(steps + 1,)...  26.2 us
    ppermute x2, waiting for transfers between devices, shards(): near.append((lax.ppermute(a, 'inp', side), lax.ppermute(b, 'inp', back)))  14.1 us
    pallas_call x2, Pallas kernels, gram(): pl.pallas_call(functools.partial(gram_body, 1.0 / depth, slot), grid_spec...  11.7 us
    all_to_all x1, starting transfers between devices, shards(): lax.all_to_all(outgoing, ('inp', 'chan'), split_axis=0, concat_axis=0, ti...  11.5 us
    pallas_call x1, Pallas kernels, channelize(): pl.pallas_call(functools.partial(channelize_body, groups), out_shape=(jax...  10.7 us
    all_to_all x1, starting transfers between devices, shards(): lax.all_to_all(leaving, 'chan', split_axis=0, concat_axis=0, tiled=True)  9.13 us
    all_to_all x1, starting transfers between devices, shards(): lax.all_to_all(later, 'chan', split_axis=0, concat_axis=0, tiled=True)  6.99 us
    ppermute x3, waiting for transfers between devices, shards(): lax.ppermute(later[:, d], 'inp', [(z, (z + d) % inp_count) for z in range...  6.9 us
  transfers between devices with their start and end apart: 14, of which 8 were waited for; matrix products, arithmetic and copies ran while one was open for 5% of the time, Pallas kernels for 33%

profile of v5, /device:TPU:1, one launch (start us, length us, event | category | flops | bytes accessed | tf_op | source)
XLA Modules:
  0.0 146.7 jit_solution(11438659906721566321)
XLA Ops:
  0.6 10.7 %channelize.1 = (bf16[128,3,16,256]{3,2,1,0:T(8,128)(2,1)}, bf16[128,16,256]{2,1,0:T(8,128)(2,1)}, bf16[256,2,16,256]{3,2,1,0:T(8,128)(2,1)}) custom-call(s32[128]{0:T(128)} %owner_ref.3, s32[1]{0:T(128)} %bitcast.inp_ref.here_ref, bf16[4096,512]{1,0:T(8,128)(2,1)} %bitcast.31, bf16[512,512]{1,0:T(8,128)(2,1)} %constant.17.clone.table_ref, ...), custom_call_target="tpu_custom_call" | custom-call | tf_op jit(solution)/shard_map/channelize/pallas_call | solution.py:149
  11.4 11.5 %all-to-all-start = ((bf16[128,3,16,256]{3,2,1,0:T(8,128)(2,1)}), bf16[128,3,16,256]{3,2,1,0:T(8,128)(2,1)S(1)}, u32[]{:S(2)}, u32[]{:S(2)}) async-start(bf16[128,3,16,256]{3,2,1,0:T(8,128)(2,1)} %get-tuple-element.37), calls=%async_computation | async-start | bytes 6291456 | tf_op jit(solution)/shard_map/all_to_all | solution.py:595
  22.9 4.0 %phases.1 = (f32[256,512]{1,0:T(8,128)}, f32[256,512]{1,0:T(8,128)}) custom-call(s32[1]{0:T(128)} %bitcast.inp_ref.here_ref, s32[256]{0:T(256)} %section_ref.1, f32[256,1024]{1,0:T(8,128)} %delay_ref.1), custom_call_target="tpu_custom_call" | custom-call | tf_op jit(solution)/shard_map/phases/pallas_call | solution.py:210
  26.9 12.9 %beamform_0.1 = (bf16[128,16,128]{2,1,0:T(8,128)(2,1)}, bf16[2,64,16,128]{3,2,1,0:T(8,128)(2,1)}, bf16[64,16,128]{2,1,0:T(8,128)(2,1)}, bf16[2,64,16,128]{3,2,1,0:T(8,128)(2,1)}, bf16[64,16,128]{2,1,0:T(8,128)(2,1)}) custom-call(bf16[256,32,256]{2,1,0:T(8,128)(2,1)} %bitcast.32, f32[256,512]{1,0:T(8,128)} %get-tuple-element.39.cos_ref, ...), custom_call_target="tpu_custom_call" | custom-call | flops 8589934592 | bytes 4194304 | tf_op jit(solution)/shard_map/beamform_0/pallas_call | solution.py:359
  39.8 1.5 %collective-permute-start = (bf16[2,64,16,128]{3,2,1,0:T(8,128)(2,1)}, bf16[2,64,16,128]{3,2,1,0:T(8,128)(2,1)S(1)}, u32[]{:S(2)}, u32[]{:S(2)}) collective-permute-start(bf16[2,64,16,128]{3,2,1,0:T(8,128)(2,1)} %get-tuple-element.43), channel_id=1, source_target_pairs={{0,32},{32,0},{64,96},{96,64},{1,33},{33,1},{65,97},{97,65},{2,34}... | collective-permute-start | bytes 1572872 | tf_op jit(solution)/shard_map/ppermute | solution.py:610
  41.3 2.1 %collective-permute-start.1 = (bf16[2,64,16,128]{3,2,1,0:T(8,128)(2,1)}, bf16[2,64,16,128]{3,2,1,0:T(8,128)(2,1)}, u32[]{:S(2)}, u32[]{:S(2)}) collective-permute-start(bf16[2,64,16,128]{3,2,1,0:T(8,128)(2,1)} %get-tuple-element.45), channel_id=1, source_target_pairs={{0,96},{32,64},{64,32},{96,0},{1,97},{33,65},{65,33},{97,1},{2,98}... | collective-permute-start | bytes 1572872 | tf_op jit(solution)/shard_map/ppermute | solution.py:610
  43.4 13.3 %beamform_128.1 = (bf16[128,16,128]{2,1,0:T(8,128)(2,1)}, bf16[2,64,16,128]{3,2,1,0:T(8,128)(2,1)}, bf16[64,16,128]{2,1,0:T(8,128)(2,1)}, bf16[2,64,16,128]{3,2,1,0:T(8,128)(2,1)}, bf16[64,16,128]{2,1,0:T(8,128)(2,1)}) custom-call(bf16[256,32,256]{2,1,0:T(8,128)(2,1)} %bitcast.33, f32[256,512]{1,0:T(8,128)} %get-tuple-element.39.cos_ref, ...), custom_call_target="tpu_custom_call" | custom-call | flops 8589934592 | bytes 4194304 | tf_op jit(solution)/shard_map/beamform_128/pallas_call | solution.py:359
  56.7 0.6 collective-permute-start.2
  57.3 0.6 collective-permute-start.3
  58.0 12.5 %collective-permute-done.a_near = bf16[2,64,16,128]{3,2,1,0:T(8,128)(2,1)S(1)} collective-permute-done((bf16[2,64,16,128]{3,2,1,0:T(8,128)(2,1)}, bf16[2,64,16,128]{3,2,1,0:T(8,128)(2,1)S(1)}, u32[]{:S(2)}, u32[]{:S(2)}) %collective-permute-start) | collective-permute-done | bytes 524320 | tf_op jit(solution)/shard_map/ppermute | solution.py:610
  70.5 0.8 copy-done.1
  71.3 1.5 %collective-permute-done.1.b_near = bf16[2,64,16,128]{3,2,1,0:T(8,128)(2,1)} collective-permute-done((bf16[2,64,16,128]{3,2,1,0:T(8,128)(2,1)}, bf16[2,64,16,128]{3,2,1,0:T(8,128)(2,1)}, u32[]{:S(2)}, u32[]{:S(2)}) %collective-permute-start.1) | collective-permute-done | bytes 524320 | tf_op jit(solution)/shard_map/ppermute | solution.py:610
  72.8 0.0 all-to-all-done.direct_ref
  72.8 2.2 %fusion.2 = bf16[64,16,128]{2,1,0:T(8,128)(2,1)} fusion(bf16[64,16,128]{2,1,0:T(8,128)(2,1)} %get-tuple-element.58, bf16[2,64,16,128]{3,2,1,0:T(8,128)(2,1)} %collective-permute-done.1.b_near), kind=kLoop, calls=%fused_computation.5 | loop fusion | flops 524288 | bytes 786432 | tf_op jit(solution)/shard_map/convert_element_type | solution.py:622
  75.0 0.0 collective-permute-start.5
  75.0 7.0 %all-to-all-start.1 = ((bf16[128,16,256]{2,1,0:T(8,128)(2,1)}), bf16[128,16,256]{2,1,0:T(8,128)(2,1)}, u32[]{:S(2)}, u32[]{:S(2)}) async-start(bf16[128,16,256]{2,1,0:T(8,128)(2,1)} %get-tuple-element.67), calls=%async_computation.1 | async-start | bytes 2097152 | tf_op jit(solution)/shard_map/all_to_all | solution.py:613
  82.0 1.1 fusion.3
  83.1 2.2 %collective-permute-start.4 = (bf16[64,16,128]{2,1,0:T(8,128)(2,1)S(1)}, bf16[64,16,128]{2,1,0:T(8,128)(2,1)S(1)}, u32[]{:S(2)}, u32[]{:S(2)}) collective-permute-start(bf16[64,16,128]{2,1,0:T(8,128)(2,1)S(1)} %fusion.3), channel_id=1, source_target_pairs={{0,96},{32,64},{64,32},{96,0},{1,97},{33,65},{65,33},{97,1},{2,98}... | collective-permute-start | bytes 786440 | tf_op jit(solution)/shard_map/ppermute | solution.py:623
  85.3 0.0 collective-permute-done.2.a_near
  85.3 0.0 collective-permute-done.3.b_near
  85.3 2.1 %collective-permute-done.5.b_far = bf16[64,16,128]{2,1,0:T(8,128)(2,1)} collective-permute-done((bf16[64,16,128]{2,1,0:T(8,128)(2,1)}, bf16[64,16,128]{2,1,0:T(8,128)(2,1)}, u32[]{:S(2)}, u32[]{:S(2)}) %collective-permute-start.5) | collective-permute-done | bytes 262176 | tf_op jit(solution)/shard_map/ppermute | solution.py:623
  87.4 4.7 %collective-permute-done.4.a_far = bf16[64,16,128]{2,1,0:T(8,128)(2,1)S(1)} collective-permute-done((bf16[64,16,128]{2,1,0:T(8,128)(2,1)S(1)}, bf16[64,16,128]{2,1,0:T(8,128)(2,1)S(1)}, u32[]{:S(2)}, u32[]{:S(2)}) %collective-permute-start.4) | collective-permute-done | bytes 262176 | tf_op jit(solution)/shard_map/ppermute | solution.py:623
  92.1 1.2 fusion
  93.3 0.1 collective-permute-start.7
  93.4 1.0 fusion.1
  94.4 2.2 %collective-permute-start.6 = (bf16[64,16,128]{2,1,0:T(8,128)(2,1)S(1)}, bf16[64,16,128]{2,1,0:T(8,128)(2,1)S(1)}, u32[]{:S(2)}, u32[]{:S(2)}) collective-permute-start(bf16[64,16,128]{2,1,0:T(8,128)(2,1)S(1)} %fusion.1), channel_id=1, source_target_pairs={{0,96},{32,64},{64,32},{96,0},{1,97},{33,65},{65,33},{97,1},{2,98}... | collective-permute-start | bytes 786440 | tf_op jit(solution)/shard_map/ppermute | solution.py:623
  96.6 2.6 %place_beams_0.1.rest_0_ = bf16[512,16,128]{2,1,0:T(8,128)(2,1)} custom-call(s32[256]{0:T(256)} %owner_ref.5, bf16[128,16,128]{2,1,0:T(8,128)(2,1)} %get-tuple-element.64.keep, bf16[2,64,16,128]{3,2,1,0:T(8,128)(2,1)} %copy-done.1, bf16[64,16,128]{2,1,0:T(8,128)(2,1)} %copy-done.6, bf16[2,64,16,128]{3,2,1,0:T(8,128)(2,1)} %collective-permute-done.1.b_near, ...), custom_call_target="tpu_custom_call" | custom-call | tf_op jit(solution)/shard_map/place_beams_0/pallas_call | solution.py:437
  99.2 0.0 copy-start.10
  99.2 0.0 copy-start.9
  99.2 0.9 collective-permute-done.7.b_far
  100.1 2.1 %collective-permute-done.6.a_far = bf16[64,16,128]{2,1,0:T(8,128)(2,1)S(1)} collective-permute-done((bf16[64,16,128]{2,1,0:T(8,128)(2,1)S(1)}, bf16[64,16,128]{2,1,0:T(8,128)(2,1)S(1)}, u32[]{:S(2)}, u32[]{:S(2)}) %collective-permute-start.6) | collective-permute-done | bytes 262176 | tf_op jit(solution)/shard_map/ppermute | solution.py:623
  102.3 0.7 copy-done.8
  103.0 3.2 %place_beams_128.1 = bf16[512,16,128]{2,1,0:T(8,128)(2,1)} custom-call(s32[256]{0:T(256)} %owner_ref.5, bf16[128,16,128]{2,1,0:T(8,128)(2,1)} %get-tuple-element.55.keep, bf16[2,64,16,128]{3,2,1,0:T(8,128)(2,1)} %collective-permute-done.2.a_near, bf16[64,16,128]{2,1,0:T(8,128)(2,1)} %copy-done.8, ...), custom_call_target="tpu_custom_call", output_to_operand_aliasing={{}: (6, {})} | custom-call | tf_op jit(solution)/shard_map/place_beams_128/pallas_call | solution.py:437
  106.2 0.0 all-to-all-done.1
  106.2 9.1 %all-to-all-start.2 = ((bf16[512,16,128]{2,1,0:T(8,128)(2,1)}), bf16[512,16,128]{2,1,0:T(8,128)(2,1)S(1)}, u32[]{:S(2)}, u32[]{:S(2)}) async-start(bf16[512,16,128]{2,1,0:T(8,128)(2,1)} %place_beams_128.1), calls=%async_computation.2 | async-start | bytes 4194304 | tf_op jit(solution)/shard_map/all_to_all | solution.py:630
  115.3 0.7 fusion.5
  116.0 0.7 fusion.4
  116.7 1.2 slice_bitcast_fusion
  117.9 2.2 %collective-permute-start.10 = (bf16[32,16,256]{2,1,0:T(8,128)(2,1)S(1)}, bf16[32,16,256]{2,1,0:T(8,128)(2,1)S(1)}, u32[]{:S(2)}, u32[]{:S(2)}) collective-permute-start(bf16[32,16,256]{2,1,0:T(8,128)(2,1)S(1)} %get-tuple-element.74), channel_id=1, source_target_pairs={{0,96},{32,0},{64,32},{96,64},{1,97},{33,1},{65,33},{97,65},{2,98}... | collective-permute-start | bytes 786440 | tf_op jit(solution)/shard_map/ppermute | solution.py:637
  120.1 1.4 collective-permute-start.9
  121.5 5.9 %gram_0.1.refs_4_ = f32[2,2,1024,1024]{3,2,1,0:T(8,128)} custom-call(s32[1]{0:T(128)} %bitcast.inp_ref.here_ref, s32[1]{0:T(128)} %bitcast.1.live_ref, bf16[128,3,16,256]{3,2,1,0:T(8,128)(2,1)} %copy-done), custom_call_target="tpu_custom_call" | custom-call | flops 4294967296 | bytes 12582912 | tf_op jit(solution)/shard_map/gram_0/pallas_call | solution.py:559
  127.3 0.0 collective-permute-done.10.refs_3_
  127.4 6.9 %collective-permute-done.8.refs_1_ = bf16[32,16,256]{2,1,0:T(8,128)(2,1)S(1)} collective-permute-done((bf16[32,16,256]{2,1,0:T(8,128)(2,1)S(1)}, bf16[32,16,256]{2,1,0:T(8,128)(2,1)S(1)}, u32[]{:S(2)}, u32[]{:S(2)}) %collective-permute-start.8) | collective-permute-done | bytes 262176 | tf_op jit(solution)/shard_map/ppermute | solution.py:637
  134.3 0.7 copy-done.3
  135.0 0.7 copy-done.4
  135.7 5.8 %gram_1.1 = f32[2,2,1024,1024]{3,2,1,0:T(8,128)} custom-call(s32[1]{0:T(128)} %bitcast.inp_ref.here_ref, s32[1]{0:T(128)} %bitcast.1.live_ref, bf16[128,3,16,256]{3,2,1,0:T(8,128)(2,1)} %copy-done, bf16[32,4,16,256]{3,2,1,0:T(8,128)(2,1)} %bitcast.9.refs_0_, bf16[32,16,256]{2,1,0:T(8,128)(2,1)} %copy-done.3, ...), custom_call_target="tpu_custom_call", output_to_operand_aliasing={{}: (7, {})} | custom-call | flops 4294967296 | bytes 12582912 | tf_op jit(solution)/shard_map/gram_1/pallas_call | solution.py:559
  141.5 1.7 %all-to-all-done.2 = bf16[512,16,128]{2,1,0:T(8,128)(2,1)S(1)} async-done(((bf16[512,16,128]{2,1,0:T(8,128)(2,1)}), bf16[512,16,128]{2,1,0:T(8,128)(2,1)S(1)}, u32[]{:S(2)}, u32[]{:S(2)}) %all-to-all-start.2) | async-done | bytes 2097184 | tf_op jit(solution)/shard_map/all_to_all | solution.py:630
  143.2 3.4 %deliver_beams.1 = f32[16,512,128]{2,1,0:T(8,128)} custom-call(s32[1]{0:T(128)} %bitcast.13.live_ref, bf16[32,16,16,128]{3,2,1,0:T(8,128)(2,1)S(1)} %bitcast.29), custom_call_target="tpu_custom_call" | custom-call | tf_op jit(solution)/shard_map/deliver_beams/pallas_call | solution.py:488
  (18 shorter events, 0.0 us)
Async XLA Ops:
  11.4 61.4 %all-to-all-start = ((bf16[128,3,16,256]{3,2,1,0:T(8,128)(2,1)}), bf16[128,3,16,256]{3,2,1,0:T(8,128)(2,1)S(1)}, u32[]{:S(2)}, u32[]{:S(2)}) async-start(bf16[128,3,16,256]{3,2,1,0:T(8,128)(2,1)} %get-tuple-element.37), calls=%async_computation | async-start | bytes 6291456 | tf_op jit(solution)/shard_map/all_to_all | solution.py:595
  39.8 30.7 %collective-permute-start = (bf16[2,64,16,128]{3,2,1,0:T(8,128)(2,1)}, bf16[2,64,16,128]{3,2,1,0:T(8,128)(2,1)S(1)}, u32[]{:S(2)}, u32[]{:S(2)}) collective-permute-start(bf16[2,64,16,128]{3,2,1,0:T(8,128)(2,1)} %get-tuple-element.43), channel_id=1, source_target_pairs={{0,32},{32,0},{64,96},{96,64},{1,33},{33,1},{65,97},{97,65},{2,34}... | collective-permute-start | bytes 1572872 | tf_op jit(solution)/shard_map/ppermute | solution.py:610
  41.3 31.5 %collective-permute-start.1 = (bf16[2,64,16,128]{3,2,1,0:T(8,128)(2,1)}, bf16[2,64,16,128]{3,2,1,0:T(8,128)(2,1)}, u32[]{:S(2)}, u32[]{:S(2)}) collective-permute-start(bf16[2,64,16,128]{3,2,1,0:T(8,128)(2,1)} %get-tuple-element.45), channel_id=1, source_target_pairs={{0,96},{32,64},{64,32},{96,0},{1,97},{33,65},{65,33},{97,1},{2,98}... | collective-permute-start | bytes 1572872 | tf_op jit(solution)/shard_map/ppermute | solution.py:610
  56.7 36.7 %copy-start.5 = (bf16[64,16,128]{2,1,0:T(8,128)(2,1)S(1)}, bf16[64,16,128]{2,1,0:T(8,128)(2,1)}, u32[]{:S(2)}) copy-start(bf16[64,16,128]{2,1,0:T(8,128)(2,1)} %get-tuple-element.61) | copy-start | bytes 786436
  56.7 28.6 %collective-permute-start.2 = (bf16[2,64,16,128]{3,2,1,0:T(8,128)(2,1)}, bf16[2,64,16,128]{3,2,1,0:T(8,128)(2,1)}, u32[]{:S(2)}, u32[]{:S(2)}) collective-permute-start(bf16[2,64,16,128]{3,2,1,0:T(8,128)(2,1)} %get-tuple-element.50), channel_id=1, source_target_pairs={{0,32},{32,0},{64,96},{96,64},{1,33},{33,1},{65,97},{97,65},{2,34}... | collective-permute-start | bytes 1572872 | tf_op jit(solution)/shard_map/ppermute | solution.py:615
  57.3 28.0 %collective-permute-start.3 = (bf16[2,64,16,128]{3,2,1,0:T(8,128)(2,1)}, bf16[2,64,16,128]{3,2,1,0:T(8,128)(2,1)}, u32[]{:S(2)}, u32[]{:S(2)}) collective-permute-start(bf16[2,64,16,128]{3,2,1,0:T(8,128)(2,1)} %get-tuple-element.52), channel_id=1, source_target_pairs={{0,96},{32,64},{64,32},{96,0},{1,97},{33,65},{65,33},{97,1},{2,98}... | collective-permute-start | bytes 1572872 | tf_op jit(solution)/shard_map/ppermute | solution.py:615
  70.5 0.8 copy-start.1
  72.8 26.4 %copy-start = (bf16[128,3,16,256]{3,2,1,0:T(8,128)(2,1)}, bf16[128,3,16,256]{3,2,1,0:T(8,128)(2,1)S(1)}, u32[]{:S(2)}) copy-start(bf16[128,3,16,256]{3,2,1,0:T(8,128)(2,1)S(1)} %all-to-all-done.direct_ref) | copy-start | bytes 9437188
  75.0 12.4 %collective-permute-start.5 = (bf16[64,16,128]{2,1,0:T(8,128)(2,1)}, bf16[64,16,128]{2,1,0:T(8,128)(2,1)}, u32[]{:S(2)}, u32[]{:S(2)}) collective-permute-start(bf16[64,16,128]{2,1,0:T(8,128)(2,1)} %fusion.2), channel_id=1, source_target_pairs={{0,32},{32,0},{64,96},{96,64},{1,33},{33,1},{65,97},{97,65},{2,34}... | collective-permute-start | bytes 786440 | tf_op jit(solution)/shard_map/ppermute | solution.py:623
  75.0 31.2 %all-to-all-start.1 = ((bf16[128,16,256]{2,1,0:T(8,128)(2,1)}), bf16[128,16,256]{2,1,0:T(8,128)(2,1)}, u32[]{:S(2)}, u32[]{:S(2)}) async-start(bf16[128,16,256]{2,1,0:T(8,128)(2,1)} %get-tuple-element.67), calls=%async_computation.1 | async-start | bytes 2097152 | tf_op jit(solution)/shard_map/all_to_all | solution.py:613
  83.1 9.0 %collective-permute-start.4 = (bf16[64,16,128]{2,1,0:T(8,128)(2,1)S(1)}, bf16[64,16,128]{2,1,0:T(8,128)(2,1)S(1)}, u32[]{:S(2)}, u32[]{:S(2)}) collective-permute-start(bf16[64,16,128]{2,1,0:T(8,128)(2,1)S(1)} %fusion.3), channel_id=1, source_target_pairs={{0,96},{32,64},{64,32},{96,0},{1,97},{33,65},{65,33},{97,1},{2,98}... | collective-permute-start | bytes 786440 | tf_op jit(solution)/shard_map/ppermute | solution.py:623
  92.1 4.5 %copy-start.6 = (bf16[64,16,128]{2,1,0:T(8,128)(2,1)}, bf16[64,16,128]{2,1,0:T(8,128)(2,1)S(1)}, u32[]{:S(2)}) copy-start(bf16[64,16,128]{2,1,0:T(8,128)(2,1)S(1)} %collective-permute-done.4.a_far) | copy-start | bytes 786436
  93.3 6.8 %collective-permute-start.7 = (bf16[64,16,128]{2,1,0:T(8,128)(2,1)S(1)}, bf16[64,16,128]{2,1,0:T(8,128)(2,1)S(1)}, u32[]{:S(2)}, u32[]{:S(2)}) collective-permute-start(bf16[64,16,128]{2,1,0:T(8,128)(2,1)S(1)} %fusion), channel_id=1, source_target_pairs={{0,32},{32,0},{64,96},{96,64},{1,33},{33,1},{65,97},{97,65},{2,34}... | collective-permute-start | bytes 786440 | tf_op jit(solution)/shard_map/ppermute | solution.py:623
  94.4 7.9 %collective-permute-start.6 = (bf16[64,16,128]{2,1,0:T(8,128)(2,1)S(1)}, bf16[64,16,128]{2,1,0:T(8,128)(2,1)S(1)}, u32[]{:S(2)}, u32[]{:S(2)}) collective-permute-start(bf16[64,16,128]{2,1,0:T(8,128)(2,1)S(1)} %fusion.1), channel_id=1, source_target_pairs={{0,96},{32,64},{64,32},{96,0},{1,97},{33,65},{65,33},{97,1},{2,98}... | collective-permute-start | bytes 786440 | tf_op jit(solution)/shard_map/ppermute | solution.py:623
  99.2 16.1 %copy-start.10 = (s32[128]{0:T(128)S(1)}, s32[128]{0:T(128)}, u32[]{:S(2)}) copy-start(s32[128]{0:T(128)} %owner_ref.3) | copy-start | bytes 1540
  99.2 16.8 %copy-start.9 = (s32[256]{0:T(256)S(1)}, s32[256]{0:T(256)}, u32[]{:S(2)}) copy-start(s32[256]{0:T(256)} %owner_ref.5) | copy-start | bytes 3076
  100.1 2.1 %copy-start.7 = (bf16[64,16,128]{2,1,0:T(8,128)(2,1)}, bf16[64,16,128]{2,1,0:T(8,128)(2,1)S(1)}, u32[]{:S(2)}) copy-start(bf16[64,16,128]{2,1,0:T(8,128)(2,1)S(1)} %collective-permute-done.7.b_far) | copy-start | bytes 786436
  102.3 0.7 copy-start.8
  106.2 37.0 %all-to-all-start.2 = ((bf16[512,16,128]{2,1,0:T(8,128)(2,1)}), bf16[512,16,128]{2,1,0:T(8,128)(2,1)S(1)}, u32[]{:S(2)}, u32[]{:S(2)}) async-start(bf16[512,16,128]{2,1,0:T(8,128)(2,1)} %place_beams_128.1), calls=%async_computation.2 | async-start | bytes 4194304 | tf_op jit(solution)/shard_map/all_to_all | solution.py:630
  117.9 9.5 %collective-permute-start.10 = (bf16[32,16,256]{2,1,0:T(8,128)(2,1)S(1)}, bf16[32,16,256]{2,1,0:T(8,128)(2,1)S(1)}, u32[]{:S(2)}, u32[]{:S(2)}) collective-permute-start(bf16[32,16,256]{2,1,0:T(8,128)(2,1)S(1)} %get-tuple-element.74), channel_id=1, source_target_pairs={{0,96},{32,0},{64,32},{96,64},{1,97},{33,1},{65,33},{97,65},{2,98}... | collective-permute-start | bytes 786440 | tf_op jit(solution)/shard_map/ppermute | solution.py:637
  120.1 14.2 %collective-permute-start.8 = (bf16[32,16,256]{2,1,0:T(8,128)(2,1)S(1)}, bf16[32,16,256]{2,1,0:T(8,128)(2,1)S(1)}, u32[]{:S(2)}, u32[]{:S(2)}) collective-permute-start(bf16[32,16,256]{2,1,0:T(8,128)(2,1)S(1)} %get-tuple-element.76), channel_id=1, source_target_pairs={{0,32},{32,64},{64,96},{96,0},{1,33},{33,65},{65,97},{97,1},{2,34}... | collective-permute-start | bytes 786440 | tf_op jit(solution)/shard_map/ppermute | solution.py:637
  120.1 14.2 %collective-permute-start.9 = (bf16[32,16,256]{2,1,0:T(8,128)(2,1)S(1)}, bf16[32,16,256]{2,1,0:T(8,128)(2,1)S(1)}, u32[]{:S(2)}, u32[]{:S(2)}) collective-permute-start(bf16[32,16,256]{2,1,0:T(8,128)(2,1)S(1)} %get-tuple-element.75), channel_id=1, source_target_pairs={{0,64},{32,96},{64,0},{96,32},{1,65},{33,97},{65,1},{97,33},{2,66}... | collective-permute-start | bytes 786440 | tf_op jit(solution)/shard_map/ppermute | solution.py:637
  127.4 6.9 %copy-start.2 = (bf16[32,16,256]{2,1,0:T(8,128)(2,1)}, bf16[32,16,256]{2,1,0:T(8,128)(2,1)S(1)}, u32[]{:S(2)}) copy-start(bf16[32,16,256]{2,1,0:T(8,128)(2,1)S(1)} %collective-permute-done.10.refs_3_) | copy-start | bytes 786436
  134.2 0.7 copy-start.3
  135.0 0.7 copy-start.4
